TPU v7x, 256 devices: a whole 4x4x8 slice. The times are simulated.
256 devices in a mesh: src: 8 (over y, x_lo), lat: 32 (over x_hi, z, core).
Axes of the slice: x: 4 (x_hi: 2, x_lo: 2; x = x_hi * 2 + x_lo), y: 4, z: 8, core: 2. Of those that a mesh axis runs over, the one named last changes fastest.
Arguments:
- residual_rows: bfloat16 [1024, 8192], P(None, 'src'), may hold values from -6 to 6
- encoder: bfloat16 [8192, 32768], P('src', 'lat'), may hold values from -0.0625 to 0.0625
- decoder: bfloat16 [32768, 8192], P('lat', 'src'), may hold values from -0.0625 to 0.0625
- enc_bias: float32 [32768], P('lat'), may hold values from -3 to 3
- dec_bias: float32 [8192], P('src'), may hold values from -3 to 3
Outputs:
- grad_encoder: bfloat16 [8192, 32768], P('src', 'lat')
- grad_decoder: bfloat16 [32768, 8192], P('lat', 'src')
All inputs are finite; a program needn't handle non-finite values.
Results may differ from a plain program's by a relative error of at most 0.024.
Values may be sent and summed in bfloat16 or wider, within the bound.
No kernel may reach another device: no remote copies, remote signals or barrier semaphores. Data moves between devices by JAX's collectives and lax.ppermute only.
A program may use at most 64 MiB of HBM per device.

v0:
```python
import math

import jax
import jax.numpy as jnp
from jax import lax
from jax.experimental import pallas as pl
from jax.experimental.pallas import tpu as pltpu
from jax.sharding import Mesh
from jax.sharding import PartitionSpec as P

D = 4096
SRCS = 2

SHARPNESS = 8.0
PENALTY = 1.0
EPSILON = 1e-06

NAMES = ("y", "xl", "xh", "z", "core")
SHAPE = (4, 2, 2, 8, 2)
N_Y, N_XL, N_XH, N_Z, N_CORE = SHAPE
SRC = ("y", "xl")
LAT = ("xh", "z", "core")
RING = ("xh", "z")
N_SRC = N_Y * N_XL
N_RING = N_XH * N_Z

NEAR = ((0, 0), (0, 1), (1, 0), (3, 0))
FAR = ((2, 0), (1, 1), (3, 1), (2, 1))

bf16 = jnp.bfloat16
f32 = jnp.float32


def swap(value, axis, size, mask):
    return lax.ppermute(value, axis, [(i, i ^ mask) for i in range(size)])


def place(offsets, slot, core):
    return offsets[(slot + 2 * core) % 4]


def behind(y, x, offset):
    return (y - offset[0]) % N_Y, x ^ offset[1]


def move(value, offsets, slot, to_owner):
    pairs = []
    for y in range(N_Y):
        for x in range(N_XL):
            for core in range(N_CORE):
                oy, ox = behind(y, x, place(offsets, slot, core))
                here = (y * N_XL + x) * N_CORE + core
                there = (oy * N_XL + ox) * N_CORE + core
                pairs.append((here, there) if to_owner else (there, here))
    return lax.ppermute(value, ("y", "xl", "core"), pairs)


def dot(a, b):
    return jnp.dot(a, b, preferred_element_type=f32)


def dot_t(a, b):
    return jnp.einsum("bk,jk->bj", a, b, preferred_element_type=f32)


def decoder_grad(latents, errors, decoder, norms, loss_scale):
    n = len(latents)
    width, feat = decoder.shape
    tile = 256

    def kernel(*refs):
        lat, err = refs[:n], refs[n : 2 * n]
        dec_ref, norm_ref, out_ref = refs[2 * n :]
        outer = jnp.zeros((tile, feat), f32)
        sums = jnp.zeros((tile, 1), f32)
        for l_ref, e_ref in zip(lat, err):
            tall = l_ref[...].T
            outer += jnp.dot(tall, e_ref[...], preferred_element_type=f32)
            sums += jnp.sum(tall.astype(f32), axis=1, keepdims=True)
        shrink = loss_scale * PENALTY * sums / norm_ref[...].T[:, :1]
        out_ref[...] = (loss_scale * outer + shrink * dec_ref[...].astype(f32)).astype(bf16)

    block = latents[0].shape[0]
    return pl.pallas_call(
        kernel,
        grid=(width // tile,),
        in_specs=[pl.BlockSpec((block, tile), lambda i: (0, i))] * n
        + [pl.BlockSpec((block, feat), lambda i: (0, 0))] * n
        + [
            pl.BlockSpec((tile, feat), lambda i: (i, 0)),
            pl.BlockSpec((8, tile), lambda i: (0, i)),
        ],
        out_specs=pl.BlockSpec((tile, feat), lambda i: (i, 0)),
        out_shape=jax.ShapeDtypeStruct(decoder.shape, bf16),
        name="decoder_grad",
    )(*latents, *errors, decoder, norms)


def transpose(value):
    rows, cols = value.shape
    tile = 256

    def kernel(in_ref, out_ref):
        out_ref[...] = in_ref[...].T

    return pl.pallas_call(
        kernel,
        grid=(cols // tile,),
        in_specs=[pl.BlockSpec((rows, tile), lambda i: (0, i))],
        out_specs=pl.BlockSpec((tile, rows), lambda i: (i, 0)),
        out_shape=jax.ShapeDtypeStruct((cols, rows), value.dtype),
        name="transpose",
    )(value)


def per_device(residual_rows, encoder, decoder, enc_bias, dec_bias):
    row_count = residual_rows.shape[0]
    loss_scale = 1.0 / math.sqrt(row_count)
    block = row_count // N_SRC
    y, x, core = (lax.axis_index(a) for a in ("y", "xl", "core"))
    ring = lax.axis_index(RING)
    first = core == 0

    def owner_row(offsets, slot):
        rows = []
        for c in range(N_CORE):
            oy, ox = behind(y, x, place(offsets, slot, c))
            rows.append((oy * N_XL + ox) * block)
        return jnp.where(first, rows[0], rows[1])

    def rows_of(start, count):
        return lax.dynamic_slice_in_dim(residual_rows, start, count, 0)

    own_row = (y * N_XL + x) * block

    twin = (NEAR[2],) * 4

    partial = dot(residual_rows, encoder).astype(bf16).reshape(N_SRC, block, -1)
    partial = lax.all_to_all(partial, SRC, 0, 0)

    squares = jnp.sum(jnp.square(decoder.astype(f32)), axis=1)
    own_sq = squares + swap(squares, "xl", N_XL, 1)
    own_sq = own_sq + swap(own_sq, "y", N_Y, 1)
    other_sq = swap(own_sq, "y", N_Y, 2)
    own_norm = jnp.sqrt(own_sq + EPSILON)
    penalty = PENALTY * (own_norm + jnp.sqrt(other_sq + EPSILON))
    res_t = transpose(residual_rows)
    enc_bias, own_norm, penalty, res_t = lax.optimization_barrier(
        (enc_bias, own_norm, penalty, res_t)
    )

    pre_act = jnp.broadcast_to(enc_bias[None, :], partial.shape[1:])
    for i in range(N_SRC):
        pre_act = pre_act + partial[i].astype(f32)
    latent = (jax.nn.softplus(SHARPNESS * pre_act) / SHARPNESS).astype(bf16)
    slope = jax.nn.sigmoid(SHARPNESS * pre_act)

    mate = move(latent, twin, 0, False)
    near1 = move(latent, NEAR, 1, False)
    near3 = move(latent, NEAR, 3, False)
    latent_far, mate = lax.optimization_barrier((latent, mate))
    far = [move(latent_far, FAR, slot, False) for slot in range(4)]
    near = [jnp.where(first, latent, mate), near1, jnp.where(first, mate, latent), near3]

    def scatter_lat(blocks, offsets):
        theirs = dot(jnp.concatenate(blocks[2:], axis=0), decoder).astype(bf16)
        theirs = swap(theirs, "core", N_CORE, 1)
        mine = dot(jnp.concatenate(blocks[:2], axis=0), decoder) + theirs.astype(f32)
        rows = 2 * block // N_RING
        shares = mine.astype(bf16).reshape(N_RING, rows, -1)
        shares = lax.all_to_all(shares, RING, 0, 0)
        recon = jnp.sum(shares.astype(f32), axis=0) + dec_bias[None, :]
        per_block = N_RING // 2
        start = jnp.where(ring < per_block, owner_row(offsets, 0), owner_row(offsets, 1))
        target = rows_of(start + (ring % per_block) * rows, rows)
        return (recon - target.astype(f32)).astype(bf16)

    def gather_lat(errors):
        errors = jnp.broadcast_to(errors[None], (N_RING,) + errors.shape)
        mine = lax.all_to_all(errors, RING, 0, 0).reshape(2 * block, -1)
        theirs = swap(mine, "core", N_CORE, 1)
        return [mine[:block], mine[block:], theirs[:block], theirs[block:]]

    near_share = scatter_lat(near, NEAR)
    far_share = scatter_lat(far, FAR)
    far_err = gather_lat(far_share)
    near_share, _ = lax.optimization_barrier((near_share, far_err[0][:8, :128]))
    near_err = gather_lat(near_share)

    got = []
    for slot in range(4):
        got.append(move(dot_t(far_err[slot], decoder).astype(bf16), FAR, slot, True))
    sent = jnp.where(first, near_err[2], near_err[0])
    kept = jnp.where(first, near_err[0], near_err[2])
    got.append(move(dot_t(sent, decoder).astype(bf16), twin, 0, True))
    got.append(move(dot_t(near_err[1], decoder).astype(bf16), NEAR, 1, True))
    got.append(move(dot_t(near_err[3], decoder).astype(bf16), NEAR, 3, True))
    act_grad = dot_t(kept, decoder) + penalty[None, :]
    for g in got:
        act_grad = act_grad + g.astype(f32)
    grad_pre = (loss_scale * act_grad * slope).astype(bf16)
    grad_pre = jnp.broadcast_to(grad_pre[None], (N_SRC,) + grad_pre.shape)
    grad_pre = lax.all_to_all(grad_pre, SRC, 0, 0).reshape(row_count, -1)

    scale = jnp.stack([own_norm] * 8)
    grad_decoder = decoder_grad(near + far, near_err + far_err, decoder, scale, loss_scale)

    grad_encoder = dot(res_t, grad_pre).astype(bf16)
    return (grad_encoder, grad_decoder)


def solution(mesh):
    fine = Mesh(mesh.devices.reshape(SHAPE), NAMES)
    in_specs = (P(None, SRC), P(SRC, LAT), P(LAT, SRC), P(LAT), P(SRC))
    out_specs = (P(SRC, LAT), P(LAT, SRC))
    return jax.shard_map(
        per_device, mesh=fine, in_specs=in_specs, out_specs=out_specs, check_vma=False
    )
```

profile of v0, /device:TPU:32, one launch (start us, length us, event | category | flops | bytes accessed | tf_op | source)
XLA Modules:
  0.0 241.3 jit_solution(5757728727942558125)
XLA Ops:
  2.2 5.2 %convolution_convert_fusion.1 = bf16[1024,1024]{1,0:T(8,128)(2,1)} fusion(bf16[1024,1024]{1,0:T(8,128)(2,1)} %in_ref.1, bf16[1024,1024]{1,0:T(8,128)(2,1)S(1)} %copy-done), kind=kOutput, calls=%fused_computation.2 | convolution fusion | flops 2148532224 | bytes 6291456 | tf_op jit(solution)/shard_map/dot_general | solution.py:59
  7.5 5.4 %all-to-all-start = ((bf16[8,128,1024]{2,1,0:T(8,128)(2,1)}), bf16[8,128,1024]{2,1,0:T(8,128)(2,1)}, u32[]{:S(2)}, u32[]{:S(2)}) async-start(bf16[8,128,1024]{2,1,0:T(8,128)(2,1)} %bitcast.86), calls=%async_computation | async-start | bytes 4194304 | tf_op jit(solution)/shard_map/all_to_all | solution.py:139
  17.0 21.7 %collective-permute-done = f32[1024]{0:T(1024)S(1)} collective-permute-done((f32[1024]{0:T(1024)S(1)}, f32[1024]{0:T(1024)S(1)}, u32[]{:S(2)}, u32[]{:S(2)}) %collective-permute-start) | collective-permute-done | bytes 4128 | tf_op jit(solution)/shard_map/ppermute | solution.py:35
  39.3 3.0 %collective-permute-done.1 = f32[1024]{0:T(1024)S(1)} collective-permute-done((f32[1024]{0:T(1024)S(1)}, f32[1024]{0:T(1024)S(1)}, u32[]{:S(2)}, u32[]{:S(2)}) %collective-permute-start.1) | collective-permute-done | bytes 4128 | tf_op jit(solution)/shard_map/ppermute | solution.py:35
  42.3 2.8 %collective-permute-start.2 = (f32[1024]{0:T(1024)S(1)}, f32[1024]{0:T(1024)S(1)}, u32[]{:S(2)}, u32[]{:S(2)}) collective-permute-start(f32[1024]{0:T(1024)S(1)} %get-tuple-element.17), channel_id=1, source_target_pairs={{0,128},{64,192},{128,0},{192,64},{1,129},{65,193},{129,1},{193,65... | collective-permute-start | bytes 12296 | tf_op jit(solution)/shard_map/ppermute | solution.py:35
  45.1 4.1 %transpose.12 = bf16[1024,1024]{1,0:T(8,128)(2,1)} custom-call(bf16[1024,1024]{1,0:T(8,128)(2,1)} %in_ref.1), custom_call_target="tpu_custom_call" | custom-call | tf_op jit(solution)/shard_map/transpose/pallas_call | solution.py:106
  49.2 2.9 %fusion.13 = (bf16[128,1024]{1,0:T(8,128)(2,1)S(1)}, f32[128,1024]{1,0:T(8,128)}) fusion(bf16[8,128,1024]{2,1,0:T(8,128)(2,1)} %all-to-all-done, f32[1024]{0:T(1024)S(1)} %copy-done.17), kind=kLoop, calls=%fused_computation.31 | loop fusion | flops 3276800 | bytes 2887680 | tf_op jit(solution)/shard_map/convert_element_type | solution.py:155
  52.2 3.2 %collective-permute-start.5 = (bf16[128,1024]{1,0:T(8,128)(2,1)S(1)}, bf16[128,1024]{1,0:T(8,128)(2,1)S(1)}, u32[]{:S(2)}, u32[]{:S(2)}) collective-permute-start(bf16[128,1024]{1,0:T(8,128)(2,1)S(1)} %get-tuple-element.12), channel_id=1, source_target_pairs={{64,0},{33,1},{96,32},{1,33},{128,64},{97,65},{160,96},{65,97},{19... | collective-permute-start | bytes 786440 | tf_op jit(solution)/shard_map/ppermute | solution.py:55
  55.4 4.3 %collective-permute-done.3 = bf16[128,1024]{1,0:T(8,128)(2,1)S(1)} collective-permute-done((bf16[128,1024]{1,0:T(8,128)(2,1)S(1)}, bf16[128,1024]{1,0:T(8,128)(2,1)S(1)}, u32[]{:S(2)}, u32[]{:S(2)}) %collective-permute-start.3) | collective-permute-done | bytes 262176 | tf_op jit(solution)/shard_map/ppermute | solution.py:55
  59.8 2.6 %convolution_convert_fusion.3 = bf16[256,1024]{1,0:T(8,128)(2,1)S(1)} fusion(bf16[1024,1024]{1,0:T(8,128)(2,1)} %refs_16_.1, bf16[128,1024]{1,0:T(8,128)(2,1)S(1)} %collective-permute-done.5.refs_3_, bf16[128,1024]{1,0:T(8,128)(2,1)S(1)} %get-tuple-element.29.refs_2_), kind=kOutput, calls=%fused_computation.7 | convolution fusion | flops 538181632 | bytes 3145728 | tf_op jit(solution)/shard_map/dot_general | solution.py:59
  62.7 2.6 %collective-permute-start.11 = (bf16[128,1024]{1,0:T(8,128)(2,1)S(1)}, bf16[128,1024]{1,0:T(8,128)(2,1)}, u32[]{:S(2)}, u32[]{:S(2)}) collective-permute-start(bf16[128,1024]{1,0:T(8,128)(2,1)S(1)} %get-tuple-element.12), channel_id=1, source_target_pairs={{160,0},{225,1},{128,32},{193,33},{224,64},{33,65},{192,96},{1,97}... | collective-permute-start | bytes 786440 | tf_op jit(solution)/shard_map/ppermute | solution.py:55
  67.0 4.2 %collective-permute-done.4.refs_1_ = bf16[128,1024]{1,0:T(8,128)(2,1)S(1)} collective-permute-done((bf16[128,1024]{1,0:T(8,128)(2,1)S(1)}, bf16[128,1024]{1,0:T(8,128)(2,1)S(1)}, u32[]{:S(2)}, u32[]{:S(2)}) %collective-permute-start.4) | collective-permute-done | bytes 262176 | tf_op jit(solution)/shard_map/ppermute | solution.py:55
  72.7 10.8 %all-to-all-start.1 = ((bf16[16,16,1024]{2,1,0:T(8,128)(2,1)}), bf16[16,16,1024]{2,1,0:T(8,128)(2,1)S(1)}, u32[]{:S(2)}, u32[]{:S(2)}) async-start(bf16[16,16,1024]{2,1,0:T(8,128)(2,1)} %bitcast.89), calls=%async_computation.1 | async-start | bytes 1048576 | tf_op jit(solution)/shard_map/all_to_all | solution.py:171
  83.5 2.6 %convolution_convert_fusion.2 = bf16[256,1024]{1,0:T(8,128)(2,1)S(1)} fusion(bf16[1024,1024]{1,0:T(8,128)(2,1)} %refs_16_.1, bf16[128,1024]{1,0:T(8,128)(2,1)} %collective-permute-done.11.refs_7_, bf16[128,1024]{1,0:T(8,128)(2,1)} %collective-permute-done.10.refs_6_), kind=kOutput, calls=%fused_computation.6 | convolution fusion | flops 538181632 | bytes 3145728 | tf_op jit(solution)/shard_map/dot_general | solution.py:59
  88.5 12.3 %collective-permute-done.9.refs_5_ = bf16[128,1024]{1,0:T(8,128)(2,1)S(1)} collective-permute-done((bf16[128,1024]{1,0:T(8,128)(2,1)S(1)}, bf16[128,1024]{1,0:T(8,128)(2,1)S(1)}, u32[]{:S(2)}, u32[]{:S(2)}) %collective-permute-start.9) | collective-permute-done | bytes 262176 | tf_op jit(solution)/shard_map/ppermute | solution.py:55
  102.4 9.8 %all-to-all-start.3 = ((bf16[16,16,1024]{2,1,0:T(8,128)(2,1)}), bf16[16,16,1024]{2,1,0:T(8,128)(2,1)S(1)}, u32[]{:S(2)}, u32[]{:S(2)}) async-start(bf16[16,16,1024]{2,1,0:T(8,128)(2,1)} %bitcast.88), calls=%async_computation.3 | async-start | bytes 1048576 | tf_op jit(solution)/shard_map/all_to_all | solution.py:171
  112.3 16.4 %all-to-all-done.3 = bf16[16,16,1024]{2,1,0:T(8,128)(2,1)S(1)} async-done(((bf16[16,16,1024]{2,1,0:T(8,128)(2,1)}), bf16[16,16,1024]{2,1,0:T(8,128)(2,1)S(1)}, u32[]{:S(2)}, u32[]{:S(2)}) %all-to-all-start.3) | async-done | bytes 524320 | tf_op jit(solution)/shard_map/all_to_all | solution.py:171
  130.4 5.9 %all-to-all-start.4 = ((bf16[16,16,1024]{2,1,0:T(8,128)(2,1)}), bf16[16,16,1024]{2,1,0:T(8,128)(2,1)}, u32[]{:S(2)}, u32[]{:S(2)}) async-start(bf16[16,16,1024]{2,1,0:T(8,128)(2,1)} %broadcast_in_dim.10), calls=%async_computation.4 | async-start | bytes 1048576 | tf_op jit(solution)/shard_map/all_to_all | solution.py:180
  136.3 16.5 %all-to-all-done.4 = bf16[16,16,1024]{2,1,0:T(8,128)(2,1)} async-done(((bf16[16,16,1024]{2,1,0:T(8,128)(2,1)}), bf16[16,16,1024]{2,1,0:T(8,128)(2,1)}, u32[]{:S(2)}, u32[]{:S(2)}) %all-to-all-start.4) | async-done | bytes 524320 | tf_op jit(solution)/shard_map/all_to_all | solution.py:180
  153.7 5.5 %all-to-all-start.2 = ((bf16[16,16,1024]{2,1,0:T(8,128)(2,1)}), bf16[16,16,1024]{2,1,0:T(8,128)(2,1)S(1)}, u32[]{:S(2)}, u32[]{:S(2)}) async-start(bf16[16,16,1024]{2,1,0:T(8,128)(2,1)} %broadcast_in_dim.9), calls=%async_computation.2 | async-start | bytes 1048576 | tf_op jit(solution)/shard_map/all_to_all | solution.py:180
  160.5 3.3 %convolution_convert_fusion.10 = bf16[128,1024]{1,0:T(8,128)(2,1)} fusion(bf16[128,1024]{1,0:T(8,128)(2,1)S(1)} %bitcast.77, bf16[1024,1024]{1,0:T(8,128)(2,1)} %refs_16_.1), kind=kOutput, calls=%fused_computation.27 | convolution fusion | flops 268566528 | bytes 2621440 | tf_op jit(solution)/shard_map/bk,jk->bj/dot_general | solution.py:63
  165.1 3.7 %collective-permute-start.14 = (bf16[128,1024]{1,0:T(8,128)(2,1)S(1)}, bf16[128,1024]{1,0:T(8,128)(2,1)}, u32[]{:S(2)}, u32[]{:S(2)}) collective-permute-start(bf16[128,1024]{1,0:T(8,128)(2,1)S(1)} %convolution_convert_fusion.9), channel_id=1, source_target_pairs={{0,224},{1,161},{32,192},{33,129},{64,32},{65,225},{96,0},{97,193}... | collective-permute-start | bytes 786440 | tf_op jit(solution)/shard_map/ppermute | solution.py:55
  168.8 6.6 %all-to-all-done.2 = bf16[16,16,1024]{2,1,0:T(8,128)(2,1)S(1)} async-done(((bf16[16,16,1024]{2,1,0:T(8,128)(2,1)}), bf16[16,16,1024]{2,1,0:T(8,128)(2,1)S(1)}, u32[]{:S(2)}, u32[]{:S(2)}) %all-to-all-start.2) | async-done | bytes 524320 | tf_op jit(solution)/shard_map/all_to_all | solution.py:180
  175.5 2.8 %convolution_convert_fusion.5 = bf16[128,1024]{1,0:T(8,128)(2,1)S(1)} fusion(bf16[128,1024]{1,0:T(8,128)(2,1)S(1)} %bitcast.84, bf16[1024,1024]{1,0:T(8,128)(2,1)} %refs_16_.1), kind=kOutput, calls=%fused_computation.22 | convolution fusion | flops 268566528 | bytes 2621440 | tf_op jit(solution)/shard_map/bk,jk->bj/dot_general | solution.py:63
  181.7 5.4 %collective-permute-start.17 = (bf16[128,1024]{1,0:T(8,128)(2,1)S(1)}, bf16[128,1024]{1,0:T(8,128)(2,1)S(1)}, u32[]{:S(2)}, u32[]{:S(2)}) collective-permute-start(bf16[128,1024]{1,0:T(8,128)(2,1)S(1)} %convolution_convert_fusion.7), channel_id=1, source_target_pairs={{0,160},{1,225},{32,128},{33,193},{64,224},{65,33},{96,192},{97,1}... | collective-permute-start | bytes 786440 | tf_op jit(solution)/shard_map/ppermute | solution.py:55
  189.2 3.2 %collective-permute-start.18 = (bf16[128,1024]{1,0:T(8,128)(2,1)S(1)}, bf16[128,1024]{1,0:T(8,128)(2,1)S(1)}, u32[]{:S(2)}, u32[]{:S(2)}) collective-permute-start(bf16[128,1024]{1,0:T(8,128)(2,1)S(1)} %convolution_convert_fusion.6), channel_id=1, source_target_pairs={{0,192},{1,193},{32,224},{33,225},{64,0},{65,1},{96,32},{97,33},{1... | collective-permute-start | bytes 786440 | tf_op jit(solution)/shard_map/ppermute | solution.py:55
  192.5 4.8 %collective-permute-done.17 = bf16[128,1024]{1,0:T(8,128)(2,1)S(1)} collective-permute-done((bf16[128,1024]{1,0:T(8,128)(2,1)S(1)}, bf16[128,1024]{1,0:T(8,128)(2,1)S(1)}, u32[]{:S(2)}, u32[]{:S(2)}) %collective-permute-start.17) | collective-permute-done | bytes 262176 | tf_op jit(solution)/shard_map/ppermute | solution.py:55
  199.8 2.1 fusion.11
  203.5 4.4 %all-to-all-start.5 = ((bf16[8,128,1024]{2,1,0:T(8,128)(2,1)}), bf16[8,128,1024]{2,1,0:T(8,128)(2,1)}, u32[]{:S(2)}, u32[]{:S(2)}) async-start(bf16[8,128,1024]{2,1,0:T(8,128)(2,1)} %broadcast_in_dim.11), calls=%async_computation.5 | async-start | bytes 4194304 | tf_op jit(solution)/shard_map/all_to_all | solution.py:203
  210.2 8.6 %decoder_grad.1 = bf16[1024,1024]{1,0:T(8,128)(2,1)} custom-call(bf16[128,1024]{1,0:T(8,128)(2,1)} %copy-done.10, bf16[128,1024]{1,0:T(8,128)(2,1)} %copy-done.14, bf16[128,1024]{1,0:T(8,128)(2,1)} %copy-done.11, bf16[128,1024]{1,0:T(8,128)(2,1)} %copy-done.13, bf16[128,1024]{1,0:T(8,128)(2,1)} %copy-done.16, bf16[128,1024]{1,0:T(8,128)(2,1)} %copy-done.15, ...), custom_call_target="tpu_custom_call" | custom-call | tf_op jit(solution)/shard_map/decoder_grad/pallas_call | solution.py:84
  218.9 16.6 %all-to-all-done.5 = bf16[8,128,1024]{2,1,0:T(8,128)(2,1)} async-done(((bf16[8,128,1024]{2,1,0:T(8,128)(2,1)}), bf16[8,128,1024]{2,1,0:T(8,128)(2,1)}, u32[]{:S(2)}, u32[]{:S(2)}) %all-to-all-start.5) | async-done | bytes 2097184 | tf_op jit(solution)/shard_map/all_to_all | solution.py:203
  235.4 5.9 %convolution_convert_fusion = bf16[1024,1024]{1,0:T(8,128)(2,1)} fusion(bf16[1024,1024]{1,0:T(8,128)(2,1)} %transpose.12, bf16[1024,1024]{1,0:T(8,128)(2,1)} %bitcast.17), kind=kOutput, calls=%fused_computation.1 | convolution fusion | flops 2148532224 | bytes 6291456 | tf_op jit(solution)/shard_map/dot_general | solution.py:59
  (93 shorter events, 31.0 us)
Async XLA Ops:
  7.5 41.8 %all-to-all-start = ((bf16[8,128,1024]{2,1,0:T(8,128)(2,1)}), bf16[8,128,1024]{2,1,0:T(8,128)(2,1)}, u32[]{:S(2)}, u32[]{:S(2)}) async-start(bf16[8,128,1024]{2,1,0:T(8,128)(2,1)} %bitcast.86), calls=%async_computation | async-start | bytes 4194304 | tf_op jit(solution)/shard_map/all_to_all | solution.py:139
  14.9 23.8 %collective-permute-start = (f32[1024]{0:T(1024)S(1)}, f32[1024]{0:T(1024)S(1)}, u32[]{:S(2)}, u32[]{:S(2)}) collective-permute-start(f32[1024]{0:T(1024)S(1)} %multiply_reduce_fusion), channel_id=1, source_target_pairs={{0,32},{32,0},{1,33},{33,1},{2,34},{34,2},{3,35},{35,3},{4,36},{36... | collective-permute-start | bytes 12296 | tf_op jit(solution)/shard_map/ppermute | solution.py:35
  38.7 3.6 %collective-permute-start.1 = (f32[1024]{0:T(1024)S(1)}, f32[1024]{0:T(1024)S(1)}, u32[]{:S(2)}, u32[]{:S(2)}) collective-permute-start(f32[1024]{0:T(1024)S(1)} %add.158), channel_id=1, source_target_pairs={{0,64},{64,0},{128,192},{192,128},{1,65},{65,1},{129,193},{193,129... | collective-permute-start | bytes 12296 | tf_op jit(solution)/shard_map/ppermute | solution.py:35
  42.3 6.9 %collective-permute-start.2 = (f32[1024]{0:T(1024)S(1)}, f32[1024]{0:T(1024)S(1)}, u32[]{:S(2)}, u32[]{:S(2)}) collective-permute-start(f32[1024]{0:T(1024)S(1)} %get-tuple-element.17), channel_id=1, source_target_pairs={{0,128},{64,192},{128,0},{192,64},{1,129},{65,193},{129,1},{193,65... | collective-permute-start | bytes 12296 | tf_op jit(solution)/shard_map/ppermute | solution.py:35
  52.1 7.6 %collective-permute-start.3 = (bf16[128,1024]{1,0:T(8,128)(2,1)S(1)}, bf16[128,1024]{1,0:T(8,128)(2,1)S(1)}, u32[]{:S(2)}, u32[]{:S(2)}) collective-permute-start(bf16[128,1024]{1,0:T(8,128)(2,1)S(1)} %get-tuple-element.12), channel_id=1, source_target_pairs={{192,0},{193,1},{224,32},{225,33},{0,64},{1,65},{32,96},{33,97},{6... | collective-permute-start | bytes 786440 | tf_op jit(solution)/shard_map/ppermute | solution.py:55
  52.2 7.7 %collective-permute-start.5 = (bf16[128,1024]{1,0:T(8,128)(2,1)S(1)}, bf16[128,1024]{1,0:T(8,128)(2,1)S(1)}, u32[]{:S(2)}, u32[]{:S(2)}) collective-permute-start(bf16[128,1024]{1,0:T(8,128)(2,1)S(1)} %get-tuple-element.12), channel_id=1, source_target_pairs={{64,0},{33,1},{96,32},{1,33},{128,64},{97,65},{160,96},{65,97},{19... | collective-permute-start | bytes 786440 | tf_op jit(solution)/shard_map/ppermute | solution.py:55
  59.8 13.0 %copy-start.10 = (bf16[128,1024]{1,0:T(8,128)(2,1)}, bf16[128,1024]{1,0:T(8,128)(2,1)S(1)}, u32[]{:S(2)}) copy-start(bf16[128,1024]{1,0:T(8,128)(2,1)S(1)} %get-tuple-element.28.refs_0_) | copy-start | bytes 786436
  59.8 12.9 %copy-start.11 = (bf16[128,1024]{1,0:T(8,128)(2,1)}, bf16[128,1024]{1,0:T(8,128)(2,1)S(1)}, u32[]{:S(2)}) copy-start(bf16[128,1024]{1,0:T(8,128)(2,1)S(1)} %get-tuple-element.29.refs_2_) | copy-start | bytes 786436
  62.4 8.8 %collective-permute-start.6 = (bf16[256,1024]{1,0:T(8,128)(2,1)S(1)}, bf16[256,1024]{1,0:T(8,128)(2,1)S(1)}, u32[]{:S(2)}, u32[]{:S(2)}) collective-permute-start(bf16[256,1024]{1,0:T(8,128)(2,1)S(1)} %convolution_convert_fusion.3), channel_id=1, source_target_pairs={{0,1},{1,0},{2,3},{3,2},{4,5},{5,4},{6,7},{7,6},{8,9},{9,8},{10,11... | collective-permute-start | bytes 1572872 | tf_op jit(solution)/shard_map/ppermute | solution.py:35
  62.5 8.7 %collective-permute-start.4 = (bf16[128,1024]{1,0:T(8,128)(2,1)S(1)}, bf16[128,1024]{1,0:T(8,128)(2,1)S(1)}, u32[]{:S(2)}, u32[]{:S(2)}) collective-permute-start(bf16[128,1024]{1,0:T(8,128)(2,1)S(1)} %get-tuple-element.12), channel_id=1, source_target_pairs={{32,0},{65,1},{0,32},{97,33},{96,64},{129,65},{64,96},{161,97},{16... | collective-permute-start | bytes 786440 | tf_op jit(solution)/shard_map/ppermute | solution.py:55
  62.7 20.8 %collective-permute-start.11 = (bf16[128,1024]{1,0:T(8,128)(2,1)S(1)}, bf16[128,1024]{1,0:T(8,128)(2,1)}, u32[]{:S(2)}, u32[]{:S(2)}) collective-permute-start(bf16[128,1024]{1,0:T(8,128)(2,1)S(1)} %get-tuple-element.12), channel_id=1, source_target_pairs={{160,0},{225,1},{128,32},{193,33},{224,64},{33,65},{192,96},{1,97}... | collective-permute-start | bytes 786440 | tf_op jit(solution)/shard_map/ppermute | solution.py:55
  65.2 18.3 %collective-permute-start.10 = (bf16[128,1024]{1,0:T(8,128)(2,1)S(1)}, bf16[128,1024]{1,0:T(8,128)(2,1)}, u32[]{:S(2)}, u32[]{:S(2)}) collective-permute-start(bf16[128,1024]{1,0:T(8,128)(2,1)S(1)} %get-tuple-element.12), channel_id=1, source_target_pairs={{96,0},{129,1},{64,32},{161,33},{160,64},{193,65},{128,96},{225,97... | collective-permute-start | bytes 786440 | tf_op jit(solution)/shard_map/ppermute | solution.py:55
  72.7 29.6 %all-to-all-start.1 = ((bf16[16,16,1024]{2,1,0:T(8,128)(2,1)}), bf16[16,16,1024]{2,1,0:T(8,128)(2,1)S(1)}, u32[]{:S(2)}, u32[]{:S(2)}) async-start(bf16[16,16,1024]{2,1,0:T(8,128)(2,1)} %bitcast.89), calls=%async_computation.1 | async-start | bytes 1048576 | tf_op jit(solution)/shard_map/all_to_all | solution.py:171
  83.5 17.4 %copy-start.2 = (bf16[1024,1024]{1,0:T(8,128)(2,1)S(1)}, bf16[1024,1024]{1,0:T(8,128)(2,1)}, u32[]{:S(2)}) copy-start(bf16[1024,1024]{1,0:T(8,128)(2,1)} %refs_16_.1) | copy-start | bytes 6291460
  86.1 14.7 %collective-permute-start.12 = (bf16[256,1024]{1,0:T(8,128)(2,1)S(1)}, bf16[256,1024]{1,0:T(8,128)(2,1)S(1)}, u32[]{:S(2)}, u32[]{:S(2)}) collective-permute-start(bf16[256,1024]{1,0:T(8,128)(2,1)S(1)} %convolution_convert_fusion.2), channel_id=1, source_target_pairs={{0,1},{1,0},{2,3},{3,2},{4,5},{5,4},{6,7},{7,6},{8,9},{9,8},{10,11... | collective-permute-start | bytes 1572872 | tf_op jit(solution)/shard_map/ppermute | solution.py:35
  87.3 13.4 %collective-permute-start.9 = (bf16[128,1024]{1,0:T(8,128)(2,1)S(1)}, bf16[128,1024]{1,0:T(8,128)(2,1)S(1)}, u32[]{:S(2)}, u32[]{:S(2)}) collective-permute-start(bf16[128,1024]{1,0:T(8,128)(2,1)S(1)} %get-tuple-element.12), channel_id=1, source_target_pairs={{224,0},{161,1},{192,32},{129,33},{32,64},{225,65},{0,96},{193,97}... | collective-permute-start | bytes 786440 | tf_op jit(solution)/shard_map/ppermute | solution.py:55
  87.3 13.5 %collective-permute-start.8 = (bf16[128,1024]{1,0:T(8,128)(2,1)S(1)}, bf16[128,1024]{1,0:T(8,128)(2,1)S(1)}, u32[]{:S(2)}, u32[]{:S(2)}) collective-permute-start(bf16[128,1024]{1,0:T(8,128)(2,1)S(1)} %get-tuple-element.12), channel_id=1, source_target_pairs={{128,0},{97,1},{160,32},{65,33},{192,64},{161,65},{224,96},{129,97... | collective-permute-start | bytes 786440 | tf_op jit(solution)/shard_map/ppermute | solution.py:55
  102.4 26.4 %copy-start.18 = (f32[1024]{0:T(1024)S(1)}, f32[1024]{0:T(1024)}, u32[]{:S(2)}) copy-start(f32[1024]{0:T(1024)} %param.9) | copy-start | bytes 12292
  102.4 26.3 %all-to-all-start.3 = ((bf16[16,16,1024]{2,1,0:T(8,128)(2,1)}), bf16[16,16,1024]{2,1,0:T(8,128)(2,1)S(1)}, u32[]{:S(2)}, u32[]{:S(2)}) async-start(bf16[16,16,1024]{2,1,0:T(8,128)(2,1)} %bitcast.88), calls=%async_computation.3 | async-start | bytes 1048576 | tf_op jit(solution)/shard_map/all_to_all | solution.py:171
  130.4 22.4 %all-to-all-start.4 = ((bf16[16,16,1024]{2,1,0:T(8,128)(2,1)}), bf16[16,16,1024]{2,1,0:T(8,128)(2,1)}, u32[]{:S(2)}, u32[]{:S(2)}) async-start(bf16[16,16,1024]{2,1,0:T(8,128)(2,1)} %broadcast_in_dim.10), calls=%async_computation.4 | async-start | bytes 1048576 | tf_op jit(solution)/shard_map/all_to_all | solution.py:180
  153.7 21.7 %all-to-all-start.2 = ((bf16[16,16,1024]{2,1,0:T(8,128)(2,1)}), bf16[16,16,1024]{2,1,0:T(8,128)(2,1)S(1)}, u32[]{:S(2)}, u32[]{:S(2)}) async-start(bf16[16,16,1024]{2,1,0:T(8,128)(2,1)} %broadcast_in_dim.9), calls=%async_computation.2 | async-start | bytes 1048576 | tf_op jit(solution)/shard_map/all_to_all | solution.py:180
  163.8 25.1 %collective-permute-start.13 = (bf16[128,1024]{1,0:T(8,128)(2,1)}, bf16[128,1024]{1,0:T(8,128)(2,1)}, u32[]{:S(2)}, u32[]{:S(2)}) collective-permute-start(bf16[128,1024]{1,0:T(8,128)(2,1)} %convolution_convert_fusion.10), channel_id=1, source_target_pairs={{0,128},{1,97},{32,160},{33,65},{64,192},{65,161},{96,224},{97,129... | collective-permute-start | bytes 786440 | tf_op jit(solution)/shard_map/ppermute | solution.py:55
  165.1 24.0 %collective-permute-start.14 = (bf16[128,1024]{1,0:T(8,128)(2,1)S(1)}, bf16[128,1024]{1,0:T(8,128)(2,1)}, u32[]{:S(2)}, u32[]{:S(2)}) collective-permute-start(bf16[128,1024]{1,0:T(8,128)(2,1)S(1)} %convolution_convert_fusion.9), channel_id=1, source_target_pairs={{0,224},{1,161},{32,192},{33,129},{64,32},{65,225},{96,0},{97,193}... | collective-permute-start | bytes 786440 | tf_op jit(solution)/shard_map/ppermute | solution.py:55
  168.8 9.7 %collective-permute-start.15 = (bf16[256,1024]{1,0:T(8,128)(2,1)}, bf16[256,1024]{1,0:T(8,128)(2,1)S(1)}, u32[]{:S(2)}, u32[]{:S(2)}) collective-permute-start(bf16[256,1024]{1,0:T(8,128)(2,1)} %bitcast.15), channel_id=1, source_target_pairs={{0,1},{1,0},{2,3},{3,2},{4,5},{5,4},{6,7},{7,6},{8,9},{9,8},{10,11... | collective-permute-start | bytes 1572872 | tf_op jit(solution)/shard_map/ppermute | solution.py:35
  175.4 24.3 %copy-start.7 = (bf16[8,16,1024]{2,1,0:T(8,128)(2,1)}, bf16[8,16,1024]{2,1,0:T(8,128)(2,1)S(1)}, u32[]{:S(2)}) copy-start(bf16[8,16,1024]{2,1,0:T(8,128)(2,1)S(1)} %get-tuple-element.26) | copy-start | bytes 786436
  178.3 14.1 %collective-permute-start.19 = (bf16[128,1024]{1,0:T(8,128)(2,1)S(1)}, bf16[128,1024]{1,0:T(8,128)(2,1)S(1)}, u32[]{:S(2)}, u32[]{:S(2)}) collective-permute-start(bf16[128,1024]{1,0:T(8,128)(2,1)S(1)} %convolution_convert_fusion.5), channel_id=1, source_target_pairs={{0,32},{1,65},{32,0},{33,97},{64,96},{65,129},{96,64},{97,161},{12... | collective-permute-start | bytes 786440 | tf_op jit(solution)/shard_map/ppermute | solution.py:55
  178.4 3.3 %collective-permute-start.7 = (bf16[256,1024]{1,0:T(8,128)(2,1)}, bf16[256,1024]{1,0:T(8,128)(2,1)S(1)}, u32[]{:S(2)}, u32[]{:S(2)}) collective-permute-start(bf16[256,1024]{1,0:T(8,128)(2,1)} %bitcast.87), channel_id=1, source_target_pairs={{0,1},{1,0},{2,3},{3,2},{4,5},{5,4},{6,7},{7,6},{8,9},{9,8},{10,11... | collective-permute-start | bytes 1572872 | tf_op jit(solution)/shard_map/ppermute | solution.py:35
  179.4 13.1 %collective-permute-start.16 = (bf16[128,1024]{1,0:T(8,128)(2,1)S(1)}, bf16[128,1024]{1,0:T(8,128)(2,1)S(1)}, u32[]{:S(2)}, u32[]{:S(2)}) collective-permute-start(bf16[128,1024]{1,0:T(8,128)(2,1)S(1)} %convolution_convert_fusion.8), channel_id=1, source_target_pairs={{0,96},{1,129},{32,64},{33,161},{64,160},{65,193},{96,128},{97,225... | collective-permute-start | bytes 786440 | tf_op jit(solution)/shard_map/ppermute | solution.py:55
  181.7 15.6 %collective-permute-start.17 = (bf16[128,1024]{1,0:T(8,128)(2,1)S(1)}, bf16[128,1024]{1,0:T(8,128)(2,1)S(1)}, u32[]{:S(2)}, u32[]{:S(2)}) collective-permute-start(bf16[128,1024]{1,0:T(8,128)(2,1)S(1)} %convolution_convert_fusion.7), channel_id=1, source_target_pairs={{0,160},{1,225},{32,128},{33,193},{64,224},{65,33},{96,192},{97,1}... | collective-permute-start | bytes 786440 | tf_op jit(solution)/shard_map/ppermute | solution.py:55
  188.8 9.6 %collective-permute-start.20 = (bf16[128,1024]{1,0:T(8,128)(2,1)S(1)}, bf16[128,1024]{1,0:T(8,128)(2,1)S(1)}, u32[]{:S(2)}, u32[]{:S(2)}) collective-permute-start(bf16[128,1024]{1,0:T(8,128)(2,1)S(1)} %convolution_convert_fusion.4), channel_id=1, source_target_pairs={{0,64},{1,33},{32,96},{33,1},{64,128},{65,97},{96,160},{97,65},{12... | collective-permute-start | bytes 786440 | tf_op jit(solution)/shard_map/ppermute | solution.py:55
  189.2 10.6 %collective-permute-start.18 = (bf16[128,1024]{1,0:T(8,128)(2,1)S(1)}, bf16[128,1024]{1,0:T(8,128)(2,1)S(1)}, u32[]{:S(2)}, u32[]{:S(2)}) collective-permute-start(bf16[128,1024]{1,0:T(8,128)(2,1)S(1)} %convolution_convert_fusion.6), channel_id=1, source_target_pairs={{0,192},{1,193},{32,224},{33,225},{64,0},{65,1},{96,32},{97,33},{1... | collective-permute-start | bytes 786440 | tf_op jit(solution)/shard_map/ppermute | solution.py:55
  203.5 31.9 %all-to-all-start.5 = ((bf16[8,128,1024]{2,1,0:T(8,128)(2,1)}), bf16[8,128,1024]{2,1,0:T(8,128)(2,1)}, u32[]{:S(2)}, u32[]{:S(2)}) async-start(bf16[8,128,1024]{2,1,0:T(8,128)(2,1)} %broadcast_in_dim.11), calls=%async_computation.5 | async-start | bytes 4194304 | tf_op jit(solution)/shard_map/all_to_all | solution.py:203
  (14 other events, 74.5 us)
where the time goes:
time: 243 us; the launch traced here: 241 us
  waiting for transfers between devices  109 us (45%)
  starting transfers between devices  72.1 us (30%)
  matrix products  31.8 us (13%)
  Pallas kernels  12.8 us (5%)
  local copies, waits for them, and re-layouts  8.55 us (4%)
  other arithmetic  5.98 us (2%)
    ppermute x14, waiting for transfers between devices, move(): return lax.ppermute(value, ('y', 'xl', 'core'), pairs)  28.3 us
    ppermute x7, waiting for transfers between devices, swap(): return lax.ppermute(value, axis, [(i, i ^ mask) for i in range(size)])  24.7 us
    ppermute x14, starting transfers between devices, move(): return lax.ppermute(value, ('y', 'xl', 'core'), pairs)  23.5 us
    all_to_all x2, waiting for transfers between devices, gather_lat(): mine = lax.all_to_all(errors, RING, 0, 0).reshape(2 * block, -1)  23.1 us
    all_to_all x2, starting transfers between devices, scatter_lat(): shares = lax.all_to_all(shares, RING, 0, 0)  20.5 us
    dot_general x6, matrix products, dot(): return jnp.dot(a, b, preferred_element_type=f32)  19.3 us
    all_to_all x1, waiting for transfers between devices, per_device(): grad_pre = lax.all_to_all(grad_pre, SRC, 0, 0).reshape(row_count, -1)  16.6 us
    all_to_all x2, waiting for transfers between devices, scatter_lat(): shares = lax.all_to_all(shares, RING, 0, 0)  16.4 us
  transfers between devices with their start and end apart: 27, of which 14 were waited for; matrix products, arithmetic and copies ran while one was open for 9% of the time, Pallas kernels for 5%

commit v1 on v0

--- a/solution.py
+++ b/solution.py
@@ -139,15 +139,8 @@
     partial = lax.all_to_all(partial, SRC, 0, 0)
 
     squares = jnp.sum(jnp.square(decoder.astype(f32)), axis=1)
-    own_sq = squares + swap(squares, "xl", N_XL, 1)
-    own_sq = own_sq + swap(own_sq, "y", N_Y, 1)
-    other_sq = swap(own_sq, "y", N_Y, 2)
-    own_norm = jnp.sqrt(own_sq + EPSILON)
-    penalty = PENALTY * (own_norm + jnp.sqrt(other_sq + EPSILON))
     res_t = transpose(residual_rows)
-    enc_bias, own_norm, penalty, res_t = lax.optimization_barrier(
-        (enc_bias, own_norm, penalty, res_t)
-    )
+    enc_bias, squares, res_t = lax.optimization_barrier((enc_bias, squares, res_t))
 
     pre_act = jnp.broadcast_to(enc_bias[None, :], partial.shape[1:])
     for i in range(N_SRC):
@@ -162,39 +155,48 @@
     far = [move(latent_far, FAR, slot, False) for slot in range(4)]
     near = [jnp.where(first, latent, mate), near1, jnp.where(first, mate, latent), near3]
 
-    def scatter_lat(blocks, offsets):
+    def core_sum(blocks):
         theirs = dot(jnp.concatenate(blocks[2:], axis=0), decoder).astype(bf16)
         theirs = swap(theirs, "core", N_CORE, 1)
         mine = dot(jnp.concatenate(blocks[:2], axis=0), decoder) + theirs.astype(f32)
-        rows = 2 * block // N_RING
-        shares = mine.astype(bf16).reshape(N_RING, rows, -1)
-        shares = lax.all_to_all(shares, RING, 0, 0)
-        recon = jnp.sum(shares.astype(f32), axis=0) + dec_bias[None, :]
-        per_block = N_RING // 2
-        start = jnp.where(ring < per_block, owner_row(offsets, 0), owner_row(offsets, 1))
-        target = rows_of(start + (ring % per_block) * rows, rows)
-        return (recon - target.astype(f32)).astype(bf16)
-
-    def gather_lat(errors):
-        errors = jnp.broadcast_to(errors[None], (N_RING,) + errors.shape)
-        mine = lax.all_to_all(errors, RING, 0, 0).reshape(2 * block, -1)
-        theirs = swap(mine, "core", N_CORE, 1)
-        return [mine[:block], mine[block:], theirs[:block], theirs[block:]]
-
-    near_share = scatter_lat(near, NEAR)
-    far_share = scatter_lat(far, FAR)
-    far_err = gather_lat(far_share)
-    near_share, _ = lax.optimization_barrier((near_share, far_err[0][:8, :128]))
-    near_err = gather_lat(near_share)
+        return mine.astype(bf16)
+
+    rows = 4 * block // N_RING
+    shares = jnp.concatenate([core_sum(near), core_sum(far)], axis=0)
+    squares, shares = lax.optimization_barrier((squares, shares))
+    shares = lax.all_to_all(shares.reshape(N_RING, rows, -1), RING, 0, 0)
+
+    own_sq = squares + swap(squares, "xl", N_XL, 1)
+    own_sq = own_sq + swap(own_sq, "y", N_Y, 1)
+    other_sq = swap(own_sq, "y", N_Y, 2)
+    own_norm = jnp.sqrt(own_sq + EPSILON)
+    penalty = PENALTY * (own_norm + jnp.sqrt(other_sq + EPSILON))
+    dec_bias, own_norm, penalty = lax.optimization_barrier((dec_bias, own_norm, penalty))
+
+    recon = jnp.broadcast_to(dec_bias[None, :], shares.shape[1:])
+    for i in range(N_RING):
+        recon = recon + shares[i].astype(f32)
+    per_block = N_RING // 4
+    starts = jnp.stack([owner_row(o, slot) for o in (NEAR, FAR) for slot in range(2)])
+    start = lax.dynamic_index_in_dim(starts, ring // per_block, 0, False)
+    target = rows_of(start + (ring % per_block) * rows, rows)
+    errors = (recon - target.astype(f32)).astype(bf16)
+    errors = jnp.broadcast_to(errors[None], (N_RING,) + errors.shape)
+    mine = lax.all_to_all(errors, RING, 0, 0).reshape(4, block, -1)
+    theirs = swap(mine, "core", N_CORE, 1)
+    near_err = [mine[0], mine[1], theirs[0], theirs[1]]
+    far_err = [mine[2], mine[3], theirs[2], theirs[3]]
 
     got = []
-    for slot in range(4):
+    for slot in range(2):
         got.append(move(dot_t(far_err[slot], decoder).astype(bf16), FAR, slot, True))
+    got.append(move(dot_t(near_err[1], decoder).astype(bf16), NEAR, 1, True))
+    for slot in range(2, 4):
+        got.append(move(dot_t(far_err[slot], decoder).astype(bf16), FAR, slot, True))
+    got.append(move(dot_t(near_err[3], decoder).astype(bf16), NEAR, 3, True))
     sent = jnp.where(first, near_err[2], near_err[0])
     kept = jnp.where(first, near_err[0], near_err[2])
     got.append(move(dot_t(sent, decoder).astype(bf16), twin, 0, True))
-    got.append(move(dot_t(near_err[1], decoder).astype(bf16), NEAR, 1, True))
-    got.append(move(dot_t(near_err[3], decoder).astype(bf16), NEAR, 3, True))
     act_grad = dot_t(kept, decoder) + penalty[None, :]
     for g in got:
         act_grad = act_grad + g.astype(f32)

time: 243 us -> 223 us (0.918)
  blocking collectives: 0 us -> 32.7 us
  starting transfers between devices: 72.1 us -> 49.7 us
  waiting for transfers between devices: 109 us -> 87.4 us
  matrix products: 31.8 us -> 22.8 us
  local copies, waits for them, and re-layouts: 8.55 us -> 5.78 us
    all_to_all x0 -> x1, blocking collectives: none -> 32.7 us  [per_device(): mine = lax.all_to_all(errors, RING, 0, 0).reshape(4, block, -1)]
    all_to_all x4 -> x1, waiting for transfers between devices: 39.5 us -> 12.8 us  [per_device(): shares = lax.all_to_all(shares.reshape(N_RING, rows, -1), RING, 0, 0)]
    all_to_all x4 -> x1, starting transfers between devices: 32 us -> 10.7 us  [per_device(): shares = lax.all_to_all(shares.reshape(N_RING, rows, -1), RING, 0, 0)]
    all_to_all x1, waiting for transfers between devices: 0.01 us -> 20.9 us  [per_device(): partial = lax.all_to_all(partial, SRC, 0, 0)]
    ppermute x7 -> x6, waiting for transfers between devices: 24.7 us -> 8.03 us  [swap(): return lax.ppermute(value, axis, [(i, i ^ mask) for i in range(size)])]
    dot_general x8, matrix products: 12.4 us -> 6.97 us  [dot_t(): return jnp.einsum('bk,jk->bj', a, b, preferred_element_type=f32)]
    dot_general x6, matrix products: 19.3 us -> 15.8 us  [dot(): return jnp.dot(a, b, preferred_element_type=f32)]
    slice x4 -> x1, local copies, waits for them, and re-layouts: 3 us -> 0.09 us  [per_device(): far_err = [mine[2], mine[3], theirs[2], theirs[3]]]
  transfers between devices with their start and end apart: 27 -> 23, of which waited for: 14 -> 12; matrix products, arithmetic and copies ran while one was open for 9% -> 7% of each run, Pallas kernels for 5% -> 6%
where the time goes in v1:
time: 223 us; the launch traced here: 221 us
  waiting for transfers between devices  87.4 us (39%)
  starting transfers between devices  49.7 us (22%)
  blocking collectives  32.7 us (15%)
  matrix products  22.8 us (10%)
  Pallas kernels  12.8 us (6%)
  other arithmetic  8.18 us (4%)
  local copies, waits for them, and re-layouts  5.78 us (3%)
    all_to_all x1, blocking collectives, per_device(): mine = lax.all_to_all(errors, RING, 0, 0).reshape(4, block, -1)  32.7 us
    ppermute x14, waiting for transfers between devices, move(): return lax.ppermute(value, ('y', 'xl', 'core'), pairs)  28 us
    ppermute x14, starting transfers between devices, move(): return lax.ppermute(value, ('y', 'xl', 'core'), pairs)  22.9 us
    all_to_all x1, waiting for transfers between devices, per_device(): partial = lax.all_to_all(partial, SRC, 0, 0)  20.9 us
    all_to_all x1, waiting for transfers between devices, per_device(): grad_pre = lax.all_to_all(grad_pre, SRC, 0, 0).reshape(row_count, -1)  17.7 us
    dot_general x6, matrix products, dot(): return jnp.dot(a, b, preferred_element_type=f32)  15.8 us
    all_to_all x1, waiting for transfers between devices, per_device(): shares = lax.all_to_all(shares.reshape(N_RING, rows, -1), RING, 0, 0)  12.8 us
    all_to_all x1, starting transfers between devices, per_device(): shares = lax.all_to_all(shares.reshape(N_RING, rows, -1), RING, 0, 0)  10.7 us
  transfers between devices with their start and end apart: 23, of which 12 were waited for; matrix products, arithmetic and copies ran while one was open for 7% of the time, Pallas kernels for 6%

profile of v1, /device:TPU:32, one launch (start us, length us, event | category | flops | bytes accessed | tf_op | source)
XLA Modules:
  0.0 221.1 jit_solution(4439949317241868758)
XLA Ops:
  0.6 1.6 copy-done
  2.2 5.2 %convolution_convert_fusion.1 = bf16[1024,1024]{1,0:T(8,128)(2,1)} fusion(bf16[1024,1024]{1,0:T(8,128)(2,1)} %in_ref.1, bf16[1024,1024]{1,0:T(8,128)(2,1)S(1)} %copy-done), kind=kOutput, calls=%fused_computation.2 | convolution fusion | flops 2148532224 | bytes 6291456 | tf_op jit(solution)/shard_map/dot_general | solution.py:59
  7.5 5.4 %all-to-all-start = ((bf16[8,128,1024]{2,1,0:T(8,128)(2,1)}), bf16[8,128,1024]{2,1,0:T(8,128)(2,1)}, u32[]{:S(2)}, u32[]{:S(2)}) async-start(bf16[8,128,1024]{2,1,0:T(8,128)(2,1)} %bitcast.188), calls=%async_computation | async-start | bytes 4194304 | tf_op jit(solution)/shard_map/all_to_all | solution.py:139
  12.9 4.1 %transpose.12 = bf16[1024,1024]{1,0:T(8,128)(2,1)} custom-call(bf16[1024,1024]{1,0:T(8,128)(2,1)} %in_ref.1), custom_call_target="tpu_custom_call" | custom-call | tf_op jit(solution)/shard_map/transpose/pallas_call | solution.py:106
  17.0 2.1 multiply_reduce_fusion
  19.1 20.9 %all-to-all-done = bf16[8,128,1024]{2,1,0:T(8,128)(2,1)} async-done(((bf16[8,128,1024]{2,1,0:T(8,128)(2,1)}), bf16[8,128,1024]{2,1,0:T(8,128)(2,1)}, u32[]{:S(2)}, u32[]{:S(2)}) %all-to-all-start) | async-done | bytes 2097184 | tf_op jit(solution)/shard_map/all_to_all | solution.py:139
  40.0 2.9 %fusion.13 = (bf16[128,1024]{1,0:T(8,128)(2,1)S(1)}, f32[128,1024]{1,0:T(8,128)}) fusion(bf16[8,128,1024]{2,1,0:T(8,128)(2,1)} %all-to-all-done, f32[1024]{0:T(1024)S(1)} %copy-done.17), kind=kLoop, calls=%fused_computation.30 | loop fusion | flops 3276800 | bytes 2887680 | tf_op jit(solution)/shard_map/convert_element_type | solution.py:148
  43.1 3.0 %collective-permute-start.2 = (bf16[128,1024]{1,0:T(8,128)(2,1)S(1)}, bf16[128,1024]{1,0:T(8,128)(2,1)S(1)}, u32[]{:S(2)}, u32[]{:S(2)}) collective-permute-start(bf16[128,1024]{1,0:T(8,128)(2,1)S(1)} %get-tuple-element.16), channel_id=1, source_target_pairs={{64,0},{33,1},{96,32},{1,33},{128,64},{97,65},{160,96},{65,97},{19... | collective-permute-start | bytes 786440 | tf_op jit(solution)/shard_map/ppermute | solution.py:55
  46.1 4.8 %collective-permute-done = bf16[128,1024]{1,0:T(8,128)(2,1)S(1)} collective-permute-done((bf16[128,1024]{1,0:T(8,128)(2,1)S(1)}, bf16[128,1024]{1,0:T(8,128)(2,1)S(1)}, u32[]{:S(2)}, u32[]{:S(2)}) %collective-permute-start) | collective-permute-done | bytes 262176 | tf_op jit(solution)/shard_map/ppermute | solution.py:55
  52.2 1.3 collective-permute-start.6
  54.6 2.6 %convolution_convert_fusion.3 = bf16[256,1024]{1,0:T(8,128)(2,1)S(1)} fusion(bf16[1024,1024]{1,0:T(8,128)(2,1)} %refs_16_.1, bf16[128,1024]{1,0:T(8,128)(2,1)S(1)} %collective-permute-done.2.refs_3_, bf16[128,1024]{1,0:T(8,128)(2,1)S(1)} %get-tuple-element.35.refs_2_), kind=kOutput, calls=%fused_computation.7 | convolution fusion | flops 538181632 | bytes 3145728 | tf_op jit(solution)/shard_map/dot_general | solution.py:59
  57.3 2.5 %collective-permute-start.1 = (bf16[128,1024]{1,0:T(8,128)(2,1)S(1)}, bf16[128,1024]{1,0:T(8,128)(2,1)S(1)}, u32[]{:S(2)}, u32[]{:S(2)}) collective-permute-start(bf16[128,1024]{1,0:T(8,128)(2,1)S(1)} %get-tuple-element.16), channel_id=1, source_target_pairs={{32,0},{65,1},{0,32},{97,33},{96,64},{129,65},{64,96},{161,97},{16... | collective-permute-start | bytes 786440 | tf_op jit(solution)/shard_map/ppermute | solution.py:55
  62.4 2.6 %collective-permute-start.5 = (bf16[128,1024]{1,0:T(8,128)(2,1)S(1)}, bf16[128,1024]{1,0:T(8,128)(2,1)S(1)}, u32[]{:S(2)}, u32[]{:S(2)}) collective-permute-start(bf16[128,1024]{1,0:T(8,128)(2,1)S(1)} %get-tuple-element.16), channel_id=1, source_target_pairs={{224,0},{161,1},{192,32},{129,33},{32,64},{225,65},{0,96},{193,97}... | collective-permute-start | bytes 786440 | tf_op jit(solution)/shard_map/ppermute | solution.py:55
  65.0 2.2 %collective-permute-start.4 = (bf16[128,1024]{1,0:T(8,128)(2,1)S(1)}, bf16[128,1024]{1,0:T(8,128)(2,1)S(1)}, u32[]{:S(2)}, u32[]{:S(2)}) collective-permute-start(bf16[128,1024]{1,0:T(8,128)(2,1)S(1)} %get-tuple-element.16), channel_id=1, source_target_pairs={{128,0},{97,1},{160,32},{65,33},{192,64},{161,65},{224,96},{129,97... | collective-permute-start | bytes 786440 | tf_op jit(solution)/shard_map/ppermute | solution.py:55
  68.1 5.6 %collective-permute-done.5.refs_5_ = bf16[128,1024]{1,0:T(8,128)(2,1)S(1)} collective-permute-done((bf16[128,1024]{1,0:T(8,128)(2,1)S(1)}, bf16[128,1024]{1,0:T(8,128)(2,1)S(1)}, u32[]{:S(2)}, u32[]{:S(2)}) %collective-permute-start.5) | collective-permute-done | bytes 262176 | tf_op jit(solution)/shard_map/ppermute | solution.py:55
  73.6 2.4 %collective-permute-done.4.refs_4_ = bf16[128,1024]{1,0:T(8,128)(2,1)S(1)} collective-permute-done((bf16[128,1024]{1,0:T(8,128)(2,1)S(1)}, bf16[128,1024]{1,0:T(8,128)(2,1)S(1)}, u32[]{:S(2)}, u32[]{:S(2)}) %collective-permute-start.4) | collective-permute-done | bytes 262176 | tf_op jit(solution)/shard_map/ppermute | solution.py:55
  77.8 10.7 %all-to-all-start.1 = ((bf16[16,32,1024]{2,1,0:T(8,128)(2,1)}), bf16[16,32,1024]{2,1,0:T(8,128)(2,1)S(1)}, u32[]{:S(2)}, u32[]{:S(2)}) async-start(bf16[16,32,1024]{2,1,0:T(8,128)(2,1)} %bitcast.177), calls=%async_computation.1 | async-start | bytes 2097152 | tf_op jit(solution)/shard_map/all_to_all | solution.py:167
  89.2 3.4 %collective-permute-done.9 = f32[1024]{0:T(1024)S(1)} collective-permute-done((f32[1024]{0:T(1024)S(1)}, f32[1024]{0:T(1024)S(1)}, u32[]{:S(2)}, u32[]{:S(2)}) %collective-permute-start.9) | collective-permute-done | bytes 4128 | tf_op jit(solution)/shard_map/ppermute | solution.py:35
  92.6 3.8 %collective-permute-start.10 = (f32[1024]{0:T(1024)S(1)}, f32[1024]{0:T(1024)S(1)}, u32[]{:S(2)}, u32[]{:S(2)}) collective-permute-start(f32[1024]{0:T(1024)S(1)} %add.201), channel_id=1, source_target_pairs={{0,64},{64,0},{128,192},{192,128},{1,65},{65,1},{129,193},{193,129... | collective-permute-start | bytes 12296 | tf_op jit(solution)/shard_map/ppermute | solution.py:35
  96.4 1.6 collective-permute-done.10
  100.0 3.0 %collective-permute-done.11 = f32[1024]{0:T(1024)S(1)} collective-permute-done((f32[1024]{0:T(1024)S(1)}, f32[1024]{0:T(1024)S(1)}, u32[]{:S(2)}, u32[]{:S(2)}) %collective-permute-start.11) | collective-permute-done | bytes 4128 | tf_op jit(solution)/shard_map/ppermute | solution.py:35
  103.1 12.8 %all-to-all-done.1 = bf16[16,32,1024]{2,1,0:T(8,128)(2,1)S(1)} async-done(((bf16[16,32,1024]{2,1,0:T(8,128)(2,1)}), bf16[16,32,1024]{2,1,0:T(8,128)(2,1)S(1)}, u32[]{:S(2)}, u32[]{:S(2)}) %all-to-all-start.1) | async-done | bytes 1048608 | tf_op jit(solution)/shard_map/all_to_all | solution.py:167
  117.1 32.7 %all_to_all.20 = bf16[16,32,1024]{2,1,0:T(8,128)(2,1)S(1)} all-to-all(bf16[16,32,1024]{2,1,0:T(8,128)(2,1)S(1)} %broadcast_in_dim.10), channel_id=1, replica_groups=mesh['y'=4,'xl'=2,'xh'=2,'z'=8,'core'=2] {'xh','z'}, dimensions={0} | all-to-all | bytes 2097152 | tf_op jit(solution)/shard_map/all_to_all | solution.py:185
  150.8 3.3 %collective-permute-start.14 = (bf16[128,1024]{1,0:T(8,128)(2,1)S(1)}, bf16[128,1024]{1,0:T(8,128)(2,1)S(1)}, u32[]{:S(2)}, u32[]{:S(2)}) collective-permute-start(bf16[128,1024]{1,0:T(8,128)(2,1)S(1)} %convolution_convert_fusion.9), channel_id=1, source_target_pairs={{0,224},{1,161},{32,192},{33,129},{64,32},{65,225},{96,0},{97,193}... | collective-permute-start | bytes 786440 | tf_op jit(solution)/shard_map/ppermute | solution.py:55
  157.8 2.3 %collective-permute-start.18 = (bf16[128,1024]{1,0:T(8,128)(2,1)S(1)}, bf16[128,1024]{1,0:T(8,128)(2,1)S(1)}, u32[]{:S(2)}, u32[]{:S(2)}) collective-permute-start(bf16[128,1024]{1,0:T(8,128)(2,1)S(1)} %convolution_convert_fusion.5), channel_id=1, source_target_pairs={{0,64},{1,33},{32,96},{33,1},{64,128},{65,97},{96,160},{97,65},{12... | collective-permute-start | bytes 786440 | tf_op jit(solution)/shard_map/ppermute | solution.py:55
  164.7 4.5 %collective-permute-done.13 = bf16[128,1024]{1,0:T(8,128)(2,1)S(1)} collective-permute-done((bf16[128,1024]{1,0:T(8,128)(2,1)S(1)}, bf16[128,1024]{1,0:T(8,128)(2,1)S(1)}, u32[]{:S(2)}, u32[]{:S(2)}) %collective-permute-start.13) | collective-permute-done | bytes 262176 | tf_op jit(solution)/shard_map/ppermute | solution.py:55
  170.1 10.1 %collective-permute-done.18 = bf16[128,1024]{1,0:T(8,128)(2,1)S(1)} collective-permute-done((bf16[128,1024]{1,0:T(8,128)(2,1)S(1)}, bf16[128,1024]{1,0:T(8,128)(2,1)S(1)}, u32[]{:S(2)}, u32[]{:S(2)}) %collective-permute-start.18) | collective-permute-done | bytes 262176 | tf_op jit(solution)/shard_map/ppermute | solution.py:55
  181.3 1.6 broadcast_in_dim.11
  182.8 4.4 %all-to-all-start.3 = ((bf16[8,128,1024]{2,1,0:T(8,128)(2,1)}), bf16[8,128,1024]{2,1,0:T(8,128)(2,1)}, u32[]{:S(2)}, u32[]{:S(2)}) async-start(bf16[8,128,1024]{2,1,0:T(8,128)(2,1)} %broadcast_in_dim.11), calls=%async_computation.3 | async-start | bytes 4194304 | tf_op jit(solution)/shard_map/all_to_all | solution.py:205
  188.9 8.7 %decoder_grad.1 = bf16[1024,1024]{1,0:T(8,128)(2,1)} custom-call(bf16[128,1024]{1,0:T(8,128)(2,1)} %copy-done.7, bf16[128,1024]{1,0:T(8,128)(2,1)} %copy-done.13, bf16[128,1024]{1,0:T(8,128)(2,1)} %copy-done.8, bf16[128,1024]{1,0:T(8,128)(2,1)} %copy-done.10, bf16[128,1024]{1,0:T(8,128)(2,1)} %copy-done.15, bf16[128,1024]{1,0:T(8,128)(2,1)} %copy-done.14, ...), custom_call_target="tpu_custom_call" | custom-call | tf_op jit(solution)/shard_map/decoder_grad/pallas_call | solution.py:84
  197.5 17.7 %all-to-all-done.3 = bf16[8,128,1024]{2,1,0:T(8,128)(2,1)} async-done(((bf16[8,128,1024]{2,1,0:T(8,128)(2,1)}), bf16[8,128,1024]{2,1,0:T(8,128)(2,1)}, u32[]{:S(2)}, u32[]{:S(2)}) %all-to-all-start.3) | async-done | bytes 2097184 | tf_op jit(solution)/shard_map/all_to_all | solution.py:205
  215.2 5.9 %convolution_convert_fusion = bf16[1024,1024]{1,0:T(8,128)(2,1)} fusion(bf16[1024,1024]{1,0:T(8,128)(2,1)} %transpose.12, bf16[1024,1024]{1,0:T(8,128)(2,1)} %bitcast.40), kind=kOutput, calls=%fused_computation.1 | convolution fusion | flops 2148532224 | bytes 6291456 | tf_op jit(solution)/shard_map/dot_general | solution.py:59
  (84 shorter events, 23.7 us)
Async XLA Ops:
  7.5 32.5 %all-to-all-start = ((bf16[8,128,1024]{2,1,0:T(8,128)(2,1)}), bf16[8,128,1024]{2,1,0:T(8,128)(2,1)}, u32[]{:S(2)}, u32[]{:S(2)}) async-start(bf16[8,128,1024]{2,1,0:T(8,128)(2,1)} %bitcast.188), calls=%async_computation | async-start | bytes 4194304 | tf_op jit(solution)/shard_map/all_to_all | solution.py:139
  17.0 23.0 %copy-start.17 = (f32[1024]{0:T(1024)S(1)}, f32[1024]{0:T(1024)}, u32[]{:S(2)}) copy-start(f32[1024]{0:T(1024)} %param.8) | copy-start | bytes 12292
  42.8 8.1 %collective-permute-start = (bf16[128,1024]{1,0:T(8,128)(2,1)S(1)}, bf16[128,1024]{1,0:T(8,128)(2,1)S(1)}, u32[]{:S(2)}, u32[]{:S(2)}) collective-permute-start(bf16[128,1024]{1,0:T(8,128)(2,1)S(1)} %get-tuple-element.16), channel_id=1, source_target_pairs={{192,0},{193,1},{224,32},{225,33},{0,64},{1,65},{32,96},{33,97},{6... | collective-permute-start | bytes 786440 | tf_op jit(solution)/shard_map/ppermute | solution.py:55
  43.1 11.5 %collective-permute-start.2 = (bf16[128,1024]{1,0:T(8,128)(2,1)S(1)}, bf16[128,1024]{1,0:T(8,128)(2,1)S(1)}, u32[]{:S(2)}, u32[]{:S(2)}) collective-permute-start(bf16[128,1024]{1,0:T(8,128)(2,1)S(1)} %get-tuple-element.16), channel_id=1, source_target_pairs={{64,0},{33,1},{96,32},{1,33},{128,64},{97,65},{160,96},{65,97},{19... | collective-permute-start | bytes 786440 | tf_op jit(solution)/shard_map/ppermute | solution.py:55
  50.9 9.7 %collective-permute-start.7 = (bf16[128,1024]{1,0:T(8,128)(2,1)S(1)}, bf16[128,1024]{1,0:T(8,128)(2,1)S(1)}, u32[]{:S(2)}, u32[]{:S(2)}) collective-permute-start(bf16[128,1024]{1,0:T(8,128)(2,1)S(1)} %get-tuple-element.16), channel_id=1, source_target_pairs={{160,0},{225,1},{128,32},{193,33},{224,64},{33,65},{192,96},{1,97}... | collective-permute-start | bytes 786440 | tf_op jit(solution)/shard_map/ppermute | solution.py:55
  52.2 8.4 %collective-permute-start.6 = (bf16[128,1024]{1,0:T(8,128)(2,1)S(1)}, bf16[128,1024]{1,0:T(8,128)(2,1)S(1)}, u32[]{:S(2)}, u32[]{:S(2)}) collective-permute-start(bf16[128,1024]{1,0:T(8,128)(2,1)S(1)} %get-tuple-element.16), channel_id=1, source_target_pairs={{96,0},{129,1},{64,32},{161,33},{160,64},{193,65},{128,96},{225,97... | collective-permute-start | bytes 786440 | tf_op jit(solution)/shard_map/ppermute | solution.py:55
  54.6 6.8 %copy-start.8 = (bf16[128,1024]{1,0:T(8,128)(2,1)}, bf16[128,1024]{1,0:T(8,128)(2,1)S(1)}, u32[]{:S(2)}) copy-start(bf16[128,1024]{1,0:T(8,128)(2,1)S(1)} %get-tuple-element.35.refs_2_) | copy-start | bytes 786436
  54.6 12.7 %copy-start.7 = (bf16[128,1024]{1,0:T(8,128)(2,1)}, bf16[128,1024]{1,0:T(8,128)(2,1)S(1)}, u32[]{:S(2)}) copy-start(bf16[128,1024]{1,0:T(8,128)(2,1)S(1)} %get-tuple-element.34.refs_0_) | copy-start | bytes 786436
  54.6 6.7 %copy-start.10 = (bf16[128,1024]{1,0:T(8,128)(2,1)}, bf16[128,1024]{1,0:T(8,128)(2,1)S(1)}, u32[]{:S(2)}) copy-start(bf16[128,1024]{1,0:T(8,128)(2,1)S(1)} %collective-permute-done.2.refs_3_) | copy-start | bytes 786436
  57.2 10.1 %collective-permute-start.3 = (bf16[256,1024]{1,0:T(8,128)(2,1)S(1)}, bf16[256,1024]{1,0:T(8,128)(2,1)S(1)}, u32[]{:S(2)}, u32[]{:S(2)}) collective-permute-start(bf16[256,1024]{1,0:T(8,128)(2,1)S(1)} %convolution_convert_fusion.3), channel_id=1, source_target_pairs={{0,1},{1,0},{2,3},{3,2},{4,5},{5,4},{6,7},{7,6},{8,9},{9,8},{10,11... | collective-permute-start | bytes 1572872 | tf_op jit(solution)/shard_map/ppermute | solution.py:35
  57.3 10.0 %collective-permute-start.1 = (bf16[128,1024]{1,0:T(8,128)(2,1)S(1)}, bf16[128,1024]{1,0:T(8,128)(2,1)S(1)}, u32[]{:S(2)}, u32[]{:S(2)}) collective-permute-start(bf16[128,1024]{1,0:T(8,128)(2,1)S(1)} %get-tuple-element.16), channel_id=1, source_target_pairs={{32,0},{65,1},{0,32},{97,33},{96,64},{129,65},{64,96},{161,97},{16... | collective-permute-start | bytes 786440 | tf_op jit(solution)/shard_map/ppermute | solution.py:55
  60.6 7.5 %copy-start.12 = (bf16[128,1024]{1,0:T(8,128)(2,1)}, bf16[128,1024]{1,0:T(8,128)(2,1)S(1)}, u32[]{:S(2)}) copy-start(bf16[128,1024]{1,0:T(8,128)(2,1)S(1)} %collective-permute-done.6.refs_6_) | copy-start | bytes 786436
  61.3 14.7 %collective-permute-start.8 = (bf16[256,1024]{1,0:T(8,128)(2,1)S(1)}, bf16[256,1024]{1,0:T(8,128)(2,1)S(1)}, u32[]{:S(2)}, u32[]{:S(2)}) collective-permute-start(bf16[256,1024]{1,0:T(8,128)(2,1)S(1)} %convolution_convert_fusion.2), channel_id=1, source_target_pairs={{0,1},{1,0},{2,3},{3,2},{4,5},{5,4},{6,7},{7,6},{8,9},{9,8},{10,11... | collective-permute-start | bytes 1572872 | tf_op jit(solution)/shard_map/ppermute | solution.py:35
  62.4 11.2 %collective-permute-start.5 = (bf16[128,1024]{1,0:T(8,128)(2,1)S(1)}, bf16[128,1024]{1,0:T(8,128)(2,1)S(1)}, u32[]{:S(2)}, u32[]{:S(2)}) collective-permute-start(bf16[128,1024]{1,0:T(8,128)(2,1)S(1)} %get-tuple-element.16), channel_id=1, source_target_pairs={{224,0},{161,1},{192,32},{129,33},{32,64},{225,65},{0,96},{193,97}... | collective-permute-start | bytes 786440 | tf_op jit(solution)/shard_map/ppermute | solution.py:55
  65.0 11.0 %collective-permute-start.4 = (bf16[128,1024]{1,0:T(8,128)(2,1)S(1)}, bf16[128,1024]{1,0:T(8,128)(2,1)S(1)}, u32[]{:S(2)}, u32[]{:S(2)}) collective-permute-start(bf16[128,1024]{1,0:T(8,128)(2,1)S(1)} %get-tuple-element.16), channel_id=1, source_target_pairs={{128,0},{97,1},{160,32},{65,33},{192,64},{161,65},{224,96},{129,97... | collective-permute-start | bytes 786440 | tf_op jit(solution)/shard_map/ppermute | solution.py:55
  76.7 39.1 %copy-start.18 = (f32[1024]{0:T(1024)S(1)}, f32[1024]{0:T(1024)}, u32[]{:S(2)}) copy-start(f32[1024]{0:T(1024)} %param.9) | copy-start | bytes 12292
  77.8 38.1 %all-to-all-start.1 = ((bf16[16,32,1024]{2,1,0:T(8,128)(2,1)}), bf16[16,32,1024]{2,1,0:T(8,128)(2,1)S(1)}, u32[]{:S(2)}, u32[]{:S(2)}) async-start(bf16[16,32,1024]{2,1,0:T(8,128)(2,1)} %bitcast.177), calls=%async_computation.1 | async-start | bytes 2097152 | tf_op jit(solution)/shard_map/all_to_all | solution.py:167
  88.5 4.0 %collective-permute-start.9 = (f32[1024]{0:T(1024)S(1)}, f32[1024]{0:T(1024)S(1)}, u32[]{:S(2)}, u32[]{:S(2)}) collective-permute-start(f32[1024]{0:T(1024)S(1)} %multiply_reduce_fusion), channel_id=1, source_target_pairs={{0,32},{32,0},{1,33},{33,1},{2,34},{34,2},{3,35},{35,3},{4,36},{36... | collective-permute-start | bytes 12296 | tf_op jit(solution)/shard_map/ppermute | solution.py:35
  92.6 5.4 %collective-permute-start.10 = (f32[1024]{0:T(1024)S(1)}, f32[1024]{0:T(1024)S(1)}, u32[]{:S(2)}, u32[]{:S(2)}) collective-permute-start(f32[1024]{0:T(1024)S(1)} %add.201), channel_id=1, source_target_pairs={{0,64},{64,0},{128,192},{192,128},{1,65},{65,1},{129,193},{193,129... | collective-permute-start | bytes 12296 | tf_op jit(solution)/shard_map/ppermute | solution.py:35
  98.0 5.1 %collective-permute-start.11 = (f32[1024]{0:T(1024)S(1)}, f32[1024]{0:T(1024)S(1)}, u32[]{:S(2)}, u32[]{:S(2)}) collective-permute-start(f32[1024]{0:T(1024)S(1)} %get-tuple-element.23), channel_id=1, source_target_pairs={{0,128},{64,192},{128,0},{192,64},{1,129},{65,193},{129,1},{193,65... | collective-permute-start | bytes 12296 | tf_op jit(solution)/shard_map/ppermute | solution.py:35
  117.1 32.9 %copy-start.2 = (bf16[1024,1024]{1,0:T(8,128)(2,1)S(1)}, bf16[1024,1024]{1,0:T(8,128)(2,1)}, u32[]{:S(2)}) copy-start(bf16[1024,1024]{1,0:T(8,128)(2,1)} %refs_16_.1) | copy-start | bytes 6291460
  149.8 7.2 %collective-permute-start.12 = (bf16[4,128,1024]{2,1,0:T(8,128)(2,1)S(1)}, bf16[4,128,1024]{2,1,0:T(8,128)(2,1)S(1)}, u32[]{:S(2)}, u32[]{:S(2)}) collective-permute-start(bf16[4,128,1024]{2,1,0:T(8,128)(2,1)S(1)} %bitcast.178), channel_id=1, source_target_pairs={{0,1},{1,0},{2,3},{3,2},{4,5},{5,4},{6,7},{7,6},{8,9},{9,8},{10,11... | collective-permute-start | bytes 3145736 | tf_op jit(solution)/shard_map/ppermute | solution.py:35
  150.0 30.2 %copy-start.6 = (bf16[4,32,1024]{2,1,0:T(8,128)(2,1)}, bf16[4,32,1024]{2,1,0:T(8,128)(2,1)S(1)}, u32[]{:S(2)}) copy-start(bf16[4,32,1024]{2,1,0:T(8,128)(2,1)S(1)} %get-tuple-element.33) | copy-start | bytes 786436
  150.8 12.9 %collective-permute-start.14 = (bf16[128,1024]{1,0:T(8,128)(2,1)S(1)}, bf16[128,1024]{1,0:T(8,128)(2,1)S(1)}, u32[]{:S(2)}, u32[]{:S(2)}) collective-permute-start(bf16[128,1024]{1,0:T(8,128)(2,1)S(1)} %convolution_convert_fusion.9), channel_id=1, source_target_pairs={{0,224},{1,161},{32,192},{33,129},{64,32},{65,225},{96,0},{97,193}... | collective-permute-start | bytes 786440 | tf_op jit(solution)/shard_map/ppermute | solution.py:55
  155.0 14.1 %collective-permute-start.13 = (bf16[128,1024]{1,0:T(8,128)(2,1)S(1)}, bf16[128,1024]{1,0:T(8,128)(2,1)S(1)}, u32[]{:S(2)}, u32[]{:S(2)}) collective-permute-start(bf16[128,1024]{1,0:T(8,128)(2,1)S(1)} %convolution_convert_fusion.10), channel_id=1, source_target_pairs={{0,128},{1,97},{32,160},{33,65},{64,192},{65,161},{96,224},{97,129... | collective-permute-start | bytes 786440 | tf_op jit(solution)/shard_map/ppermute | solution.py:55
  156.2 13.8 %collective-permute-start.15 = (bf16[128,1024]{1,0:T(8,128)(2,1)S(1)}, bf16[128,1024]{1,0:T(8,128)(2,1)S(1)}, u32[]{:S(2)}, u32[]{:S(2)}) collective-permute-start(bf16[128,1024]{1,0:T(8,128)(2,1)S(1)} %convolution_convert_fusion.8), channel_id=1, source_target_pairs={{0,32},{1,65},{32,0},{33,97},{64,96},{65,129},{96,64},{97,161},{12... | collective-permute-start | bytes 786440 | tf_op jit(solution)/shard_map/ppermute | solution.py:55
  157.8 22.3 %collective-permute-start.18 = (bf16[128,1024]{1,0:T(8,128)(2,1)S(1)}, bf16[128,1024]{1,0:T(8,128)(2,1)S(1)}, u32[]{:S(2)}, u32[]{:S(2)}) collective-permute-start(bf16[128,1024]{1,0:T(8,128)(2,1)S(1)} %convolution_convert_fusion.5), channel_id=1, source_target_pairs={{0,64},{1,33},{32,96},{33,1},{64,128},{65,97},{96,160},{97,65},{12... | collective-permute-start | bytes 786440 | tf_op jit(solution)/shard_map/ppermute | solution.py:55
  160.9 19.2 %copy-start.9 = (f32[128,1024]{1,0:T(8,128)S(1)}, f32[128,1024]{1,0:T(8,128)}, u32[]{:S(2)}) copy-start(f32[128,1024]{1,0:T(8,128)} %get-tuple-element.25) | copy-start | bytes 1572868
  161.0 19.2 %collective-permute-start.19 = (bf16[128,1024]{1,0:T(8,128)(2,1)S(1)}, bf16[128,1024]{1,0:T(8,128)(2,1)S(1)}, u32[]{:S(2)}, u32[]{:S(2)}) collective-permute-start(bf16[128,1024]{1,0:T(8,128)(2,1)S(1)} %convolution_convert_fusion.4), channel_id=1, source_target_pairs={{0,192},{1,193},{32,224},{33,225},{64,0},{65,1},{96,32},{97,33},{1... | collective-permute-start | bytes 786440 | tf_op jit(solution)/shard_map/ppermute | solution.py:55
  163.8 16.4 %collective-permute-start.16 = (bf16[128,1024]{1,0:T(8,128)(2,1)S(1)}, bf16[128,1024]{1,0:T(8,128)(2,1)S(1)}, u32[]{:S(2)}, u32[]{:S(2)}) collective-permute-start(bf16[128,1024]{1,0:T(8,128)(2,1)S(1)} %convolution_convert_fusion.7), channel_id=1, source_target_pairs={{0,96},{1,129},{32,64},{33,161},{64,160},{65,193},{96,128},{97,225... | collective-permute-start | bytes 786440 | tf_op jit(solution)/shard_map/ppermute | solution.py:55
  169.1 11.0 %collective-permute-start.17 = (bf16[128,1024]{1,0:T(8,128)(2,1)S(1)}, bf16[128,1024]{1,0:T(8,128)(2,1)S(1)}, u32[]{:S(2)}, u32[]{:S(2)}) collective-permute-start(bf16[128,1024]{1,0:T(8,128)(2,1)S(1)} %convolution_convert_fusion.6), channel_id=1, source_target_pairs={{0,160},{1,225},{32,128},{33,193},{64,224},{65,33},{96,192},{97,1}... | collective-permute-start | bytes 786440 | tf_op jit(solution)/shard_map/ppermute | solution.py:55
  182.8 32.4 %all-to-all-start.3 = ((bf16[8,128,1024]{2,1,0:T(8,128)(2,1)}), bf16[8,128,1024]{2,1,0:T(8,128)(2,1)}, u32[]{:S(2)}, u32[]{:S(2)}) async-start(bf16[8,128,1024]{2,1,0:T(8,128)(2,1)} %broadcast_in_dim.11), calls=%async_computation.3 | async-start | bytes 4194304 | tf_op jit(solution)/shard_map/all_to_all | solution.py:205
  (10 other events, 35.9 us)

commit v2 on v1

v2 whole, which is shorter than its diff:
```python
import math

import jax
import jax.numpy as jnp
from jax import lax
from jax.experimental import pallas as pl
from jax.sharding import Mesh
from jax.sharding import PartitionSpec as P

SHARPNESS = 8.0
PENALTY = 1.0
EPSILON = 1e-06

NAMES = ("y", "xl", "xh", "z", "core")
SHAPE = (4, 2, 2, 8, 2)
N_Y, N_XL, N_XH, N_Z, N_CORE = SHAPE
SRC = ("y", "xl")
LAT = ("xh", "z", "core")

bf16 = jnp.bfloat16
f32 = jnp.float32


def swap(value, axis, size, mask=1):
    return lax.ppermute(value, axis, [(i, i ^ mask) for i in range(size)])


def exchange(value, axis, size):
    return lax.all_to_all(value.reshape(size, value.shape[0] // size, -1), axis, 0, 0)


def spread(value, axis, size):
    copies = jnp.broadcast_to(value[None], (size,) + value.shape)
    return lax.all_to_all(copies, axis, 0, 0).reshape(size * value.shape[0], -1)


def add_up(parts):
    total = parts[0].astype(f32)
    for i in range(1, parts.shape[0]):
        total = total + parts[i].astype(f32)
    return total


def half_of(value, index):
    return lax.dynamic_index_in_dim(
        value.reshape(2, value.shape[0] // 2, -1), index, 0, False
    )


def in_order(index, own, other):
    first = index == 0
    return jnp.concatenate(
        [jnp.where(first, own, other), jnp.where(first, other, own)], axis=0
    )


def dot(a, b):
    return jnp.dot(a, b, preferred_element_type=f32)


def dot_t(a, b):
    return jnp.einsum("bk,jk->bj", a, b, preferred_element_type=f32)


def transpose(value):
    rows, cols = value.shape
    tile = 256

    def kernel(in_ref, out_ref):
        out_ref[...] = in_ref[...].T

    return pl.pallas_call(
        kernel,
        grid=(cols // tile,),
        in_specs=[pl.BlockSpec((rows, tile), lambda i: (0, i))],
        out_specs=pl.BlockSpec((tile, rows), lambda i: (i, 0)),
        out_shape=jax.ShapeDtypeStruct((cols, rows), value.dtype),
        name="transpose",
    )(value)


def decoder_grad(latents, errors, decoder, norms, loss_scale):
    n = len(latents)
    width, feat = decoder.shape
    tile = 256

    def kernel(*refs):
        lat, err = refs[:n], refs[n : 2 * n]
        dec_ref, norm_ref, out_ref = refs[2 * n :]
        outer = jnp.zeros((tile, feat), f32)
        sums = jnp.zeros((tile, 1), f32)
        for l_ref, e_ref in zip(lat, err):
            tall = l_ref[...].T
            outer += jnp.dot(tall, e_ref[...], preferred_element_type=f32)
            sums += jnp.sum(tall.astype(f32), axis=1, keepdims=True)
        shrink = loss_scale * PENALTY * sums / norm_ref[...].T[:, :1]
        out_ref[...] = (loss_scale * outer + shrink * dec_ref[...].astype(f32)).astype(bf16)

    return pl.pallas_call(
        kernel,
        grid=(width // tile,),
        in_specs=[pl.BlockSpec((v.shape[0], tile), lambda i: (0, i)) for v in latents]
        + [pl.BlockSpec((v.shape[0], feat), lambda i: (0, 0)) for v in errors]
        + [
            pl.BlockSpec((tile, feat), lambda i: (i, 0)),
            pl.BlockSpec((8, tile), lambda i: (0, i)),
        ],
        out_specs=pl.BlockSpec((tile, feat), lambda i: (i, 0)),
        out_shape=jax.ShapeDtypeStruct(decoder.shape, bf16),
        name="decoder_grad",
    )(*latents, *errors, decoder, norms)


def encoder_grad(res_t, grads):
    n = len(grads)
    feat, rows = res_t.shape
    width = grads[0].shape[1]
    tile = 256

    def kernel(res_ref, *refs):
        total = jnp.zeros((tile, width), f32)
        low = 0
        for g_ref in refs[:n]:
            high = low + g_ref.shape[0]
            total += jnp.dot(res_ref[:, low:high], g_ref[...], preferred_element_type=f32)
            low = high
        refs[n][...] = total.astype(bf16)

    return pl.pallas_call(
        kernel,
        grid=(feat // tile,),
        in_specs=[pl.BlockSpec((tile, rows), lambda i: (i, 0))]
        + [pl.BlockSpec(g.shape, lambda i: (0, 0)) for g in grads],
        out_specs=pl.BlockSpec((tile, width), lambda i: (i, 0)),
        out_shape=jax.ShapeDtypeStruct((feat, width), bf16),
        name="encoder_grad",
    )(res_t, *grads)


def scatter_src(a_part, b_send, b_keep, x):
    a_parts = exchange(a_part, "y", N_Y)
    b_sum = (b_keep + swap(b_send, "xl", N_XL).astype(f32)).astype(bf16)
    a_sum = add_up(a_parts)
    a_got = swap(half_of(a_sum, 1 - x).astype(bf16), "xl", N_XL)
    b_total = add_up(exchange(b_sum, "y", N_Y))
    a_total = half_of(a_sum, x) + a_got.astype(f32)
    return jnp.concatenate([a_total, b_total], axis=0)


def gather_src(shard, x):
    half = shard.shape[0] // 2
    a_own, b_own = shard[:half], shard[half:]
    pair = in_order(x, a_own, swap(a_own, "xl", N_XL))
    b_near = spread(b_own, "y", N_Y)
    pair, b_near = lax.optimization_barrier((pair, b_near))
    b_far = swap(b_near, "xl", N_XL)
    return spread(pair, "y", N_Y), b_near, b_far


def per_device(residual_rows, encoder, decoder, enc_bias, dec_bias):
    row_count = residual_rows.shape[0]
    loss_scale = 1.0 / math.sqrt(row_count)
    half = row_count // 2
    quarter = half // 2
    y, x, xh, z, core = (lax.axis_index(a) for a in NAMES)

    def rows_of(start, count):
        return lax.dynamic_slice_in_dim(residual_rows, start, count, 0)

    b_near_rows = half + x * quarter
    b_far_rows = half + (1 - x) * quarter

    a_part = dot(residual_rows[:half], encoder).astype(bf16)
    b_send = dot(rows_of(b_far_rows, quarter), encoder).astype(bf16)
    b_keep = dot(rows_of(b_near_rows, quarter), encoder)
    pre_act = scatter_src(a_part, b_send, b_keep, x)

    squares = jnp.sum(jnp.square(decoder.astype(f32)), axis=1)
    res_t = transpose(
        jnp.concatenate(
            [residual_rows[:half], rows_of(b_near_rows, quarter), rows_of(b_far_rows, quarter)],
            axis=0,
        )
    )
    enc_bias, squares, res_t = lax.optimization_barrier((enc_bias, squares, res_t))

    pre_act = pre_act + enc_bias[None, :]
    latent = (jax.nn.softplus(SHARPNESS * pre_act) / SHARPNESS).astype(bf16)
    slope = jax.nn.sigmoid(SHARPNESS * pre_act)
    lat_a, lat_near, lat_far = gather_src(latent, x)

    def core_sum(mine, theirs):
        theirs = swap(dot(theirs, decoder).astype(bf16), "core", N_CORE)
        return dot(mine, decoder) + theirs.astype(f32)

    same = core == x
    b_mine = jnp.where(same, lat_near, lat_far)
    b_theirs = jnp.where(same, lat_far, lat_near)
    b_sum = core_sum(b_mine, b_theirs)
    a_sum = core_sum(half_of(lat_a, core), half_of(lat_a, 1 - core)).astype(bf16)
    squares, a_sum = lax.optimization_barrier((squares, a_sum))

    a_sum = add_up(exchange(a_sum, "z", N_Z))
    b_got = swap(half_of(b_sum, 1 - xh).astype(bf16), "xh", N_XH)
    b_sum = (half_of(b_sum, xh) + b_got.astype(f32)).astype(bf16)
    a_got = swap(half_of(a_sum, 1 - xh).astype(bf16), "xh", N_XH)
    b_sum = add_up(exchange(b_sum, "z", N_Z))
    a_sum = half_of(a_sum, xh) + a_got.astype(f32)

    own_sq = squares + swap(squares, "xl", N_XL)
    own_sq = own_sq + swap(own_sq, "y", N_Y)
    other_sq = swap(own_sq, "y", N_Y, 2)
    own_norm = jnp.sqrt(own_sq + EPSILON)
    penalty = PENALTY * (own_norm + jnp.sqrt(other_sq + EPSILON))
    dec_bias, own_norm, penalty = lax.optimization_barrier((dec_bias, own_norm, penalty))

    share = quarter // (N_XH * N_Z)
    a_target = rows_of(core * quarter + (z * N_XH + xh) * share, share)
    b_target = rows_of(half + core * quarter + (xh * N_Z + z) * share, share)
    a_err = (a_sum + dec_bias[None, :] - a_target.astype(f32)).astype(bf16)
    b_err = (b_sum + dec_bias[None, :] - b_target.astype(f32)).astype(bf16)

    a_pair = in_order(xh, a_err, swap(a_err, "xh", N_XH))
    b_err = spread(b_err, "z", N_Z)
    a_pair, b_err = lax.optimization_barrier((a_pair, b_err))
    b_mine = in_order(xh, b_err, swap(b_err, "xh", N_XH))
    a_mine = spread(a_pair, "z", N_Z)
    b_theirs = swap(b_mine, "core", N_CORE)
    err_near = jnp.where(same, b_mine, b_theirs)
    err_far = jnp.where(same, b_theirs, b_mine)
    err_a = in_order(core, a_mine, swap(a_mine, "core", N_CORE))

    b_send = dot_t(err_far, decoder).astype(bf16)
    b_keep = dot_t(err_near, decoder)
    a_part = dot_t(err_a, decoder).astype(bf16)
    act_grad = scatter_src(a_part, b_send, b_keep, x) + penalty[None, :]
    grad_pre = (loss_scale * act_grad * slope).astype(bf16)
    grads = gather_src(grad_pre, x)

    grad_decoder = decoder_grad(
        [lat_a, lat_near, lat_far],
        [err_a, err_near, err_far],
        decoder,
        jnp.stack([own_norm] * 8),
        loss_scale,
    )
    return (encoder_grad(res_t, grads), grad_decoder)


def solution(mesh):
    fine = Mesh(mesh.devices.reshape(SHAPE), NAMES)
    in_specs = (P(None, SRC), P(SRC, LAT), P(LAT, SRC), P(LAT), P(SRC))
    out_specs = (P(SRC, LAT), P(LAT, SRC))
    return jax.shard_map(
        per_device, mesh=fine, in_specs=in_specs, out_specs=out_specs, check_vma=False
    )
```

time: 223 us -> 257 us (1.15); the launches traced: 221 us -> 253 us
  blocking collectives: 32.7 us -> 0 us
  starting transfers between devices: 49.7 us -> 77.5 us
  other arithmetic: 8.18 us -> 20.1 us
  local copies, waits for them, and re-layouts: 5.78 us -> 15.9 us
  waiting for transfers between devices: 87.4 us -> 96.8 us
  Pallas kernels: 12.8 us -> 17 us
    all_to_all x3 -> x12, starting transfers between devices: 20.5 us -> 58.6 us  [the longest x6 32 us: exchange(): lax.all_to_all(value.reshape(size, value.shape[0] // size, -1), axis, 0, 0)]
    all_to_all x1 -> x0, blocking collectives: 32.7 us -> none  [per_device(): mine = lax.all_to_all(errors, RING, 0, 0).reshape(4, block, -1)]
    ppermute x14 -> x0, waiting for transfers between devices: 28 us -> none  [move(): return lax.ppermute(value, ('y', 'xl', 'core'), pairs)]
    ppermute x6 -> x19, waiting for transfers between devices: 8.03 us -> 32.5 us  [swap(): return lax.ppermute(value, axis, [(i, i ^ mask) for i in range(size)])]
    ppermute x14 -> x0, starting transfers between devices: 22.9 us -> none  [move(): return lax.ppermute(value, ('y', 'xl', 'core'), pairs)]
    all_to_all x3 -> x12, waiting for transfers between devices: 51.3 us -> 64.3 us  [the longest x6 40.3 us: spread(): return lax.all_to_all(copies, axis, 0, 0).reshape(size * value.shape[0], -1)]
    ppermute x6 -> x19, starting transfers between devices: 6.28 us -> 18.9 us  [swap(): return lax.ppermute(value, axis, [(i, i ^ mask) for i in range(size)])]
    add x1 -> x8, other arithmetic: 0.01 us -> 5.73 us  [the longest x5 3.77 us: add_up(): total = total + parts[i].astype(f32)]
  transfers between devices with their start and end apart: 23 -> 31, of which waited for: 12 -> 18; matrix products, arithmetic and copies ran while one was open for 7% -> 17% of each run, Pallas kernels for 6% -> 4%
where the time goes in v2:
time: 257 us; the launch traced here: 253 us
  waiting for transfers between devices  96.8 us (38%)
  starting transfers between devices  77.5 us (30%)
  matrix products  24.1 us (9%)
  other arithmetic  20.1 us (8%)
  Pallas kernels  17 us (7%)
  local copies, waits for them, and re-layouts  15.9 us (6%)
    all_to_all x6, waiting for transfers between devices, spread(): return lax.all_to_all(copies, axis, 0, 0).reshape(size * value.shape[0], -1)  40.3 us
    ppermute x19, waiting for transfers between devices, swap(): return lax.ppermute(value, axis, [(i, i ^ mask) for i in range(size)])  32.5 us
    all_to_all x6, starting transfers between devices, exchange(): lax.all_to_all(value.reshape(size, value.shape[0] // size, -1), axis, 0, 0)  32 us
    all_to_all x6, starting transfers between devices, spread(): return lax.all_to_all(copies, axis, 0, 0).reshape(size * value.shape[0], -1)  26.6 us
    all_to_all x6, waiting for transfers between devices, exchange(): lax.all_to_all(value.reshape(size, value.shape[0] // size, -1), axis, 0, 0)  24 us
    ppermute x19, starting transfers between devices, swap(): return lax.ppermute(value, axis, [(i, i ^ mask) for i in range(size)])  18.9 us
    dot_general x7, matrix products, dot(): return jnp.dot(a, b, preferred_element_type=f32)  16.9 us
    dot_general x3, matrix products, dot_t(): return jnp.einsum('bk,jk->bj', a, b, preferred_element_type=f32)  7.18 us
  transfers between devices with their start and end apart: 31, of which 18 were waited for; matrix products, arithmetic and copies ran while one was open for 17% of the time, Pallas kernels for 4%

profile of v2, /device:TPU:32, one launch (start us, length us, event | category | flops | bytes accessed | tf_op | source)
XLA Modules:
  0.0 252.5 jit_solution(11746643346252201094)
XLA Ops:
  8.9 4.5 %all-to-all-start = ((bf16[4,128,1024]{2,1,0:T(8,128)(2,1)}), bf16[4,128,1024]{2,1,0:T(8,128)(2,1)S(1)}, u32[]{:S(2)}, u32[]{:S(2)}) async-start(bf16[4,128,1024]{2,1,0:T(8,128)(2,1)} %bitcast.88), calls=%async_computation | async-start | bytes 2097152 | tf_op jit(solution)/shard_map/all_to_all | solution.py:29
  21.7 6.5 %all-to-all-done = bf16[4,128,1024]{2,1,0:T(8,128)(2,1)S(1)} async-done(((bf16[4,128,1024]{2,1,0:T(8,128)(2,1)}), bf16[4,128,1024]{2,1,0:T(8,128)(2,1)S(1)}, u32[]{:S(2)}, u32[]{:S(2)}) %all-to-all-start) | async-done | bytes 1048608 | tf_op jit(solution)/shard_map/all_to_all | solution.py:29
  28.2 4.1 %all-to-all-start.1 = ((bf16[4,64,1024]{2,1,0:T(8,128)(2,1)}), bf16[4,64,1024]{2,1,0:T(8,128)(2,1)}, u32[]{:S(2)}, u32[]{:S(2)}) async-start(bf16[4,64,1024]{2,1,0:T(8,128)(2,1)} %bitcast.93), calls=%async_computation.1 | async-start | bytes 1048576 | tf_op jit(solution)/shard_map/all_to_all | solution.py:29
  35.4 4.1 %transpose.10.res_ref = bf16[1024,1024]{1,0:T(8,128)(2,1)} custom-call(bf16[1024,1024]{1,0:T(8,128)(2,1)} %pad_maximum_fusion.in_ref), custom_call_target="tpu_custom_call" | custom-call | tf_op jit(solution)/shard_map/transpose/pallas_call | solution.py:72
  42.3 3.3 %collective-permute-done = bf16[64,1024]{1,0:T(8,128)(2,1)S(1)} collective-permute-done((bf16[64,1024]{1,0:T(8,128)(2,1)S(1)}, bf16[64,1024]{1,0:T(8,128)(2,1)S(1)}, u32[]{:S(2)}, u32[]{:S(2)}) %collective-permute-start) | collective-permute-done | bytes 131104 | tf_op jit(solution)/shard_map/ppermute | solution.py:25
  48.2 4.4 %collective-permute-done.2 = bf16[64,1024]{1,0:T(8,128)(2,1)S(1)} collective-permute-done((bf16[64,1024]{1,0:T(8,128)(2,1)S(1)}, bf16[64,1024]{1,0:T(8,128)(2,1)S(1)}, u32[]{:S(2)}, u32[]{:S(2)}) %collective-permute-start.2) | collective-permute-done | bytes 131104 | tf_op jit(solution)/shard_map/ppermute | solution.py:25
  53.5 4.7 %all-to-all-start.2 = ((bf16[4,64,1024]{2,1,0:T(8,128)(2,1)}), bf16[4,64,1024]{2,1,0:T(8,128)(2,1)S(1)}, u32[]{:S(2)}, u32[]{:S(2)}) async-start(bf16[4,64,1024]{2,1,0:T(8,128)(2,1)} %broadcast_in_dim.12), calls=%async_computation.2 | async-start | bytes 1048576 | tf_op jit(solution)/shard_map/all_to_all | solution.py:34
  58.3 8.1 %all-to-all-done.2 = bf16[4,64,1024]{2,1,0:T(8,128)(2,1)S(1)} async-done(((bf16[4,64,1024]{2,1,0:T(8,128)(2,1)}), bf16[4,64,1024]{2,1,0:T(8,128)(2,1)S(1)}, u32[]{:S(2)}, u32[]{:S(2)}) %all-to-all-start.2) | async-done | bytes 524320 | tf_op jit(solution)/shard_map/all_to_all | solution.py:34
  67.5 4.2 %all-to-all-start.3 = ((bf16[4,128,1024]{2,1,0:T(8,128)(2,1)}), bf16[4,128,1024]{2,1,0:T(8,128)(2,1)}, u32[]{:S(2)}, u32[]{:S(2)}) async-start(bf16[4,128,1024]{2,1,0:T(8,128)(2,1)} %broadcast_in_dim.13), calls=%async_computation.3 | async-start | bytes 2097152 | tf_op jit(solution)/shard_map/all_to_all | solution.py:34
  72.4 10.3 %all-to-all-done.3 = bf16[4,128,1024]{2,1,0:T(8,128)(2,1)} async-done(((bf16[4,128,1024]{2,1,0:T(8,128)(2,1)}), bf16[4,128,1024]{2,1,0:T(8,128)(2,1)}, u32[]{:S(2)}, u32[]{:S(2)}) %all-to-all-start.3) | async-done | bytes 1048608 | tf_op jit(solution)/shard_map/all_to_all | solution.py:34
  82.7 3.4 %convolution_convert_fusion.4 = bf16[256,1024]{1,0:T(8,128)(2,1)} fusion(bf16[1024,1024]{1,0:T(8,128)(2,1)} %refs_6_.1, bf16[2,256,1024]{2,1,0:T(8,128)(2,1)} %bitcast.7, s32[]{:T(128)S(6)} %select_n.129), kind=kOutput, calls=%fused_computation.9 | convolution fusion | flops 537133056 | bytes 3145732 | tf_op jit(solution)/shard_map/dot_general | solution.py:58
  88.4 3.3 %add_convert_fusion = bf16[256,1024]{1,0:T(8,128)(2,1)} fusion(bf16[256,1024]{1,0:T(8,128)(2,1)} %collective-permute-done.3, bf16[1024,1024]{1,0:T(8,128)(2,1)} %refs_6_.1, bf16[2,256,1024]{2,1,0:T(8,128)(2,1)} %bitcast.7, s32[]{:T(128)S(6)} %select_n.128), kind=kOutput, calls=%fused_computation.13 | convolution fusion | flops 537657344 | bytes 3670020 | tf_op jit(solution)/shard_map/dot_general | solution.py:58
  91.7 8.6 %all-to-all-start.4 = ((bf16[8,32,1024]{2,1,0:T(8,128)(2,1)}), bf16[8,32,1024]{2,1,0:T(8,128)(2,1)}, u32[]{:S(2)}, u32[]{:S(2)}) async-start(bf16[8,32,1024]{2,1,0:T(8,128)(2,1)} %bitcast.92), calls=%async_computation.4 | async-start | bytes 1048576 | tf_op jit(solution)/shard_map/all_to_all | solution.py:29
  106.7 5.8 %collective-permute-done.5 = f32[1024]{0:T(1024)S(1)} collective-permute-done((f32[1024]{0:T(1024)S(1)}, f32[1024]{0:T(1024)S(1)}, u32[]{:S(2)}, u32[]{:S(2)}) %collective-permute-start.5) | collective-permute-done | bytes 4128 | tf_op jit(solution)/shard_map/ppermute | solution.py:25
  117.1 7.2 %all-to-all-start.5 = ((bf16[8,16,1024]{2,1,0:T(8,128)(2,1)}), bf16[8,16,1024]{2,1,0:T(8,128)(2,1)S(1)}, u32[]{:S(2)}, u32[]{:S(2)}) async-start(bf16[8,16,1024]{2,1,0:T(8,128)(2,1)} %bitcast.17), calls=%async_computation.5 | async-start | bytes 524288 | tf_op jit(solution)/shard_map/all_to_all | solution.py:29
  127.3 6.1 %all-to-all-done.5 = bf16[8,16,1024]{2,1,0:T(8,128)(2,1)S(1)} async-done(((bf16[8,16,1024]{2,1,0:T(8,128)(2,1)}), bf16[8,16,1024]{2,1,0:T(8,128)(2,1)S(1)}, u32[]{:S(2)}, u32[]{:S(2)}) %all-to-all-start.5) | async-done | bytes 262176 | tf_op jit(solution)/shard_map/all_to_all | solution.py:29
  134.9 4.8 %all-to-all-start.6 = ((bf16[8,16,1024]{2,1,0:T(8,128)(2,1)}), bf16[8,16,1024]{2,1,0:T(8,128)(2,1)S(1)}, u32[]{:S(2)}, u32[]{:S(2)}) async-start(bf16[8,16,1024]{2,1,0:T(8,128)(2,1)} %broadcast_in_dim.14), calls=%async_computation.6 | async-start | bytes 524288 | tf_op jit(solution)/shard_map/all_to_all | solution.py:34
  141.5 3.7 %collective-permute-done.8 = bf16[16,1024]{1,0:T(8,128)(2,1)S(1)} collective-permute-done((bf16[16,1024]{1,0:T(8,128)(2,1)S(1)}, bf16[16,1024]{1,0:T(8,128)(2,1)S(1)}, u32[]{:S(2)}, u32[]{:S(2)}) %collective-permute-start.8) | collective-permute-done | bytes 32800 | tf_op jit(solution)/shard_map/ppermute | solution.py:25
  151.1 5.7 %all-to-all-start.7 = ((bf16[8,32,1024]{2,1,0:T(8,128)(2,1)}), bf16[8,32,1024]{2,1,0:T(8,128)(2,1)}, u32[]{:S(2)}, u32[]{:S(2)}) async-start(bf16[8,32,1024]{2,1,0:T(8,128)(2,1)} %broadcast_in_dim.15), calls=%async_computation.7 | async-start | bytes 1048576 | tf_op jit(solution)/shard_map/all_to_all | solution.py:34
  158.0 10.7 %all-to-all-done.7 = bf16[8,32,1024]{2,1,0:T(8,128)(2,1)} async-done(((bf16[8,32,1024]{2,1,0:T(8,128)(2,1)}), bf16[8,32,1024]{2,1,0:T(8,128)(2,1)}, u32[]{:S(2)}, u32[]{:S(2)}) %all-to-all-start.7) | async-done | bytes 524320 | tf_op jit(solution)/shard_map/all_to_all | solution.py:34
  176.1 3.5 %all-to-all-start.8 = ((bf16[4,128,1024]{2,1,0:T(8,128)(2,1)}), bf16[4,128,1024]{2,1,0:T(8,128)(2,1)S(1)}, u32[]{:S(2)}, u32[]{:S(2)}) async-start(bf16[4,128,1024]{2,1,0:T(8,128)(2,1)} %bitcast.89), calls=%async_computation.8 | async-start | bytes 2097152 | tf_op jit(solution)/shard_map/all_to_all | solution.py:29
  179.6 7.4 %collective-permute-done.16 = bf16[256,1024]{1,0:T(8,128)(2,1)} collective-permute-done((bf16[256,1024]{1,0:T(8,128)(2,1)}, bf16[256,1024]{1,0:T(8,128)(2,1)}, u32[]{:S(2)}, u32[]{:S(2)}) %collective-permute-start.16) | collective-permute-done | bytes 524320 | tf_op jit(solution)/shard_map/ppermute | solution.py:25
  187.0 3.4 %fusion = bf16[256,1024]{1,0:T(8,128)(2,1)} fusion(bf16[256,1024]{1,0:T(8,128)(2,1)} %get-tuple-element.39.refs_4_, bf16[1024,1024]{1,0:T(8,128)(2,1)} %refs_6_.1, bf16[256,1024]{1,0:T(8,128)(2,1)} %collective-permute-done.16), kind=kOutput, calls=%fused_computation.11 | convolution fusion | flops 537657344 | bytes 3670016 | tf_op jit(solution)/shard_map/bk,jk->bj/dot_general | solution.py:62
  190.3 4.9 %all-to-all-done.8 = bf16[4,128,1024]{2,1,0:T(8,128)(2,1)S(1)} async-done(((bf16[4,128,1024]{2,1,0:T(8,128)(2,1)}), bf16[4,128,1024]{2,1,0:T(8,128)(2,1)S(1)}, u32[]{:S(2)}, u32[]{:S(2)}) %all-to-all-start.8) | async-done | bytes 1048608 | tf_op jit(solution)/shard_map/all_to_all | solution.py:29
  195.3 4.1 %all-to-all-start.9 = ((bf16[4,64,1024]{2,1,0:T(8,128)(2,1)}), bf16[4,64,1024]{2,1,0:T(8,128)(2,1)}, u32[]{:S(2)}, u32[]{:S(2)}) async-start(bf16[4,64,1024]{2,1,0:T(8,128)(2,1)} %bitcast.94), calls=%async_computation.9 | async-start | bytes 1048576 | tf_op jit(solution)/shard_map/all_to_all | solution.py:29
  202.2 6.5 %all-to-all-done.9 = bf16[4,64,1024]{2,1,0:T(8,128)(2,1)} async-done(((bf16[4,64,1024]{2,1,0:T(8,128)(2,1)}), bf16[4,64,1024]{2,1,0:T(8,128)(2,1)}, u32[]{:S(2)}, u32[]{:S(2)}) %all-to-all-start.9) | async-done | bytes 524320 | tf_op jit(solution)/shard_map/all_to_all | solution.py:29
  213.6 3.5 %collective-permute-done.17 = bf16[64,1024]{1,0:T(8,128)(2,1)S(1)} collective-permute-done((bf16[64,1024]{1,0:T(8,128)(2,1)S(1)}, bf16[64,1024]{1,0:T(8,128)(2,1)S(1)}, u32[]{:S(2)}, u32[]{:S(2)}) %collective-permute-start.17) | collective-permute-done | bytes 131104 | tf_op jit(solution)/shard_map/ppermute | solution.py:25
  218.0 3.5 %all-to-all-start.10 = ((bf16[4,64,1024]{2,1,0:T(8,128)(2,1)}), bf16[4,64,1024]{2,1,0:T(8,128)(2,1)S(1)}, u32[]{:S(2)}, u32[]{:S(2)}) async-start(bf16[4,64,1024]{2,1,0:T(8,128)(2,1)} %broadcast_in_dim.16), calls=%async_computation.10 | async-start | bytes 1048576 | tf_op jit(solution)/shard_map/all_to_all | solution.py:34
  221.5 8.0 %all-to-all-done.10 = bf16[4,64,1024]{2,1,0:T(8,128)(2,1)S(1)} async-done(((bf16[4,64,1024]{2,1,0:T(8,128)(2,1)}), bf16[4,64,1024]{2,1,0:T(8,128)(2,1)S(1)}, u32[]{:S(2)}, u32[]{:S(2)}) %all-to-all-start.10) | async-done | bytes 524320 | tf_op jit(solution)/shard_map/all_to_all | solution.py:34
  230.7 3.5 %all-to-all-start.11 = ((bf16[4,128,1024]{2,1,0:T(8,128)(2,1)}), bf16[4,128,1024]{2,1,0:T(8,128)(2,1)S(1)}, u32[]{:S(2)}, u32[]{:S(2)}) async-start(bf16[4,128,1024]{2,1,0:T(8,128)(2,1)} %broadcast_in_dim.17), calls=%async_computation.11 | async-start | bytes 2097152 | tf_op jit(solution)/shard_map/all_to_all | solution.py:34
  238.6 7.0 %decoder_grad.1 = bf16[1024,1024]{1,0:T(8,128)(2,1)} custom-call(bf16[512,1024]{1,0:T(8,128)(2,1)} %bitcast.29.refs_0_, bf16[256,1024]{1,0:T(8,128)(2,1)} %bitcast.78, bf16[256,1024]{1,0:T(8,128)(2,1)} %copy-done.9, bf16[512,1024]{1,0:T(8,128)(2,1)} %pad_maximum_fusion.1.refs_3_, bf16[256,1024]{1,0:T(8,128)(2,1)} %get-tuple-element.39.refs_4_, ...), custom_call_target="tpu_custom_call" | custom-call | tf_op jit(solution)/shard_map/decoder_grad/pallas_call | solution.py:99
  246.6 5.9 %encoder_grad.1 = bf16[1024,1024]{1,0:T(8,128)(2,1)} custom-call(bf16[1024,1024]{1,0:T(8,128)(2,1)} %transpose.10.res_ref, bf16[512,1024]{1,0:T(8,128)(2,1)} %bitcast.79, bf16[256,1024]{1,0:T(8,128)(2,1)} %bitcast.83, bf16[256,1024]{1,0:T(8,128)(2,1)} %collective-permute-done.18.refs_2_), custom_call_target="tpu_custom_call" | custom-call | tf_op jit(solution)/shard_map/encoder_grad/pallas_call | solution.py:129
  (125 shorter events, 76.6 us)
Async XLA Ops:
  5.2 14.0 %collective-permute-start.1 = (bf16[256,1024]{1,0:T(8,128)(2,1)}, bf16[256,1024]{1,0:T(8,128)(2,1)}, u32[]{:S(2)}, u32[]{:S(2)}) collective-permute-start(bf16[256,1024]{1,0:T(8,128)(2,1)} %convolution_convert_fusion.5), channel_id=1, source_target_pairs={{0,32},{32,0},{1,33},{33,1},{2,34},{34,2},{3,35},{35,3},{4,36},{36... | collective-permute-start | bytes 1572872 | tf_op jit(solution)/shard_map/ppermute | solution.py:25
  8.9 19.3 %all-to-all-start = ((bf16[4,128,1024]{2,1,0:T(8,128)(2,1)}), bf16[4,128,1024]{2,1,0:T(8,128)(2,1)S(1)}, u32[]{:S(2)}, u32[]{:S(2)}) async-start(bf16[4,128,1024]{2,1,0:T(8,128)(2,1)} %bitcast.88), calls=%async_computation | async-start | bytes 2097152 | tf_op jit(solution)/shard_map/all_to_all | solution.py:29
  28.2 12.9 %all-to-all-start.1 = ((bf16[4,64,1024]{2,1,0:T(8,128)(2,1)}), bf16[4,64,1024]{2,1,0:T(8,128)(2,1)}, u32[]{:S(2)}, u32[]{:S(2)}) async-start(bf16[4,64,1024]{2,1,0:T(8,128)(2,1)} %bitcast.93), calls=%async_computation.1 | async-start | bytes 1048576 | tf_op jit(solution)/shard_map/all_to_all | solution.py:29
  40.5 5.1 %collective-permute-start = (bf16[64,1024]{1,0:T(8,128)(2,1)S(1)}, bf16[64,1024]{1,0:T(8,128)(2,1)S(1)}, u32[]{:S(2)}, u32[]{:S(2)}) collective-permute-start(bf16[64,1024]{1,0:T(8,128)(2,1)S(1)} %fusion.20), channel_id=1, source_target_pairs={{0,32},{32,0},{1,33},{33,1},{2,34},{34,2},{3,35},{35,3},{4,36},{36... | collective-permute-start | bytes 393224 | tf_op jit(solution)/shard_map/ppermute | solution.py:25
  47.6 5.1 %collective-permute-start.2 = (bf16[64,1024]{1,0:T(8,128)(2,1)S(1)}, bf16[64,1024]{1,0:T(8,128)(2,1)S(1)}, u32[]{:S(2)}, u32[]{:S(2)}) collective-permute-start(bf16[64,1024]{1,0:T(8,128)(2,1)S(1)} %slice.157), channel_id=1, source_target_pairs={{0,32},{32,0},{1,33},{33,1},{2,34},{34,2},{3,35},{35,3},{4,36},{36... | collective-permute-start | bytes 393224 | tf_op jit(solution)/shard_map/ppermute | solution.py:25
  53.5 12.8 %all-to-all-start.2 = ((bf16[4,64,1024]{2,1,0:T(8,128)(2,1)}), bf16[4,64,1024]{2,1,0:T(8,128)(2,1)S(1)}, u32[]{:S(2)}, u32[]{:S(2)}) async-start(bf16[4,64,1024]{2,1,0:T(8,128)(2,1)} %broadcast_in_dim.12), calls=%async_computation.2 | async-start | bytes 1048576 | tf_op jit(solution)/shard_map/all_to_all | solution.py:34
  66.4 33.9 %copy-start.4 = (bf16[4,64,1024]{2,1,0:T(8,128)(2,1)}, bf16[4,64,1024]{2,1,0:T(8,128)(2,1)S(1)}, u32[]{:S(2)}) copy-start(bf16[4,64,1024]{2,1,0:T(8,128)(2,1)S(1)} %all-to-all-done.2) | copy-start | bytes 1572868
  67.5 15.2 %all-to-all-start.3 = ((bf16[4,128,1024]{2,1,0:T(8,128)(2,1)}), bf16[4,128,1024]{2,1,0:T(8,128)(2,1)}, u32[]{:S(2)}, u32[]{:S(2)}) async-start(bf16[4,128,1024]{2,1,0:T(8,128)(2,1)} %broadcast_in_dim.13), calls=%async_computation.3 | async-start | bytes 2097152 | tf_op jit(solution)/shard_map/all_to_all | solution.py:34
  71.7 14.4 %collective-permute-start.9 = (bf16[256,1024]{1,0:T(8,128)(2,1)S(1)}, bf16[256,1024]{1,0:T(8,128)(2,1)S(1)}, u32[]{:S(2)}, u32[]{:S(2)}) collective-permute-start(bf16[256,1024]{1,0:T(8,128)(2,1)S(1)} %bitcast.75), channel_id=1, source_target_pairs={{0,32},{32,0},{1,33},{33,1},{2,34},{34,2},{3,35},{35,3},{4,36},{36... | collective-permute-start | bytes 1572872 | tf_op jit(solution)/shard_map/ppermute | solution.py:25
  86.1 2.3 collective-permute-start.3
  87.6 12.6 %collective-permute-start.10 = (bf16[256,1024]{1,0:T(8,128)(2,1)}, bf16[256,1024]{1,0:T(8,128)(2,1)}, u32[]{:S(2)}, u32[]{:S(2)}) collective-permute-start(bf16[256,1024]{1,0:T(8,128)(2,1)} %convolution_convert_fusion.3), channel_id=1, source_target_pairs={{0,1},{1,0},{2,3},{3,2},{4,5},{5,4},{6,7},{7,6},{8,9},{9,8},{10,11... | collective-permute-start | bytes 1572872 | tf_op jit(solution)/shard_map/ppermute | solution.py:25
  91.7 25.4 %all-to-all-start.4 = ((bf16[8,32,1024]{2,1,0:T(8,128)(2,1)}), bf16[8,32,1024]{2,1,0:T(8,128)(2,1)}, u32[]{:S(2)}, u32[]{:S(2)}) async-start(bf16[8,32,1024]{2,1,0:T(8,128)(2,1)} %bitcast.92), calls=%async_computation.4 | async-start | bytes 1048576 | tf_op jit(solution)/shard_map/all_to_all | solution.py:29
  103.7 9.5 %collective-permute-start.11 = (bf16[128,1024]{1,0:T(8,128)(2,1)S(1)}, bf16[128,1024]{1,0:T(8,128)(2,1)S(1)}, u32[]{:S(2)}, u32[]{:S(2)}) collective-permute-start(bf16[128,1024]{1,0:T(8,128)(2,1)S(1)} %fusion.19), channel_id=1, source_target_pairs={{0,16},{16,0},{1,17},{17,1},{2,18},{18,2},{3,19},{19,3},{4,20},{20... | collective-permute-start | bytes 786440 | tf_op jit(solution)/shard_map/ppermute | solution.py:25
  106.5 6.1 %collective-permute-start.5 = (f32[1024]{0:T(1024)S(1)}, f32[1024]{0:T(1024)S(1)}, u32[]{:S(2)}, u32[]{:S(2)}) collective-permute-start(f32[1024]{0:T(1024)S(1)} %multiply_reduce_fusion), channel_id=1, source_target_pairs={{0,32},{32,0},{1,33},{33,1},{2,34},{34,2},{3,35},{35,3},{4,36},{36... | collective-permute-start | bytes 12296 | tf_op jit(solution)/shard_map/ppermute | solution.py:25
  112.6 3.6 %collective-permute-start.6 = (f32[1024]{0:T(1024)S(1)}, f32[1024]{0:T(1024)S(1)}, u32[]{:S(2)}, u32[]{:S(2)}) collective-permute-start(f32[1024]{0:T(1024)S(1)} %add.298), channel_id=1, source_target_pairs={{0,64},{64,0},{128,192},{192,128},{1,65},{65,1},{129,193},{193,129... | collective-permute-start | bytes 12296 | tf_op jit(solution)/shard_map/ppermute | solution.py:25
  116.2 11.1 %collective-permute-start.7 = (f32[1024]{0:T(1024)S(1)}, f32[1024]{0:T(1024)S(1)}, u32[]{:S(2)}, u32[]{:S(2)}) collective-permute-start(f32[1024]{0:T(1024)S(1)} %get-tuple-element.31), channel_id=1, source_target_pairs={{0,128},{64,192},{128,0},{192,64},{1,129},{65,193},{129,1},{193,65... | collective-permute-start | bytes 12296 | tf_op jit(solution)/shard_map/ppermute | solution.py:25
  117.1 16.2 %all-to-all-start.5 = ((bf16[8,16,1024]{2,1,0:T(8,128)(2,1)}), bf16[8,16,1024]{2,1,0:T(8,128)(2,1)S(1)}, u32[]{:S(2)}, u32[]{:S(2)}) async-start(bf16[8,16,1024]{2,1,0:T(8,128)(2,1)} %bitcast.17), calls=%async_computation.5 | async-start | bytes 524288 | tf_op jit(solution)/shard_map/all_to_all | solution.py:29
  125.5 7.9 %collective-permute-start.4 = (bf16[16,1024]{1,0:T(8,128)(2,1)S(1)}, bf16[16,1024]{1,0:T(8,128)(2,1)S(1)}, u32[]{:S(2)}, u32[]{:S(2)}) collective-permute-start(bf16[16,1024]{1,0:T(8,128)(2,1)S(1)} %fusion.27), channel_id=1, source_target_pairs={{0,16},{16,0},{1,17},{17,1},{2,18},{18,2},{3,19},{19,3},{4,20},{20... | collective-permute-start | bytes 98312 | tf_op jit(solution)/shard_map/ppermute | solution.py:25
  134.9 13.5 %all-to-all-start.6 = ((bf16[8,16,1024]{2,1,0:T(8,128)(2,1)}), bf16[8,16,1024]{2,1,0:T(8,128)(2,1)S(1)}, u32[]{:S(2)}, u32[]{:S(2)}) async-start(bf16[8,16,1024]{2,1,0:T(8,128)(2,1)} %broadcast_in_dim.14), calls=%async_computation.6 | async-start | bytes 524288 | tf_op jit(solution)/shard_map/all_to_all | solution.py:34
  139.8 5.4 %collective-permute-start.8 = (bf16[16,1024]{1,0:T(8,128)(2,1)S(1)}, bf16[16,1024]{1,0:T(8,128)(2,1)S(1)}, u32[]{:S(2)}, u32[]{:S(2)}) collective-permute-start(bf16[16,1024]{1,0:T(8,128)(2,1)S(1)} %get-tuple-element.33), channel_id=1, source_target_pairs={{0,16},{16,0},{1,17},{17,1},{2,18},{18,2},{3,19},{19,3},{4,20},{20... | collective-permute-start | bytes 98312 | tf_op jit(solution)/shard_map/ppermute | solution.py:25
  148.5 8.4 %collective-permute-start.14 = (bf16[128,1024]{1,0:T(8,128)(2,1)S(1)}, bf16[128,1024]{1,0:T(8,128)(2,1)}, u32[]{:S(2)}, u32[]{:S(2)}) collective-permute-start(bf16[128,1024]{1,0:T(8,128)(2,1)S(1)} %bitcast.90), channel_id=1, source_target_pairs={{0,16},{16,0},{1,17},{17,1},{2,18},{18,2},{3,19},{19,3},{4,20},{20... | collective-permute-start | bytes 786440 | tf_op jit(solution)/shard_map/ppermute | solution.py:25
  151.1 17.5 %all-to-all-start.7 = ((bf16[8,32,1024]{2,1,0:T(8,128)(2,1)}), bf16[8,32,1024]{2,1,0:T(8,128)(2,1)}, u32[]{:S(2)}, u32[]{:S(2)}) async-start(bf16[8,32,1024]{2,1,0:T(8,128)(2,1)} %broadcast_in_dim.15), calls=%async_computation.7 | async-start | bytes 1048576 | tf_op jit(solution)/shard_map/all_to_all | solution.py:34
  157.9 10.8 %collective-permute-start.15 = (bf16[256,1024]{1,0:T(8,128)(2,1)S(1)}, bf16[256,1024]{1,0:T(8,128)(2,1)}, u32[]{:S(2)}, u32[]{:S(2)}) collective-permute-start(bf16[256,1024]{1,0:T(8,128)(2,1)S(1)} %pad_maximum_fusion.2), channel_id=1, source_target_pairs={{0,1},{1,0},{2,3},{3,2},{4,5},{5,4},{6,7},{7,6},{8,9},{9,8},{10,11... | collective-permute-start | bytes 1572872 | tf_op jit(solution)/shard_map/ppermute | solution.py:25
  168.7 4.0 %collective-permute-start.12 = (bf16[256,1024]{1,0:T(8,128)(2,1)}, bf16[256,1024]{1,0:T(8,128)(2,1)S(1)}, u32[]{:S(2)}, u32[]{:S(2)}) collective-permute-start(bf16[256,1024]{1,0:T(8,128)(2,1)} %bitcast.20), channel_id=1, source_target_pairs={{0,1},{1,0},{2,3},{3,2},{4,5},{5,4},{6,7},{7,6},{8,9},{9,8},{10,11... | collective-permute-start | bytes 1572872 | tf_op jit(solution)/shard_map/ppermute | solution.py:25
  172.5 14.5 %collective-permute-start.16 = (bf16[256,1024]{1,0:T(8,128)(2,1)}, bf16[256,1024]{1,0:T(8,128)(2,1)}, u32[]{:S(2)}, u32[]{:S(2)}) collective-permute-start(bf16[256,1024]{1,0:T(8,128)(2,1)} %convolution_convert_fusion.2), channel_id=1, source_target_pairs={{0,32},{32,0},{1,33},{33,1},{2,34},{34,2},{3,35},{35,3},{4,36},{36... | collective-permute-start | bytes 1572872 | tf_op jit(solution)/shard_map/ppermute | solution.py:25
  176.1 19.2 %all-to-all-start.8 = ((bf16[4,128,1024]{2,1,0:T(8,128)(2,1)}), bf16[4,128,1024]{2,1,0:T(8,128)(2,1)S(1)}, u32[]{:S(2)}, u32[]{:S(2)}) async-start(bf16[4,128,1024]{2,1,0:T(8,128)(2,1)} %bitcast.89), calls=%async_computation.8 | async-start | bytes 2097152 | tf_op jit(solution)/shard_map/all_to_all | solution.py:29
  195.3 13.5 %all-to-all-start.9 = ((bf16[4,64,1024]{2,1,0:T(8,128)(2,1)}), bf16[4,64,1024]{2,1,0:T(8,128)(2,1)}, u32[]{:S(2)}, u32[]{:S(2)}) async-start(bf16[4,64,1024]{2,1,0:T(8,128)(2,1)} %bitcast.94), calls=%async_computation.9 | async-start | bytes 1048576 | tf_op jit(solution)/shard_map/all_to_all | solution.py:29
  200.4 9.5 %collective-permute-start.13 = (bf16[64,1024]{1,0:T(8,128)(2,1)S(1)}, bf16[64,1024]{1,0:T(8,128)(2,1)S(1)}, u32[]{:S(2)}, u32[]{:S(2)}) collective-permute-start(bf16[64,1024]{1,0:T(8,128)(2,1)S(1)} %fusion.21), channel_id=1, source_target_pairs={{0,32},{32,0},{1,33},{33,1},{2,34},{34,2},{3,35},{35,3},{4,36},{36... | collective-permute-start | bytes 393224 | tf_op jit(solution)/shard_map/ppermute | solution.py:25
  212.1 5.1 %collective-permute-start.17 = (bf16[64,1024]{1,0:T(8,128)(2,1)S(1)}, bf16[64,1024]{1,0:T(8,128)(2,1)S(1)}, u32[]{:S(2)}, u32[]{:S(2)}) collective-permute-start(bf16[64,1024]{1,0:T(8,128)(2,1)S(1)} %slice.183), channel_id=1, source_target_pairs={{0,32},{32,0},{1,33},{33,1},{2,34},{34,2},{3,35},{35,3},{4,36},{36... | collective-permute-start | bytes 393224 | tf_op jit(solution)/shard_map/ppermute | solution.py:25
  218.0 11.5 %all-to-all-start.10 = ((bf16[4,64,1024]{2,1,0:T(8,128)(2,1)}), bf16[4,64,1024]{2,1,0:T(8,128)(2,1)S(1)}, u32[]{:S(2)}, u32[]{:S(2)}) async-start(bf16[4,64,1024]{2,1,0:T(8,128)(2,1)} %broadcast_in_dim.16), calls=%async_computation.10 | async-start | bytes 1048576 | tf_op jit(solution)/shard_map/all_to_all | solution.py:34
  230.7 14.9 %all-to-all-start.11 = ((bf16[4,128,1024]{2,1,0:T(8,128)(2,1)}), bf16[4,128,1024]{2,1,0:T(8,128)(2,1)S(1)}, u32[]{:S(2)}, u32[]{:S(2)}) async-start(bf16[4,128,1024]{2,1,0:T(8,128)(2,1)} %broadcast_in_dim.17), calls=%async_computation.11 | async-start | bytes 2097152 | tf_op jit(solution)/shard_map/all_to_all | solution.py:34
  234.2 11.4 %collective-permute-start.18 = (bf16[256,1024]{1,0:T(8,128)(2,1)}, bf16[256,1024]{1,0:T(8,128)(2,1)}, u32[]{:S(2)}, u32[]{:S(2)}) collective-permute-start(bf16[256,1024]{1,0:T(8,128)(2,1)} %bitcast.82), channel_id=1, source_target_pairs={{0,32},{32,0},{1,33},{33,1},{2,34},{34,2},{3,35},{35,3},{4,36},{36... | collective-permute-start | bytes 1572872 | tf_op jit(solution)/shard_map/ppermute | solution.py:25
  (19 other events, 86.9 us)

commit v3 on v1

--- a/solution.py
+++ b/solution.py
@@ -96,21 +96,53 @@
     )(*latents, *errors, decoder, norms)
 
 
-def transpose(value):
+def transpose(value, order, block):
     rows, cols = value.shape
-    tile = 256
-
-    def kernel(in_ref, out_ref):
+
+    def kernel(order_ref, in_ref, out_ref):
         out_ref[...] = in_ref[...].T
 
     return pl.pallas_call(
         kernel,
-        grid=(cols // tile,),
-        in_specs=[pl.BlockSpec((rows, tile), lambda i: (0, i))],
-        out_specs=pl.BlockSpec((tile, rows), lambda i: (i, 0)),
+        grid_spec=pltpu.PrefetchScalarGridSpec(
+            num_scalar_prefetch=1,
+            grid=(rows // block,),
+            in_specs=[pl.BlockSpec((block, cols), lambda i, order_ref: (order_ref[i], 0))],
+            out_specs=pl.BlockSpec((cols, block), lambda i, order_ref: (0, i)),
+        ),
         out_shape=jax.ShapeDtypeStruct((cols, rows), value.dtype),
         name="transpose",
-    )(value)
+    )(order, value)
+
+
+def encoder_grad(res_t, grads, part, so_far):
+    n = len(grads)
+    feat = res_t.shape[0]
+    block, width = grads[0].shape
+    tile = 256
+    last = so_far is not None
+
+    def kernel(res_ref, *refs):
+        total = refs[n][...] if last else jnp.zeros((tile, width), f32)
+        for i in range(n):
+            total += jnp.dot(
+                res_ref[:, i * block : (i + 1) * block],
+                refs[i][...],
+                preferred_element_type=f32,
+            )
+        refs[-1][...] = total.astype(refs[-1].dtype)
+
+    spec = pl.BlockSpec((tile, width), lambda i: (i, 0))
+    return pl.pallas_call(
+        kernel,
+        grid=(feat // tile,),
+        in_specs=[pl.BlockSpec((tile, n * block), lambda i: (i, part))]
+        + [pl.BlockSpec((block, width), lambda i: (0, 0))] * n
+        + [spec] * last,
+        out_specs=spec,
+        out_shape=jax.ShapeDtypeStruct((feat, width), bf16 if last else f32),
+        name="encoder_grad",
+    )(res_t, *grads, *([so_far] if last else []))
 
 
 def per_device(residual_rows, encoder, decoder, enc_bias, dec_bias):
@@ -135,11 +167,19 @@
 
     twin = (NEAR[2],) * 4
 
+    def gather_src(shard):
+        far = [move(shard, FAR, slot, False) for slot in (3, 2, 1, 0)][::-1]
+        near3, near1 = (move(shard, NEAR, slot, False) for slot in (3, 1))
+        mate = move(shard, twin, 0, False)
+        near = [jnp.where(first, shard, mate), near1, jnp.where(first, mate, shard), near3]
+        return near, far
+
     partial = dot(residual_rows, encoder).astype(bf16).reshape(N_SRC, block, -1)
     partial = lax.all_to_all(partial, SRC, 0, 0)
 
     squares = jnp.sum(jnp.square(decoder.astype(f32)), axis=1)
-    res_t = transpose(residual_rows)
+    order = [owner_row(o, s) // block for o in (NEAR, FAR) for s in range(4)]
+    res_t = transpose(residual_rows, jnp.stack(order), block)
     enc_bias, squares, res_t = lax.optimization_barrier((enc_bias, squares, res_t))
 
     pre_act = jnp.broadcast_to(enc_bias[None, :], partial.shape[1:])
@@ -148,12 +188,7 @@
     latent = (jax.nn.softplus(SHARPNESS * pre_act) / SHARPNESS).astype(bf16)
     slope = jax.nn.sigmoid(SHARPNESS * pre_act)
 
-    mate = move(latent, twin, 0, False)
-    near1 = move(latent, NEAR, 1, False)
-    near3 = move(latent, NEAR, 3, False)
-    latent_far, mate = lax.optimization_barrier((latent, mate))
-    far = [move(latent_far, FAR, slot, False) for slot in range(4)]
-    near = [jnp.where(first, latent, mate), near1, jnp.where(first, mate, latent), near3]
+    near, far = gather_src(latent)
 
     def core_sum(blocks):
         theirs = dot(jnp.concatenate(blocks[2:], axis=0), decoder).astype(bf16)
@@ -201,13 +236,13 @@
     for g in got:
         act_grad = act_grad + g.astype(f32)
     grad_pre = (loss_scale * act_grad * slope).astype(bf16)
-    grad_pre = jnp.broadcast_to(grad_pre[None], (N_SRC,) + grad_pre.shape)
-    grad_pre = lax.all_to_all(grad_pre, SRC, 0, 0).reshape(row_count, -1)
+    near_grad, far_grad = gather_src(grad_pre)
 
     scale = jnp.stack([own_norm] * 8)
     grad_decoder = decoder_grad(near + far, near_err + far_err, decoder, scale, loss_scale)
 
-    grad_encoder = dot(res_t, grad_pre).astype(bf16)
+    grad_encoder = encoder_grad(res_t, near_grad, 0, None)
+    grad_encoder = encoder_grad(res_t, far_grad, 1, grad_encoder)
     return (grad_encoder, grad_decoder)
 
 

time: 223 us -> 233 us (1.045)
  Pallas kernels: 12.8 us -> 27.2 us
  matrix products: 22.8 us -> 15.8 us
  waiting for transfers between devices: 87.4 us -> 93.7 us
  starting transfers between devices: 49.7 us -> 44.9 us
    ppermute x14 -> x21, waiting for transfers between devices: 28 us -> 53 us  [move(): return lax.ppermute(value, ('y', 'xl', 'core'), pairs)]
    all_to_all x1 -> x0, waiting for transfers between devices: 17.7 us -> none  [per_device(): grad_pre = lax.all_to_all(grad_pre, SRC, 0, 0).reshape(row_count, -1)]
    pallas_call x1 -> x3, Pallas kernels: 4.12 us -> 18.5 us  [the longest x2 11.8 us: encoder_grad(): pl.pallas_call(kernel, grid=(feat // tile,), in_specs=[pl.BlockSpec((tile...]
    dot_general x6 -> x5, matrix products: 15.8 us -> 8.08 us  [dot(): return jnp.dot(a, b, preferred_element_type=f32)]
    all_to_all x1 -> x0, starting transfers between devices: 4.37 us -> none  [per_device(): grad_pre = lax.all_to_all(grad_pre, SRC, 0, 0).reshape(row_count, -1)]
    all_to_all x1, waiting for transfers between devices: 20.9 us -> 17.6 us  [per_device(): partial = lax.all_to_all(partial, SRC, 0, 0)]
    ppermute x6, starting transfers between devices: 6.28 us -> 3.19 us  [swap(): return lax.ppermute(value, axis, [(i, i ^ mask) for i in range(size)])]
    ppermute x14 -> x21, starting transfers between devices: 22.9 us -> 25.5 us  [move(): return lax.ppermute(value, ('y', 'xl', 'core'), pairs)]
  transfers between devices with their start and end apart: 23 -> 29, of which waited for: 12 -> 13; matrix products, arithmetic and copies ran while one was open for 7% -> 6% of each run, Pallas kernels for 6% -> 9%
where the time goes in v3:
time: 233 us; the launch traced here: 231 us
  waiting for transfers between devices  93.7 us (40%)
  starting transfers between devices  44.9 us (19%)
  blocking collectives  32.7 us (14%)
  Pallas kernels  27.2 us (12%)
  matrix products  15.8 us (7%)
  other arithmetic  9.23 us (4%)
  local copies, waits for them, and re-layouts  6.35 us (3%)
    ppermute x21, waiting for transfers between devices, move(): return lax.ppermute(value, ('y', 'xl', 'core'), pairs)  53 us
    all_to_all x1, blocking collectives, per_device(): mine = lax.all_to_all(errors, RING, 0, 0).reshape(4, block, -1)  32.7 us
    ppermute x21, starting transfers between devices, move(): return lax.ppermute(value, ('y', 'xl', 'core'), pairs)  25.5 us
    all_to_all x1, waiting for transfers between devices, per_device(): partial = lax.all_to_all(partial, SRC, 0, 0)  17.6 us
    all_to_all x1, waiting for transfers between devices, per_device(): shares = lax.all_to_all(shares.reshape(N_RING, rows, -1), RING, 0, 0)  14.8 us
    pallas_call x2, Pallas kernels, encoder_grad(): pl.pallas_call(kernel, grid=(feat // tile,), in_specs=[pl.BlockSpec((tile...  11.8 us
    all_to_all x1, starting transfers between devices, per_device(): shares = lax.all_to_all(shares.reshape(N_RING, rows, -1), RING, 0, 0)  10.8 us
    pallas_call x1, Pallas kernels, decoder_grad(): pl.pallas_call(kernel, grid=(width // tile,), in_specs=[pl.BlockSpec((blo...  8.65 us
  transfers between devices with their start and end apart: 29, of which 13 were waited for; matrix products, arithmetic and copies ran while one was open for 6% of the time, Pallas kernels for 9%

profile of v3, /device:TPU:32, one launch (start us, length us, event | category | flops | bytes accessed | tf_op | source)
XLA Modules:
  0.0 231.5 jit_solution(9144223990233918231)
XLA Ops:
  2.2 5.2 %convolution_convert_fusion = bf16[1024,1024]{1,0:T(8,128)(2,1)} fusion(bf16[1024,1024]{1,0:T(8,128)(2,1)} %in_ref.1, bf16[1024,1024]{1,0:T(8,128)(2,1)S(1)} %copy-done), kind=kOutput, calls=%fused_computation.1 | convolution fusion | flops 2148532224 | bytes 6291456 | tf_op jit(solution)/shard_map/dot_general | solution.py:59
  7.5 5.4 %all-to-all-start = ((bf16[8,128,1024]{2,1,0:T(8,128)(2,1)}), bf16[8,128,1024]{2,1,0:T(8,128)(2,1)}, u32[]{:S(2)}, u32[]{:S(2)}) async-start(bf16[8,128,1024]{2,1,0:T(8,128)(2,1)} %bitcast.193), calls=%async_computation | async-start | bytes 4194304 | tf_op jit(solution)/shard_map/all_to_all | solution.py:178
  13.5 6.8 %transpose.19.res_ref = bf16[1024,1024]{1,0:T(8,128)(2,1)} custom-call(s32[8]{0:T(128)} %stack.61.order_ref, bf16[1024,1024]{1,0:T(8,128)(2,1)} %in_ref.1), custom_call_target="tpu_custom_call" | custom-call | tf_op jit(solution)/shard_map/transpose/pallas_call | solution.py:105
  20.3 2.1 multiply_reduce_fusion
  22.3 17.6 %all-to-all-done = bf16[8,128,1024]{2,1,0:T(8,128)(2,1)} async-done(((bf16[8,128,1024]{2,1,0:T(8,128)(2,1)}), bf16[8,128,1024]{2,1,0:T(8,128)(2,1)}, u32[]{:S(2)}, u32[]{:S(2)}) %all-to-all-start) | async-done | bytes 2097184 | tf_op jit(solution)/shard_map/all_to_all | solution.py:178
  40.0 3.0 %fusion.13 = (bf16[128,1024]{1,0:T(8,128)(2,1)S(1)}, f32[128,1024]{1,0:T(8,128)}) fusion(bf16[8,128,1024]{2,1,0:T(8,128)(2,1)} %all-to-all-done, f32[1024]{0:T(1024)S(1)} %copy-done.21), kind=kLoop, calls=%fused_computation.29 | loop fusion | flops 3276800 | bytes 2887680 | tf_op jit(solution)/shard_map/convert_element_type | solution.py:188
  44.4 1.8 collective-permute-start.7
  46.4 3.9 %collective-permute-start.4 = (bf16[128,1024]{1,0:T(8,128)(2,1)S(1)}, bf16[128,1024]{1,0:T(8,128)(2,1)S(1)}, u32[]{:S(2)}, u32[]{:S(2)}) collective-permute-start(bf16[128,1024]{1,0:T(8,128)(2,1)S(1)} %get-tuple-element.20), channel_id=1, source_target_pairs={{128,0},{97,1},{160,32},{65,33},{192,64},{161,65},{224,96},{129,97... | collective-permute-start | bytes 786440 | tf_op jit(solution)/shard_map/ppermute | solution.py:55
  51.5 1.7 collective-permute-done.6.refs_6_
  53.3 6.1 %collective-permute-done.7.refs_7_ = bf16[128,1024]{1,0:T(8,128)(2,1)S(1)} collective-permute-done((bf16[128,1024]{1,0:T(8,128)(2,1)S(1)}, bf16[128,1024]{1,0:T(8,128)(2,1)S(1)}, u32[]{:S(2)}, u32[]{:S(2)}) %collective-permute-start.7) | collective-permute-done | bytes 262176 | tf_op jit(solution)/shard_map/ppermute | solution.py:55
  60.2 9.0 %collective-permute-done = bf16[128,1024]{1,0:T(8,128)(2,1)S(1)} collective-permute-done((bf16[128,1024]{1,0:T(8,128)(2,1)S(1)}, bf16[128,1024]{1,0:T(8,128)(2,1)S(1)}, u32[]{:S(2)}, u32[]{:S(2)}) %collective-permute-start) | collective-permute-done | bytes 262176 | tf_op jit(solution)/shard_map/ppermute | solution.py:55
  72.3 4.4 %collective-permute-done.1.refs_1_ = bf16[128,1024]{1,0:T(8,128)(2,1)S(1)} collective-permute-done((bf16[128,1024]{1,0:T(8,128)(2,1)S(1)}, bf16[128,1024]{1,0:T(8,128)(2,1)S(1)}, u32[]{:S(2)}, u32[]{:S(2)}) %collective-permute-start.1) | collective-permute-done | bytes 262176 | tf_op jit(solution)/shard_map/ppermute | solution.py:55
  78.5 10.8 %all-to-all-start.1 = ((bf16[16,32,1024]{2,1,0:T(8,128)(2,1)}), bf16[16,32,1024]{2,1,0:T(8,128)(2,1)S(1)}, u32[]{:S(2)}, u32[]{:S(2)}) async-start(bf16[16,32,1024]{2,1,0:T(8,128)(2,1)} %bitcast.182), calls=%async_computation.1 | async-start | bytes 2097152 | tf_op jit(solution)/shard_map/all_to_all | solution.py:202
  89.8 3.3 %collective-permute-done.9 = f32[1024]{0:T(1024)S(1)} collective-permute-done((f32[1024]{0:T(1024)S(1)}, f32[1024]{0:T(1024)S(1)}, u32[]{:S(2)}, u32[]{:S(2)}) %collective-permute-start.9) | collective-permute-done | bytes 4128 | tf_op jit(solution)/shard_map/ppermute | solution.py:35
  93.5 3.2 %collective-permute-done.10 = f32[1024]{0:T(1024)S(1)} collective-permute-done((f32[1024]{0:T(1024)S(1)}, f32[1024]{0:T(1024)S(1)}, u32[]{:S(2)}, u32[]{:S(2)}) %collective-permute-start.10) | collective-permute-done | bytes 4128 | tf_op jit(solution)/shard_map/ppermute | solution.py:35
  96.7 1.9 collective-permute-start.11
  100.0 1.8 collective-permute-done.11
  101.8 14.8 %all-to-all-done.1 = bf16[16,32,1024]{2,1,0:T(8,128)(2,1)S(1)} async-done(((bf16[16,32,1024]{2,1,0:T(8,128)(2,1)}), bf16[16,32,1024]{2,1,0:T(8,128)(2,1)S(1)}, u32[]{:S(2)}, u32[]{:S(2)}) %all-to-all-start.1) | async-done | bytes 1048608 | tf_op jit(solution)/shard_map/all_to_all | solution.py:202
  117.9 32.7 %all_to_all.15 = bf16[16,32,1024]{2,1,0:T(8,128)(2,1)S(1)} all-to-all(bf16[16,32,1024]{2,1,0:T(8,128)(2,1)S(1)} %broadcast_in_dim.8), channel_id=1, replica_groups=mesh['y'=4,'xl'=2,'xh'=2,'z'=8,'core'=2] {'xh','z'}, dimensions={0} | all-to-all | bytes 2097152 | tf_op jit(solution)/shard_map/all_to_all | solution.py:220
  151.6 2.3 %collective-permute-start.14 = (bf16[128,1024]{1,0:T(8,128)(2,1)S(1)}, bf16[128,1024]{1,0:T(8,128)(2,1)S(1)}, u32[]{:S(2)}, u32[]{:S(2)}) collective-permute-start(bf16[128,1024]{1,0:T(8,128)(2,1)S(1)} %convolution_convert_fusion.8), channel_id=1, source_target_pairs={{0,224},{1,161},{32,192},{33,129},{64,32},{65,225},{96,0},{97,193}... | collective-permute-start | bytes 786440 | tf_op jit(solution)/shard_map/ppermute | solution.py:55
  159.5 2.5 %collective-permute-start.19 = (bf16[128,1024]{1,0:T(8,128)(2,1)S(1)}, bf16[128,1024]{1,0:T(8,128)(2,1)S(1)}, u32[]{:S(2)}, u32[]{:S(2)}) collective-permute-start(bf16[128,1024]{1,0:T(8,128)(2,1)S(1)} %convolution_convert_fusion.3), channel_id=1, source_target_pairs={{0,192},{1,193},{32,224},{33,225},{64,0},{65,1},{96,32},{97,33},{1... | collective-permute-start | bytes 786440 | tf_op jit(solution)/shard_map/ppermute | solution.py:55
  165.0 4.5 %collective-permute-done.13 = bf16[128,1024]{1,0:T(8,128)(2,1)S(1)} collective-permute-done((bf16[128,1024]{1,0:T(8,128)(2,1)S(1)}, bf16[128,1024]{1,0:T(8,128)(2,1)S(1)}, u32[]{:S(2)}, u32[]{:S(2)}) %collective-permute-start.13) | collective-permute-done | bytes 262176 | tf_op jit(solution)/shard_map/ppermute | solution.py:55
  170.0 10.8 %collective-permute-done.18 = bf16[128,1024]{1,0:T(8,128)(2,1)S(1)} collective-permute-done((bf16[128,1024]{1,0:T(8,128)(2,1)S(1)}, bf16[128,1024]{1,0:T(8,128)(2,1)S(1)}, u32[]{:S(2)}, u32[]{:S(2)}) %collective-permute-start.18) | collective-permute-done | bytes 262176 | tf_op jit(solution)/shard_map/ppermute | solution.py:55
  180.8 1.8 fusion.11
  183.5 2.4 %collective-permute-start.26 = (bf16[128,1024]{1,0:T(8,128)(2,1)}, bf16[128,1024]{1,0:T(8,128)(2,1)S(1)}, u32[]{:S(2)}, u32[]{:S(2)}) collective-permute-start(bf16[128,1024]{1,0:T(8,128)(2,1)} %fusion.11), channel_id=1, source_target_pairs={{64,0},{33,1},{96,32},{1,33},{128,64},{97,65},{160,96},{65,97},{19... | collective-permute-start | bytes 786440 | tf_op jit(solution)/shard_map/ppermute | solution.py:55
  186.6 2.5 %collective-permute-start.22 = (bf16[128,1024]{1,0:T(8,128)(2,1)}, bf16[128,1024]{1,0:T(8,128)(2,1)S(1)}, u32[]{:S(2)}, u32[]{:S(2)}) collective-permute-start(bf16[128,1024]{1,0:T(8,128)(2,1)} %fusion.11), channel_id=1, source_target_pairs={{96,0},{129,1},{64,32},{161,33},{160,64},{193,65},{128,96},{225,97... | collective-permute-start | bytes 786440 | tf_op jit(solution)/shard_map/ppermute | solution.py:55
  189.1 2.4 %collective-permute-done.25.refs_1_ = bf16[128,1024]{1,0:T(8,128)(2,1)S(1)} collective-permute-done((bf16[128,1024]{1,0:T(8,128)(2,1)}, bf16[128,1024]{1,0:T(8,128)(2,1)S(1)}, u32[]{:S(2)}, u32[]{:S(2)}) %collective-permute-start.25) | collective-permute-done | bytes 262176 | tf_op jit(solution)/shard_map/ppermute | solution.py:55
  191.7 14.2 %collective-permute-done.24 = bf16[128,1024]{1,0:T(8,128)(2,1)} collective-permute-done((bf16[128,1024]{1,0:T(8,128)(2,1)}, bf16[128,1024]{1,0:T(8,128)(2,1)}, u32[]{:S(2)}, u32[]{:S(2)}) %collective-permute-start.24) | collective-permute-done | bytes 262176 | tf_op jit(solution)/shard_map/ppermute | solution.py:55
  207.6 8.7 %decoder_grad.1 = bf16[1024,1024]{1,0:T(8,128)(2,1)} custom-call(bf16[128,1024]{1,0:T(8,128)(2,1)} %copy-done.7, bf16[128,1024]{1,0:T(8,128)(2,1)} %copy-done.15, bf16[128,1024]{1,0:T(8,128)(2,1)} %copy-done.8, bf16[128,1024]{1,0:T(8,128)(2,1)} %copy-done.14, bf16[128,1024]{1,0:T(8,128)(2,1)} %copy-done.13, bf16[128,1024]{1,0:T(8,128)(2,1)} %copy-done.12, ...), custom_call_target="tpu_custom_call" | custom-call | tf_op jit(solution)/shard_map/decoder_grad/pallas_call | solution.py:84
  216.2 1.9 broadcast_select_fusion
  218.8 5.7 %encoder_grad.2.refs_4_ = f32[1024,1024]{1,0:T(8,128)} custom-call(bf16[1024,1024]{1,0:T(8,128)(2,1)} %transpose.19.res_ref, bf16[128,1024]{1,0:T(8,128)(2,1)} %get-tuple-element.31.refs_0_, bf16[128,1024]{1,0:T(8,128)(2,1)} %copy-done.18, bf16[128,1024]{1,0:T(8,128)(2,1)} %get-tuple-element.30.refs_2_, bf16[128,1024]{1,0:T(8,128)(2,1)} %copy-done.20), custom_call_target="tpu_custom_call" | custom-call | tf_op jit(solution)/shard_map/encoder_grad/pallas_call | solution.py:136
  225.4 6.1 %encoder_grad.3 = bf16[1024,1024]{1,0:T(8,128)(2,1)} custom-call(bf16[1024,1024]{1,0:T(8,128)(2,1)} %transpose.19.res_ref, bf16[128,1024]{1,0:T(8,128)(2,1)} %collective-permute-done.20.refs_0_, bf16[128,1024]{1,0:T(8,128)(2,1)} %copy-done.19, bf16[128,1024]{1,0:T(8,128)(2,1)} %copy-done.17, bf16[128,1024]{1,0:T(8,128)(2,1)} %copy-done.16, ...), custom_call_target="tpu_custom_call" | custom-call | tf_op jit(solution)/shard_map/encoder_grad/pallas_call | solution.py:136
  (106 shorter events, 28.7 us)
Async XLA Ops:
  7.5 32.5 %all-to-all-start = ((bf16[8,128,1024]{2,1,0:T(8,128)(2,1)}), bf16[8,128,1024]{2,1,0:T(8,128)(2,1)}, u32[]{:S(2)}, u32[]{:S(2)}) async-start(bf16[8,128,1024]{2,1,0:T(8,128)(2,1)} %bitcast.193), calls=%async_computation | async-start | bytes 4194304 | tf_op jit(solution)/shard_map/all_to_all | solution.py:178
  43.0 10.2 %collective-permute-start.6 = (bf16[128,1024]{1,0:T(8,128)(2,1)S(1)}, bf16[128,1024]{1,0:T(8,128)(2,1)S(1)}, u32[]{:S(2)}, u32[]{:S(2)}) collective-permute-start(bf16[128,1024]{1,0:T(8,128)(2,1)S(1)} %get-tuple-element.20), channel_id=1, source_target_pairs={{96,0},{129,1},{64,32},{161,33},{160,64},{193,65},{128,96},{225,97... | collective-permute-start | bytes 786440 | tf_op jit(solution)/shard_map/ppermute | solution.py:55
  44.4 14.9 %collective-permute-start.7 = (bf16[128,1024]{1,0:T(8,128)(2,1)S(1)}, bf16[128,1024]{1,0:T(8,128)(2,1)S(1)}, u32[]{:S(2)}, u32[]{:S(2)}) collective-permute-start(bf16[128,1024]{1,0:T(8,128)(2,1)S(1)} %get-tuple-element.20), channel_id=1, source_target_pairs={{160,0},{225,1},{128,32},{193,33},{224,64},{33,65},{192,96},{1,97}... | collective-permute-start | bytes 786440 | tf_op jit(solution)/shard_map/ppermute | solution.py:55
  46.2 25.3 %collective-permute-start.5 = (bf16[128,1024]{1,0:T(8,128)(2,1)S(1)}, bf16[128,1024]{1,0:T(8,128)(2,1)S(1)}, u32[]{:S(2)}, u32[]{:S(2)}) collective-permute-start(bf16[128,1024]{1,0:T(8,128)(2,1)S(1)} %get-tuple-element.20), channel_id=1, source_target_pairs={{224,0},{161,1},{192,32},{129,33},{32,64},{225,65},{0,96},{193,97}... | collective-permute-start | bytes 786440 | tf_op jit(solution)/shard_map/ppermute | solution.py:55
  46.4 25.1 %collective-permute-start.4 = (bf16[128,1024]{1,0:T(8,128)(2,1)S(1)}, bf16[128,1024]{1,0:T(8,128)(2,1)S(1)}, u32[]{:S(2)}, u32[]{:S(2)}) collective-permute-start(bf16[128,1024]{1,0:T(8,128)(2,1)S(1)} %get-tuple-element.20), channel_id=1, source_target_pairs={{128,0},{97,1},{160,32},{65,33},{192,64},{161,65},{224,96},{129,97... | collective-permute-start | bytes 786440 | tf_op jit(solution)/shard_map/ppermute | solution.py:55
  50.3 18.9 %collective-permute-start.2 = (bf16[128,1024]{1,0:T(8,128)(2,1)S(1)}, bf16[128,1024]{1,0:T(8,128)(2,1)S(1)}, u32[]{:S(2)}, u32[]{:S(2)}) collective-permute-start(bf16[128,1024]{1,0:T(8,128)(2,1)S(1)} %get-tuple-element.20), channel_id=1, source_target_pairs={{64,0},{33,1},{96,32},{1,33},{128,64},{97,65},{160,96},{65,97},{19... | collective-permute-start | bytes 786440 | tf_op jit(solution)/shard_map/ppermute | solution.py:55
  53.2 15.9 %collective-permute-start = (bf16[128,1024]{1,0:T(8,128)(2,1)S(1)}, bf16[128,1024]{1,0:T(8,128)(2,1)S(1)}, u32[]{:S(2)}, u32[]{:S(2)}) collective-permute-start(bf16[128,1024]{1,0:T(8,128)(2,1)S(1)} %get-tuple-element.20), channel_id=1, source_target_pairs={{192,0},{193,1},{224,32},{225,33},{0,64},{1,65},{32,96},{33,97},{6... | collective-permute-start | bytes 786440 | tf_op jit(solution)/shard_map/ppermute | solution.py:55
  60.0 11.5 %collective-permute-start.8 = (bf16[256,1024]{1,0:T(8,128)(2,1)S(1)}, bf16[256,1024]{1,0:T(8,128)(2,1)S(1)}, u32[]{:S(2)}, u32[]{:S(2)}) collective-permute-start(bf16[256,1024]{1,0:T(8,128)(2,1)S(1)} %convolution_convert_fusion.1), channel_id=1, source_target_pairs={{0,1},{1,0},{2,3},{3,2},{4,5},{5,4},{6,7},{7,6},{8,9},{9,8},{10,11... | collective-permute-start | bytes 1572872 | tf_op jit(solution)/shard_map/ppermute | solution.py:35
  69.9 6.7 %collective-permute-start.3 = (bf16[256,1024]{1,0:T(8,128)(2,1)S(1)}, bf16[256,1024]{1,0:T(8,128)(2,1)S(1)}, u32[]{:S(2)}, u32[]{:S(2)}) collective-permute-start(bf16[256,1024]{1,0:T(8,128)(2,1)S(1)} %convolution_convert_fusion.2), channel_id=1, source_target_pairs={{0,1},{1,0},{2,3},{3,2},{4,5},{5,4},{6,7},{7,6},{8,9},{9,8},{10,11... | collective-permute-start | bytes 1572872 | tf_op jit(solution)/shard_map/ppermute | solution.py:35
  70.0 6.6 %collective-permute-start.1 = (bf16[128,1024]{1,0:T(8,128)(2,1)S(1)}, bf16[128,1024]{1,0:T(8,128)(2,1)S(1)}, u32[]{:S(2)}, u32[]{:S(2)}) collective-permute-start(bf16[128,1024]{1,0:T(8,128)(2,1)S(1)} %get-tuple-element.20), channel_id=1, source_target_pairs={{32,0},{65,1},{0,32},{97,33},{96,64},{129,65},{64,96},{161,97},{16... | collective-permute-start | bytes 786440 | tf_op jit(solution)/shard_map/ppermute | solution.py:55
  77.4 39.2 %copy-start.22 = (f32[1024]{0:T(1024)S(1)}, f32[1024]{0:T(1024)}, u32[]{:S(2)}) copy-start(f32[1024]{0:T(1024)} %param.9) | copy-start | bytes 12292
  78.5 38.2 %all-to-all-start.1 = ((bf16[16,32,1024]{2,1,0:T(8,128)(2,1)}), bf16[16,32,1024]{2,1,0:T(8,128)(2,1)S(1)}, u32[]{:S(2)}, u32[]{:S(2)}) async-start(bf16[16,32,1024]{2,1,0:T(8,128)(2,1)} %bitcast.182), calls=%async_computation.1 | async-start | bytes 2097152 | tf_op jit(solution)/shard_map/all_to_all | solution.py:202
  89.2 3.9 %collective-permute-start.9 = (f32[1024]{0:T(1024)S(1)}, f32[1024]{0:T(1024)S(1)}, u32[]{:S(2)}, u32[]{:S(2)}) collective-permute-start(f32[1024]{0:T(1024)S(1)} %multiply_reduce_fusion), channel_id=1, source_target_pairs={{0,32},{32,0},{1,33},{33,1},{2,34},{34,2},{3,35},{35,3},{4,36},{36... | collective-permute-start | bytes 12296 | tf_op jit(solution)/shard_map/ppermute | solution.py:35
  93.1 3.6 %collective-permute-start.10 = (f32[1024]{0:T(1024)S(1)}, f32[1024]{0:T(1024)S(1)}, u32[]{:S(2)}, u32[]{:S(2)}) collective-permute-start(f32[1024]{0:T(1024)S(1)} %add.253), channel_id=1, source_target_pairs={{0,64},{64,0},{128,192},{192,128},{1,65},{65,1},{129,193},{193,129... | collective-permute-start | bytes 12296 | tf_op jit(solution)/shard_map/ppermute | solution.py:35
  96.7 5.1 %collective-permute-start.11 = (f32[1024]{0:T(1024)S(1)}, f32[1024]{0:T(1024)S(1)}, u32[]{:S(2)}, u32[]{:S(2)}) collective-permute-start(f32[1024]{0:T(1024)S(1)} %get-tuple-element.19), channel_id=1, source_target_pairs={{0,128},{64,192},{128,0},{192,64},{1,129},{65,193},{129,1},{193,65... | collective-permute-start | bytes 12296 | tf_op jit(solution)/shard_map/ppermute | solution.py:35
  117.8 32.9 %copy-start.2 = (bf16[1024,1024]{1,0:T(8,128)(2,1)S(1)}, bf16[1024,1024]{1,0:T(8,128)(2,1)}, u32[]{:S(2)}) copy-start(bf16[1024,1024]{1,0:T(8,128)(2,1)} %refs_16_.1) | copy-start | bytes 6291460
  150.6 6.3 %collective-permute-start.12 = (bf16[4,128,1024]{2,1,0:T(8,128)(2,1)S(1)}, bf16[4,128,1024]{2,1,0:T(8,128)(2,1)S(1)}, u32[]{:S(2)}, u32[]{:S(2)}) collective-permute-start(bf16[4,128,1024]{2,1,0:T(8,128)(2,1)S(1)} %bitcast.183), channel_id=1, source_target_pairs={{0,1},{1,0},{2,3},{3,2},{4,5},{5,4},{6,7},{7,6},{8,9},{9,8},{10,11... | collective-permute-start | bytes 3145736 | tf_op jit(solution)/shard_map/ppermute | solution.py:35
  150.7 30.1 %copy-start.6 = (bf16[4,32,1024]{2,1,0:T(8,128)(2,1)}, bf16[4,32,1024]{2,1,0:T(8,128)(2,1)S(1)}, u32[]{:S(2)}) copy-start(bf16[4,32,1024]{2,1,0:T(8,128)(2,1)S(1)} %get-tuple-element.29) | copy-start | bytes 786436
  151.6 12.1 %collective-permute-start.14 = (bf16[128,1024]{1,0:T(8,128)(2,1)S(1)}, bf16[128,1024]{1,0:T(8,128)(2,1)S(1)}, u32[]{:S(2)}, u32[]{:S(2)}) collective-permute-start(bf16[128,1024]{1,0:T(8,128)(2,1)S(1)} %convolution_convert_fusion.8), channel_id=1, source_target_pairs={{0,224},{1,161},{32,192},{33,129},{64,32},{65,225},{96,0},{97,193}... | collective-permute-start | bytes 786440 | tf_op jit(solution)/shard_map/ppermute | solution.py:55
  154.8 14.7 %collective-permute-start.13 = (bf16[128,1024]{1,0:T(8,128)(2,1)S(1)}, bf16[128,1024]{1,0:T(8,128)(2,1)S(1)}, u32[]{:S(2)}, u32[]{:S(2)}) collective-permute-start(bf16[128,1024]{1,0:T(8,128)(2,1)S(1)} %convolution_convert_fusion.9), channel_id=1, source_target_pairs={{0,128},{1,97},{32,160},{33,65},{64,192},{65,161},{96,224},{97,129... | collective-permute-start | bytes 786440 | tf_op jit(solution)/shard_map/ppermute | solution.py:55
  156.8 13.2 %collective-permute-start.15 = (bf16[128,1024]{1,0:T(8,128)(2,1)S(1)}, bf16[128,1024]{1,0:T(8,128)(2,1)S(1)}, u32[]{:S(2)}, u32[]{:S(2)}) collective-permute-start(bf16[128,1024]{1,0:T(8,128)(2,1)S(1)} %convolution_convert_fusion.7), channel_id=1, source_target_pairs={{0,32},{1,65},{32,0},{33,97},{64,96},{65,129},{96,64},{97,161},{12... | collective-permute-start | bytes 786440 | tf_op jit(solution)/shard_map/ppermute | solution.py:55
  157.7 23.0 %collective-permute-start.18 = (bf16[128,1024]{1,0:T(8,128)(2,1)S(1)}, bf16[128,1024]{1,0:T(8,128)(2,1)S(1)}, u32[]{:S(2)}, u32[]{:S(2)}) collective-permute-start(bf16[128,1024]{1,0:T(8,128)(2,1)S(1)} %convolution_convert_fusion.4), channel_id=1, source_target_pairs={{0,64},{1,33},{32,96},{33,1},{64,128},{65,97},{96,160},{97,65},{12... | collective-permute-start | bytes 786440 | tf_op jit(solution)/shard_map/ppermute | solution.py:55
  159.5 21.2 %collective-permute-start.19 = (bf16[128,1024]{1,0:T(8,128)(2,1)S(1)}, bf16[128,1024]{1,0:T(8,128)(2,1)S(1)}, u32[]{:S(2)}, u32[]{:S(2)}) collective-permute-start(bf16[128,1024]{1,0:T(8,128)(2,1)S(1)} %convolution_convert_fusion.3), channel_id=1, source_target_pairs={{0,192},{1,193},{32,224},{33,225},{64,0},{65,1},{96,32},{97,33},{1... | collective-permute-start | bytes 786440 | tf_op jit(solution)/shard_map/ppermute | solution.py:55
  163.7 17.1 %collective-permute-start.16 = (bf16[128,1024]{1,0:T(8,128)(2,1)S(1)}, bf16[128,1024]{1,0:T(8,128)(2,1)S(1)}, u32[]{:S(2)}, u32[]{:S(2)}) collective-permute-start(bf16[128,1024]{1,0:T(8,128)(2,1)S(1)} %convolution_convert_fusion.6), channel_id=1, source_target_pairs={{0,96},{1,129},{32,64},{33,161},{64,160},{65,193},{96,128},{97,225... | collective-permute-start | bytes 786440 | tf_op jit(solution)/shard_map/ppermute | solution.py:55
  169.5 11.2 %collective-permute-start.17 = (bf16[128,1024]{1,0:T(8,128)(2,1)S(1)}, bf16[128,1024]{1,0:T(8,128)(2,1)S(1)}, u32[]{:S(2)}, u32[]{:S(2)}) collective-permute-start(bf16[128,1024]{1,0:T(8,128)(2,1)S(1)} %convolution_convert_fusion.5), channel_id=1, source_target_pairs={{0,160},{1,225},{32,128},{33,193},{64,224},{65,33},{96,192},{97,1}... | collective-permute-start | bytes 786440 | tf_op jit(solution)/shard_map/ppermute | solution.py:55
  182.6 8.9 %collective-permute-start.25 = (bf16[128,1024]{1,0:T(8,128)(2,1)}, bf16[128,1024]{1,0:T(8,128)(2,1)S(1)}, u32[]{:S(2)}, u32[]{:S(2)}) collective-permute-start(bf16[128,1024]{1,0:T(8,128)(2,1)} %fusion.11), channel_id=1, source_target_pairs={{32,0},{65,1},{0,32},{97,33},{96,64},{129,65},{64,96},{161,97},{16... | collective-permute-start | bytes 786440 | tf_op jit(solution)/shard_map/ppermute | solution.py:55
  182.6 23.3 %collective-permute-start.24 = (bf16[128,1024]{1,0:T(8,128)(2,1)}, bf16[128,1024]{1,0:T(8,128)(2,1)}, u32[]{:S(2)}, u32[]{:S(2)}) collective-permute-start(bf16[128,1024]{1,0:T(8,128)(2,1)} %fusion.11), channel_id=1, source_target_pairs={{192,0},{193,1},{224,32},{225,33},{0,64},{1,65},{32,96},{33,97},{6... | collective-permute-start | bytes 786440 | tf_op jit(solution)/shard_map/ppermute | solution.py:55
  183.5 34.6 %collective-permute-start.26 = (bf16[128,1024]{1,0:T(8,128)(2,1)}, bf16[128,1024]{1,0:T(8,128)(2,1)S(1)}, u32[]{:S(2)}, u32[]{:S(2)}) collective-permute-start(bf16[128,1024]{1,0:T(8,128)(2,1)} %fusion.11), channel_id=1, source_target_pairs={{64,0},{33,1},{96,32},{1,33},{128,64},{97,65},{160,96},{65,97},{19... | collective-permute-start | bytes 786440 | tf_op jit(solution)/shard_map/ppermute | solution.py:55
  185.8 38.7 %collective-permute-start.23 = (bf16[128,1024]{1,0:T(8,128)(2,1)}, bf16[128,1024]{1,0:T(8,128)(2,1)S(1)}, u32[]{:S(2)}, u32[]{:S(2)}) collective-permute-start(bf16[128,1024]{1,0:T(8,128)(2,1)} %fusion.11), channel_id=1, source_target_pairs={{160,0},{225,1},{128,32},{193,33},{224,64},{33,65},{192,96},{1,97}... | collective-permute-start | bytes 786440 | tf_op jit(solution)/shard_map/ppermute | solution.py:55
  186.6 37.9 %collective-permute-start.22 = (bf16[128,1024]{1,0:T(8,128)(2,1)}, bf16[128,1024]{1,0:T(8,128)(2,1)S(1)}, u32[]{:S(2)}, u32[]{:S(2)}) collective-permute-start(bf16[128,1024]{1,0:T(8,128)(2,1)} %fusion.11), channel_id=1, source_target_pairs={{96,0},{129,1},{64,32},{161,33},{160,64},{193,65},{128,96},{225,97... | collective-permute-start | bytes 786440 | tf_op jit(solution)/shard_map/ppermute | solution.py:55
  191.5 33.1 %collective-permute-start.21 = (bf16[128,1024]{1,0:T(8,128)(2,1)}, bf16[128,1024]{1,0:T(8,128)(2,1)S(1)}, u32[]{:S(2)}, u32[]{:S(2)}) collective-permute-start(bf16[128,1024]{1,0:T(8,128)(2,1)} %fusion.11), channel_id=1, source_target_pairs={{224,0},{161,1},{192,32},{129,33},{32,64},{225,65},{0,96},{193,97}... | collective-permute-start | bytes 786440 | tf_op jit(solution)/shard_map/ppermute | solution.py:55
  205.9 18.6 %collective-permute-start.20 = (bf16[128,1024]{1,0:T(8,128)(2,1)}, bf16[128,1024]{1,0:T(8,128)(2,1)}, u32[]{:S(2)}, u32[]{:S(2)}) collective-permute-start(bf16[128,1024]{1,0:T(8,128)(2,1)} %fusion.11), channel_id=1, source_target_pairs={{128,0},{97,1},{160,32},{65,33},{192,64},{161,65},{224,96},{129,97... | collective-permute-start | bytes 786440 | tf_op jit(solution)/shard_map/ppermute | solution.py:55
  (20 other events, 135.2 us)

commit v4 on v3

--- a/solution.py
+++ b/solution.py
@@ -63,24 +63,74 @@
     return jnp.einsum("bk,jk->bj", a, b, preferred_element_type=f32)
 
 
+def blocks_dot(weight, contract, dtypes, blocks=None, source=None, order=None):
+    n = len(dtypes)
+    tile = 256
+    depth = weight.shape[contract]
+    width = weight.shape[1 - contract]
+    block = blocks[0].shape[0] if source is None else source.shape[0] // N_SRC
+
+    def kernel(order_ref, *refs):
+        ins, w_ref, outs, all_ref = refs[:n], refs[n], refs[n + 1 : 2 * n + 1], refs[-1]
+
+        @pl.when(pl.program_id(0) == 0)
+        def _():
+            for i in range(n):
+                all_ref[i * block : (i + 1) * block] = ins[i][...]
+
+        product = lax.dot_general(
+            all_ref[...], w_ref[...], (((1,), (contract,)), ((), ())), preferred_element_type=f32
+        )
+        for i in range(n):
+            outs[i][...] = product[i * block : (i + 1) * block].astype(outs[i].dtype)
+
+    if source is None:
+        order = jnp.zeros((1,), jnp.int32)
+        in_specs = [pl.BlockSpec((block, depth), lambda i, o: (0, 0))] * n
+    else:
+        blocks = [source] * n
+        in_specs = [pl.BlockSpec((block, depth), lambda i, o, p=p: (o[p], 0)) for p in range(n)]
+    if contract == 0:
+        w_spec = pl.BlockSpec((depth, tile), lambda i, o: (0, i))
+    else:
+        w_spec = pl.BlockSpec((tile, depth), lambda i, o: (i, 0))
+    return pl.pallas_call(
+        kernel,
+        grid_spec=pltpu.PrefetchScalarGridSpec(
+            num_scalar_prefetch=1,
+            grid=(width // tile,),
+            in_specs=in_specs + [w_spec],
+            out_specs=[pl.BlockSpec((block, tile), lambda i, o: (0, i))] * n,
+            scratch_shapes=[pltpu.VMEM((n * block, depth), bf16)],
+        ),
+        out_shape=[jax.ShapeDtypeStruct((block, width), d) for d in dtypes],
+        name="blocks_dot",
+    )(order, *blocks, weight)
+
+
 def decoder_grad(latents, errors, decoder, norms, loss_scale):
     n = len(latents)
     width, feat = decoder.shape
+    block = latents[0].shape[0]
+    rows = n * block
     tile = 256
 
     def kernel(*refs):
         lat, err = refs[:n], refs[n : 2 * n]
-        dec_ref, norm_ref, out_ref = refs[2 * n :]
-        outer = jnp.zeros((tile, feat), f32)
-        sums = jnp.zeros((tile, 1), f32)
-        for l_ref, e_ref in zip(lat, err):
-            tall = l_ref[...].T
-            outer += jnp.dot(tall, e_ref[...], preferred_element_type=f32)
-            sums += jnp.sum(tall.astype(f32), axis=1, keepdims=True)
+        dec_ref, norm_ref, out_ref, err_all = refs[2 * n :]
+
+        @pl.when(pl.program_id(0) == 0)
+        def _():
+            for i in range(n):
+                err_all[i * block : (i + 1) * block] = err[i][...]
+
+        tall = jnp.concatenate([l_ref[...] for l_ref in lat], axis=0).T
+        outer = jnp.dot(tall, err_all[...], preferred_element_type=f32)
+        ones = jnp.ones((rows, 128), bf16)
+        sums = jnp.dot(tall, ones, preferred_element_type=f32)[:, :1]
         shrink = loss_scale * PENALTY * sums / norm_ref[...].T[:, :1]
         out_ref[...] = (loss_scale * outer + shrink * dec_ref[...].astype(f32)).astype(bf16)
 
-    block = latents[0].shape[0]
     return pl.pallas_call(
         kernel,
         grid=(width // tile,),
@@ -92,6 +142,7 @@
         ],
         out_specs=pl.BlockSpec((tile, feat), lambda i: (i, 0)),
         out_shape=jax.ShapeDtypeStruct(decoder.shape, bf16),
+        scratch_shapes=[pltpu.VMEM((rows, feat), bf16)],
         name="decoder_grad",
     )(*latents, *errors, decoder, norms)
 
@@ -123,14 +174,17 @@
     last = so_far is not None
 
     def kernel(res_ref, *refs):
-        total = refs[n][...] if last else jnp.zeros((tile, width), f32)
-        for i in range(n):
-            total += jnp.dot(
-                res_ref[:, i * block : (i + 1) * block],
-                refs[i][...],
-                preferred_element_type=f32,
-            )
-        refs[-1][...] = total.astype(refs[-1].dtype)
+        out_ref, grad_all = refs[-2:]
+
+        @pl.when(pl.program_id(0) == 0)
+        def _():
+            for i in range(n):
+                grad_all[i * block : (i + 1) * block] = refs[i][...]
+
+        total = jnp.dot(res_ref[...], grad_all[...], preferred_element_type=f32)
+        if last:
+            total += refs[n][...]
+        out_ref[...] = total.astype(out_ref.dtype)
 
     spec = pl.BlockSpec((tile, width), lambda i: (i, 0))
     return pl.pallas_call(
@@ -141,6 +195,7 @@
         + [spec] * last,
         out_specs=spec,
         out_shape=jax.ShapeDtypeStruct((feat, width), bf16 if last else f32),
+        scratch_shapes=[pltpu.VMEM((n * block, width), bf16)],
         name="encoder_grad",
     )(res_t, *grads, *([so_far] if last else []))
 
@@ -163,9 +218,16 @@
     def rows_of(start, count):
         return lax.dynamic_slice_in_dim(residual_rows, start, count, 0)
 
-    own_row = (y * N_XL + x) * block
-
     twin = (NEAR[2],) * 4
+
+    def sum_src(far_parts, near_parts):
+        near1, near3, sent, kept = near_parts
+        got = [move(part, FAR, slot, True) for slot, part in enumerate(far_parts)]
+        got += [move(near1, NEAR, 1, True), move(near3, NEAR, 3, True), move(sent, twin, 0, True)]
+        total = kept.astype(f32)
+        for part in got:
+            total = total + part.astype(f32)
+        return total
 
     def gather_src(shard):
         far = [move(shard, FAR, slot, False) for slot in (3, 2, 1, 0)][::-1]
@@ -174,31 +236,39 @@
         near = [jnp.where(first, shard, mate), near1, jnp.where(first, mate, shard), near3]
         return near, far
 
-    partial = dot(residual_rows, encoder).astype(bf16).reshape(N_SRC, block, -1)
-    partial = lax.all_to_all(partial, SRC, 0, 0)
-
-    squares = jnp.sum(jnp.square(decoder.astype(f32)), axis=1)
-    order = [owner_row(o, s) // block for o in (NEAR, FAR) for s in range(4)]
-    res_t = transpose(residual_rows, jnp.stack(order), block)
-    enc_bias, squares, res_t = lax.optimization_barrier((enc_bias, squares, res_t))
-
-    pre_act = jnp.broadcast_to(enc_bias[None, :], partial.shape[1:])
-    for i in range(N_SRC):
-        pre_act = pre_act + partial[i].astype(f32)
+    far_rows = [owner_row(FAR, slot) // block for slot in range(4)]
+    near_rows = [owner_row(NEAR, slot) // block for slot in range(4)]
+    own_row = (y * N_XL + x) * block
+    twin_row = owner_row(twin, 0)
+    far_parts = blocks_dot(
+        encoder, 0, [bf16] * 4, source=residual_rows, order=jnp.stack(far_rows)
+    )
+    near_parts = blocks_dot(
+        encoder,
+        0,
+        [bf16, bf16, bf16, f32],
+        source=residual_rows,
+        order=jnp.stack([near_rows[1], near_rows[3], twin_row // block, own_row // block]),
+    )
+    pre_act = sum_src(far_parts, near_parts) + enc_bias[None, :]
     latent = (jax.nn.softplus(SHARPNESS * pre_act) / SHARPNESS).astype(bf16)
     slope = jax.nn.sigmoid(SHARPNESS * pre_act)
 
     near, far = gather_src(latent)
 
     def core_sum(blocks):
-        theirs = dot(jnp.concatenate(blocks[2:], axis=0), decoder).astype(bf16)
-        theirs = swap(theirs, "core", N_CORE, 1)
+        sent = dot(jnp.concatenate(blocks[2:], axis=0), decoder).astype(bf16)
+        theirs = swap(sent, "core", N_CORE, 1)
         mine = dot(jnp.concatenate(blocks[:2], axis=0), decoder) + theirs.astype(f32)
-        return mine.astype(bf16)
+        return mine.astype(bf16), sent
 
     rows = 4 * block // N_RING
-    shares = jnp.concatenate([core_sum(near), core_sum(far)], axis=0)
-    squares, shares = lax.optimization_barrier((squares, shares))
+    near_sum, theirs_done = core_sum(near)
+    far_blocks = lax.optimization_barrier(tuple(far) + (theirs_done, near[1]))[:4]
+    far_sum, _ = core_sum(far_blocks)
+    shares = jnp.concatenate([near_sum, far_sum], axis=0)
+    weights, shares = lax.optimization_barrier((decoder, shares))
+    squares = jnp.sum(jnp.square(weights.astype(f32)), axis=1)
     shares = lax.all_to_all(shares.reshape(N_RING, rows, -1), RING, 0, 0)
 
     own_sq = squares + swap(squares, "xl", N_XL, 1)
@@ -216,30 +286,31 @@
     start = lax.dynamic_index_in_dim(starts, ring // per_block, 0, False)
     target = rows_of(start + (ring % per_block) * rows, rows)
     errors = (recon - target.astype(f32)).astype(bf16)
+    order = jnp.stack(near_rows + far_rows)
+    order, errors = lax.optimization_barrier((order, errors))
+    res_t = transpose(residual_rows, order, block)
     errors = jnp.broadcast_to(errors[None], (N_RING,) + errors.shape)
     mine = lax.all_to_all(errors, RING, 0, 0).reshape(4, block, -1)
+    mine, res_t = lax.optimization_barrier((mine, res_t))
     theirs = swap(mine, "core", N_CORE, 1)
     near_err = [mine[0], mine[1], theirs[0], theirs[1]]
     far_err = [mine[2], mine[3], theirs[2], theirs[3]]
 
-    got = []
-    for slot in range(2):
-        got.append(move(dot_t(far_err[slot], decoder).astype(bf16), FAR, slot, True))
-    got.append(move(dot_t(near_err[1], decoder).astype(bf16), NEAR, 1, True))
-    for slot in range(2, 4):
-        got.append(move(dot_t(far_err[slot], decoder).astype(bf16), FAR, slot, True))
-    got.append(move(dot_t(near_err[3], decoder).astype(bf16), NEAR, 3, True))
-    sent = jnp.where(first, near_err[2], near_err[0])
-    kept = jnp.where(first, near_err[0], near_err[2])
-    got.append(move(dot_t(sent, decoder).astype(bf16), twin, 0, True))
-    act_grad = dot_t(kept, decoder) + penalty[None, :]
-    for g in got:
-        act_grad = act_grad + g.astype(f32)
+    types = [bf16] * 4
+    far0, far1, near1, low = blocks_dot(
+        decoder, 1, types, blocks=[far_err[0], far_err[1], near_err[1], near_err[0]]
+    )
+    far2, far3, near3, high = blocks_dot(
+        decoder, 1, types, blocks=[far_err[2], far_err[3], near_err[3], near_err[2]]
+    )
+    sent, kept = jnp.where(first, high, low), jnp.where(first, low, high)
+    act_grad = sum_src([far0, far1, far2, far3], [near1, near3, sent, kept]) + penalty[None, :]
+    grad_decoder = decoder_grad(
+        near + far, near_err + far_err, decoder, jnp.stack([own_norm] * 8), loss_scale
+    )
+    slope, grad_decoder = lax.optimization_barrier((slope, grad_decoder))
     grad_pre = (loss_scale * act_grad * slope).astype(bf16)
     near_grad, far_grad = gather_src(grad_pre)
-
-    scale = jnp.stack([own_norm] * 8)
-    grad_decoder = decoder_grad(near + far, near_err + far_err, decoder, scale, loss_scale)
 
     grad_encoder = encoder_grad(res_t, near_grad, 0, None)
     grad_encoder = encoder_grad(res_t, far_grad, 1, grad_encoder)

time: 233 us -> 218 us (0.936)
  blocking collectives: 32.7 us -> 0 us
  starting transfers between devices: 44.9 us -> 67.3 us
  Pallas kernels: 27.2 us -> 45.6 us
  matrix products: 15.8 us -> 2.85 us
  waiting for transfers between devices: 93.7 us -> 83.5 us
    all_to_all x1 -> x0, blocking collectives: 32.7 us -> none  [per_device(): mine = lax.all_to_all(errors, RING, 0, 0).reshape(4, block, -1)]
    pallas_call x0 -> x4, Pallas kernels: none -> 20.4 us  [blocks_dot(): pl.pallas_call(kernel, grid_spec=pltpu.PrefetchScalarGridSpec(num_scalar_...]
    ppermute x21 -> x28, starting transfers between devices: 25.5 us -> 44.6 us  [move(): return lax.ppermute(value, ('y', 'xl', 'core'), pairs)]
    ppermute x21 -> x28, waiting for transfers between devices: 53 us -> 41.6 us  [move(): return lax.ppermute(value, ('y', 'xl', 'core'), pairs)]
    dot_general x8 -> x0, matrix products: 7.68 us -> none  [dot_t(): return jnp.einsum('bk,jk->bj', a, b, preferred_element_type=f32)]
    dot_general x5 -> x4, matrix products: 8.08 us -> 2.85 us  [dot(): return jnp.dot(a, b, preferred_element_type=f32)]
    all_to_all x1, waiting for transfers between devices: 17.6 us -> 21.1 us  [per_device(): mine = lax.all_to_all(errors, RING, 0, 0).reshape(4, block, -1)]
    ppermute x6, starting transfers between devices: 3.19 us -> 6.01 us  [swap(): return lax.ppermute(value, axis, [(i, i ^ mask) for i in range(size)])]
  transfers between devices with their start and end apart: 29 -> 36, of which waited for: 13 -> 21; matrix products, arithmetic and copies ran while one was open for 6% -> 4% of each run, Pallas kernels for 9% -> 16%
where the time goes in v4:
time: 218 us; the launch traced here: 217 us
  waiting for transfers between devices  83.5 us (38%)
  starting transfers between devices  67.3 us (31%)
  Pallas kernels  45.6 us (21%)
  other arithmetic  9.16 us (4%)
  local copies, waits for them, and re-layouts  6.43 us (3%)
  matrix products  2.85 us (1%)
    ppermute x28, starting transfers between devices, move(): return lax.ppermute(value, ('y', 'xl', 'core'), pairs)  44.6 us
    ppermute x28, waiting for transfers between devices, move(): return lax.ppermute(value, ('y', 'xl', 'core'), pairs)  41.6 us
    all_to_all x1, waiting for transfers between devices, per_device(): mine = lax.all_to_all(errors, RING, 0, 0).reshape(4, block, -1)  21.1 us
    pallas_call x4, Pallas kernels, blocks_dot(): pl.pallas_call(kernel, grid_spec=pltpu.PrefetchScalarGridSpec(num_scalar_...  20.4 us
    all_to_all x1, waiting for transfers between devices, per_device(): shares = lax.all_to_all(shares.reshape(N_RING, rows, -1), RING, 0, 0)  13.7 us
    all_to_all x1, starting transfers between devices, per_device(): shares = lax.all_to_all(shares.reshape(N_RING, rows, -1), RING, 0, 0)  11.3 us
    pallas_call x2, Pallas kernels, encoder_grad(): pl.pallas_call(kernel, grid=(feat // tile,), in_specs=[pl.BlockSpec((tile...  10.7 us
    pallas_call x1, Pallas kernels, decoder_grad(): pl.pallas_call(kernel, grid=(width // tile,), in_specs=[pl.BlockSpec((blo...  7.73 us
  transfers between devices with their start and end apart: 36, of which 21 were waited for; matrix products, arithmetic and copies ran while one was open for 4% of the time, Pallas kernels for 16%

profile of v4, /device:TPU:32, one launch (start us, length us, event | category | flops | bytes accessed | tf_op | source)
XLA Modules:
  0.0 216.6 jit_solution(13536775438395360082)
XLA Ops:
  1.4 5.4 %blocks_dot.5 = (bf16[128,1024]{1,0:T(8,128)(2,1)}, bf16[128,1024]{1,0:T(8,128)(2,1)}, bf16[128,1024]{1,0:T(8,128)(2,1)}, bf16[128,1024]{1,0:T(8,128)(2,1)}) custom-call(s32[4]{0:T(128)} %pad_add_fusion.1.order_ref, bf16[1024,1024]{1,0:T(8,128)(2,1)} %in_ref.1, bf16[1024,1024]{1,0:T(8,128)(2,1)} %in_ref.1, bf16[1024,1024]{1,0:T(8,128)(2,1)} %in_ref.1, ...), custom_call_target="tpu_custom_call" | custom-call | tf_op jit(solution)/shard_map/blocks_dot/pallas_call | solution.py:97
  6.8 3.2 %collective-permute-start = (bf16[128,1024]{1,0:T(8,128)(2,1)}, bf16[128,1024]{1,0:T(8,128)(2,1)S(1)}, u32[]{:S(2)}, u32[]{:S(2)}) collective-permute-start(bf16[128,1024]{1,0:T(8,128)(2,1)} %get-tuple-element.34), channel_id=1, source_target_pairs={{0,128},{1,97},{32,160},{33,65},{64,192},{65,161},{96,224},{97,129... | collective-permute-start | bytes 786440 | tf_op jit(solution)/shard_map/ppermute | solution.py:55
  10.0 2.0 collective-permute-start.1
  14.7 5.5 %blocks_dot.4 = (bf16[128,1024]{1,0:T(8,128)(2,1)}, bf16[128,1024]{1,0:T(8,128)(2,1)}, bf16[128,1024]{1,0:T(8,128)(2,1)}, f32[128,1024]{1,0:T(8,128)}) custom-call(s32[4]{0:T(128)} %pad_add_fusion.order_ref, bf16[1024,1024]{1,0:T(8,128)(2,1)} %in_ref.1, bf16[1024,1024]{1,0:T(8,128)(2,1)} %in_ref.1, bf16[1024,1024]{1,0:T(8,128)(2,1)} %in_ref.1, ...), custom_call_target="tpu_custom_call" | custom-call | tf_op jit(solution)/shard_map/blocks_dot/pallas_call | solution.py:97
  21.2 3.3 %collective-permute-done = bf16[128,1024]{1,0:T(8,128)(2,1)S(1)} collective-permute-done((bf16[128,1024]{1,0:T(8,128)(2,1)}, bf16[128,1024]{1,0:T(8,128)(2,1)S(1)}, u32[]{:S(2)}, u32[]{:S(2)}) %collective-permute-start) | collective-permute-done | bytes 262176 | tf_op jit(solution)/shard_map/ppermute | solution.py:55
  25.4 2.4 %collective-permute-start.6 = (bf16[128,1024]{1,0:T(8,128)(2,1)}, bf16[128,1024]{1,0:T(8,128)(2,1)S(1)}, u32[]{:S(2)}, u32[]{:S(2)}) collective-permute-start(bf16[128,1024]{1,0:T(8,128)(2,1)} %get-tuple-element.40), channel_id=1, source_target_pairs={{0,192},{1,193},{32,224},{33,225},{64,0},{65,1},{96,32},{97,33},{1... | collective-permute-start | bytes 786440 | tf_op jit(solution)/shard_map/ppermute | solution.py:55
  27.8 4.5 %collective-permute-done.3 = bf16[128,1024]{1,0:T(8,128)(2,1)S(1)} collective-permute-done((bf16[128,1024]{1,0:T(8,128)(2,1)}, bf16[128,1024]{1,0:T(8,128)(2,1)S(1)}, u32[]{:S(2)}, u32[]{:S(2)}) %collective-permute-start.3) | collective-permute-done | bytes 262176 | tf_op jit(solution)/shard_map/ppermute | solution.py:55
  34.9 2.4 %add_divide_fusion = (f32[128,1024]{1,0:T(8,128)}, f32[128,1024]{1,0:T(8,128)S(1)}) fusion(f32[1024]{0:T(1024)S(1)} %copy-done.18, bf16[128,1024]{1,0:T(8,128)(2,1)S(1)} %collective-permute-done.6, bf16[128,1024]{1,0:T(8,128)(2,1)S(1)} %collective-permute-done.5, bf16[128,1024]{1,0:T(8,128)(2,1)S(1)} %collective-permute-done.4, ...), kind=kLoop, calls=%fused_computation.24 | loop fusion | flops 2490368 | bytes 3411968 | tf_op jit(solution)/shard_map/div | solution.py:255
  42.3 2.5 %collective-permute-start.11 = (bf16[128,1024]{1,0:T(8,128)(2,1)S(1)}, bf16[128,1024]{1,0:T(8,128)(2,1)S(1)}, u32[]{:S(2)}, u32[]{:S(2)}) collective-permute-start(bf16[128,1024]{1,0:T(8,128)(2,1)S(1)} %fusion.2), channel_id=1, source_target_pairs={{128,0},{97,1},{160,32},{65,33},{192,64},{161,65},{224,96},{129,97... | collective-permute-start | bytes 786440 | tf_op jit(solution)/shard_map/ppermute | solution.py:55
  45.7 6.3 %collective-permute-done.7 = bf16[128,1024]{1,0:T(8,128)(2,1)S(1)} collective-permute-done((bf16[128,1024]{1,0:T(8,128)(2,1)S(1)}, bf16[128,1024]{1,0:T(8,128)(2,1)S(1)}, u32[]{:S(2)}, u32[]{:S(2)}) %collective-permute-start.7) | collective-permute-done | bytes 262176 | tf_op jit(solution)/shard_map/ppermute | solution.py:55
  54.1 2.0 collective-permute-start.13
  57.0 4.8 %collective-permute-done.11.refs_4_ = bf16[128,1024]{1,0:T(8,128)(2,1)S(1)} collective-permute-done((bf16[128,1024]{1,0:T(8,128)(2,1)S(1)}, bf16[128,1024]{1,0:T(8,128)(2,1)S(1)}, u32[]{:S(2)}, u32[]{:S(2)}) %collective-permute-start.11) | collective-permute-done | bytes 262176 | tf_op jit(solution)/shard_map/ppermute | solution.py:55
  61.8 2.8 %collective-permute-done.13.refs_6_ = bf16[128,1024]{1,0:T(8,128)(2,1)S(1)} collective-permute-done((bf16[128,1024]{1,0:T(8,128)(2,1)S(1)}, bf16[128,1024]{1,0:T(8,128)(2,1)S(1)}, u32[]{:S(2)}, u32[]{:S(2)}) %collective-permute-start.13) | collective-permute-done | bytes 262176 | tf_op jit(solution)/shard_map/ppermute | solution.py:55
  69.1 11.3 %all-to-all-start = ((bf16[16,32,1024]{2,1,0:T(8,128)(2,1)}), bf16[16,32,1024]{2,1,0:T(8,128)(2,1)S(1)}, u32[]{:S(2)}, u32[]{:S(2)}) async-start(bf16[16,32,1024]{2,1,0:T(8,128)(2,1)} %bitcast.117), calls=%async_computation | async-start | bytes 2097152 | tf_op jit(solution)/shard_map/all_to_all | solution.py:272
  81.6 3.1 %collective-permute-done.16 = f32[1024]{0:T(1024)S(1)} collective-permute-done((f32[1024]{0:T(1024)S(1)}, f32[1024]{0:T(1024)S(1)}, u32[]{:S(2)}, u32[]{:S(2)}) %collective-permute-start.16) | collective-permute-done | bytes 4128 | tf_op jit(solution)/shard_map/ppermute | solution.py:35
  84.7 3.2 %collective-permute-start.17 = (f32[1024]{0:T(1024)S(1)}, f32[1024]{0:T(1024)S(1)}, u32[]{:S(2)}, u32[]{:S(2)}) collective-permute-start(f32[1024]{0:T(1024)S(1)} %add.269), channel_id=1, source_target_pairs={{0,64},{64,0},{128,192},{192,128},{1,65},{65,1},{129,193},{193,129... | collective-permute-start | bytes 12296 | tf_op jit(solution)/shard_map/ppermute | solution.py:35
  94.7 13.7 %all-to-all-done = bf16[16,32,1024]{2,1,0:T(8,128)(2,1)S(1)} async-done(((bf16[16,32,1024]{2,1,0:T(8,128)(2,1)}), bf16[16,32,1024]{2,1,0:T(8,128)(2,1)S(1)}, u32[]{:S(2)}, u32[]{:S(2)}) %all-to-all-start) | async-done | bytes 1048608 | tf_op jit(solution)/shard_map/all_to_all | solution.py:272
  110.5 5.4 %all-to-all-start.1 = ((bf16[16,32,1024]{2,1,0:T(8,128)(2,1)}), bf16[16,32,1024]{2,1,0:T(8,128)(2,1)S(1)}, u32[]{:S(2)}, u32[]{:S(2)}) async-start(bf16[16,32,1024]{2,1,0:T(8,128)(2,1)} %broadcast_in_dim.5), calls=%async_computation.1 | async-start | bytes 2097152 | tf_op jit(solution)/shard_map/all_to_all | solution.py:293
  115.9 6.8 %transpose.21.res_ref = bf16[1024,1024]{1,0:T(8,128)(2,1)} custom-call(s32[8]{0:T(128)} %stack.79.order_ref, bf16[1024,1024]{1,0:T(8,128)(2,1)} %in_ref.1), custom_call_target="tpu_custom_call" | custom-call | tf_op jit(solution)/shard_map/transpose/pallas_call | solution.py:156
  122.7 21.1 %all-to-all-done.1 = bf16[16,32,1024]{2,1,0:T(8,128)(2,1)S(1)} async-done(((bf16[16,32,1024]{2,1,0:T(8,128)(2,1)}), bf16[16,32,1024]{2,1,0:T(8,128)(2,1)S(1)}, u32[]{:S(2)}, u32[]{:S(2)}) %all-to-all-start.1) | async-done | bytes 1048608 | tf_op jit(solution)/shard_map/all_to_all | solution.py:293
  144.8 4.7 %blocks_dot.6 = (bf16[128,1024]{1,0:T(8,128)(2,1)}, bf16[128,1024]{1,0:T(8,128)(2,1)}, bf16[128,1024]{1,0:T(8,128)(2,1)}, bf16[128,1024]{1,0:T(8,128)(2,1)}) custom-call(s32[1]{0:T(128)} %constant.215.clone.1.order_ref, bf16[128,1024]{1,0:T(8,128)(2,1)} %get-tuple-element.75.refs_0_.refs_12_, bf16[128,1024]{1,0:T(8,128)(2,1)} %get-tuple-element.72.refs_1_.refs_13_, ...), custom_call_target="tpu_custom_call" | custom-call | tf_op jit(solution)/shard_map/blocks_dot/pallas_call | solution.py:97
  149.5 3.3 %collective-permute-start.20 = (bf16[128,1024]{1,0:T(8,128)(2,1)}, bf16[128,1024]{1,0:T(8,128)(2,1)S(1)}, u32[]{:S(2)}, u32[]{:S(2)}) collective-permute-start(bf16[128,1024]{1,0:T(8,128)(2,1)} %get-tuple-element.54), channel_id=1, source_target_pairs={{0,128},{1,97},{32,160},{33,65},{64,192},{65,161},{96,224},{97,129... | collective-permute-start | bytes 786440 | tf_op jit(solution)/shard_map/ppermute | solution.py:55
  152.8 2.8 %collective-permute-start.21 = (bf16[128,1024]{1,0:T(8,128)(2,1)}, bf16[128,1024]{1,0:T(8,128)(2,1)S(1)}, u32[]{:S(2)}, u32[]{:S(2)}) collective-permute-start(bf16[128,1024]{1,0:T(8,128)(2,1)} %get-tuple-element.55), channel_id=1, source_target_pairs={{0,224},{1,161},{32,192},{33,129},{64,32},{65,225},{96,0},{97,193}... | collective-permute-start | bytes 786440 | tf_op jit(solution)/shard_map/ppermute | solution.py:55
  158.1 4.8 %blocks_dot.7 = (bf16[128,1024]{1,0:T(8,128)(2,1)}, bf16[128,1024]{1,0:T(8,128)(2,1)}, bf16[128,1024]{1,0:T(8,128)(2,1)}, bf16[128,1024]{1,0:T(8,128)(2,1)}) custom-call(s32[1]{0:T(128)} %constant.215.clone.1.order_ref, bf16[128,1024]{1,0:T(8,128)(2,1)} %get-tuple-element.71.refs_0_.refs_14_, bf16[128,1024]{1,0:T(8,128)(2,1)} %get-tuple-element.68.refs_1_.refs_15_, ...), custom_call_target="tpu_custom_call" | custom-call | tf_op jit(solution)/shard_map/blocks_dot/pallas_call | solution.py:97
  163.9 2.1 collective-permute-start.22
  166.0 2.6 %collective-permute-start.23 = (bf16[128,1024]{1,0:T(8,128)(2,1)}, bf16[128,1024]{1,0:T(8,128)(2,1)S(1)}, u32[]{:S(2)}, u32[]{:S(2)}) collective-permute-start(bf16[128,1024]{1,0:T(8,128)(2,1)} %get-tuple-element.57), channel_id=1, source_target_pairs={{0,160},{1,225},{32,128},{33,193},{64,224},{65,33},{96,192},{97,1}... | collective-permute-start | bytes 786440 | tf_op jit(solution)/shard_map/ppermute | solution.py:55
  169.8 7.7 %decoder_grad.1 = bf16[1024,1024]{1,0:T(8,128)(2,1)} custom-call(bf16[128,1024]{1,0:T(8,128)(2,1)} %copy-done.2, bf16[128,1024]{1,0:T(8,128)(2,1)} %copy-done.10, bf16[128,1024]{1,0:T(8,128)(2,1)} %copy-done.3, bf16[128,1024]{1,0:T(8,128)(2,1)} %copy-done.6, bf16[128,1024]{1,0:T(8,128)(2,1)} %copy-done.8, bf16[128,1024]{1,0:T(8,128)(2,1)} %copy-done.7, ...), custom_call_target="tpu_custom_call" | custom-call | tf_op jit(solution)/shard_map/decoder_grad/pallas_call | solution.py:134
  182.4 2.5 %collective-permute-start.33 = (bf16[128,1024]{1,0:T(8,128)(2,1)S(1)}, bf16[128,1024]{1,0:T(8,128)(2,1)S(1)}, u32[]{:S(2)}, u32[]{:S(2)}) collective-permute-start(bf16[128,1024]{1,0:T(8,128)(2,1)S(1)} %multiply_convert_fusion), channel_id=1, source_target_pairs={{64,0},{33,1},{96,32},{1,33},{128,64},{97,65},{160,96},{65,97},{19... | collective-permute-start | bytes 786440 | tf_op jit(solution)/shard_map/ppermute | solution.py:55
  191.1 9.5 %collective-permute-done.31 = bf16[128,1024]{1,0:T(8,128)(2,1)S(1)} collective-permute-done((bf16[128,1024]{1,0:T(8,128)(2,1)S(1)}, bf16[128,1024]{1,0:T(8,128)(2,1)S(1)}, u32[]{:S(2)}, u32[]{:S(2)}) %collective-permute-start.31) | collective-permute-done | bytes 262176 | tf_op jit(solution)/shard_map/ppermute | solution.py:55
  202.1 5.2 %encoder_grad.2.refs_4_ = f32[1024,1024]{1,0:T(8,128)} custom-call(bf16[1024,1024]{1,0:T(8,128)(2,1)} %transpose.21.res_ref, bf16[128,1024]{1,0:T(8,128)(2,1)} %get-tuple-element.77.refs_0_, bf16[128,1024]{1,0:T(8,128)(2,1)} %copy-done.14, bf16[128,1024]{1,0:T(8,128)(2,1)} %get-tuple-element.76.refs_2_, bf16[128,1024]{1,0:T(8,128)(2,1)} %copy-done.16), custom_call_target="tpu_custom_call" | custom-call | tf_op jit(solution)/shard_map/encoder_grad/pallas_call | solution.py:190
  207.5 2.8 %collective-permute-done.27.refs_0_ = bf16[128,1024]{1,0:T(8,128)(2,1)S(1)} collective-permute-done((bf16[128,1024]{1,0:T(8,128)(2,1)S(1)}, bf16[128,1024]{1,0:T(8,128)(2,1)S(1)}, u32[]{:S(2)}, u32[]{:S(2)}) %collective-permute-start.27) | collective-permute-done | bytes 262176 | tf_op jit(solution)/shard_map/ppermute | solution.py:55
  211.1 5.5 %encoder_grad.3 = bf16[1024,1024]{1,0:T(8,128)(2,1)} custom-call(bf16[1024,1024]{1,0:T(8,128)(2,1)} %transpose.21.res_ref, bf16[128,1024]{1,0:T(8,128)(2,1)} %copy-done.17, bf16[128,1024]{1,0:T(8,128)(2,1)} %copy-done.15, bf16[128,1024]{1,0:T(8,128)(2,1)} %copy-done.13, bf16[128,1024]{1,0:T(8,128)(2,1)} %copy-done.12, f32[1024,1024]{1,0:T(8,128)} %encoder_grad.2.refs_4_), custom_call_target="tpu_custom_call" | custom-call | tf_op jit(solution)/shard_map/encoder_grad/pallas_call | solution.py:190
  (113 shorter events, 49.7 us)
Async XLA Ops:
  6.8 17.8 %collective-permute-start = (bf16[128,1024]{1,0:T(8,128)(2,1)}, bf16[128,1024]{1,0:T(8,128)(2,1)S(1)}, u32[]{:S(2)}, u32[]{:S(2)}) collective-permute-start(bf16[128,1024]{1,0:T(8,128)(2,1)} %get-tuple-element.34), channel_id=1, source_target_pairs={{0,128},{1,97},{32,160},{33,65},{64,192},{65,161},{96,224},{97,129... | collective-permute-start | bytes 786440 | tf_op jit(solution)/shard_map/ppermute | solution.py:55
  10.0 15.4 %collective-permute-start.1 = (bf16[128,1024]{1,0:T(8,128)(2,1)}, bf16[128,1024]{1,0:T(8,128)(2,1)S(1)}, u32[]{:S(2)}, u32[]{:S(2)}) collective-permute-start(bf16[128,1024]{1,0:T(8,128)(2,1)} %get-tuple-element.35), channel_id=1, source_target_pairs={{0,224},{1,161},{32,192},{33,129},{64,32},{65,225},{96,0},{97,193}... | collective-permute-start | bytes 786440 | tf_op jit(solution)/shard_map/ppermute | solution.py:55
  11.9 15.8 %collective-permute-start.2 = (bf16[128,1024]{1,0:T(8,128)(2,1)}, bf16[128,1024]{1,0:T(8,128)(2,1)S(1)}, u32[]{:S(2)}, u32[]{:S(2)}) collective-permute-start(bf16[128,1024]{1,0:T(8,128)(2,1)} %get-tuple-element.36), channel_id=1, source_target_pairs={{0,96},{1,129},{32,64},{33,161},{64,160},{65,193},{96,128},{97,225... | collective-permute-start | bytes 786440 | tf_op jit(solution)/shard_map/ppermute | solution.py:55
  12.9 19.4 %collective-permute-start.3 = (bf16[128,1024]{1,0:T(8,128)(2,1)}, bf16[128,1024]{1,0:T(8,128)(2,1)S(1)}, u32[]{:S(2)}, u32[]{:S(2)}) collective-permute-start(bf16[128,1024]{1,0:T(8,128)(2,1)} %get-tuple-element.37), channel_id=1, source_target_pairs={{0,160},{1,225},{32,128},{33,193},{64,224},{65,33},{96,192},{97,1}... | collective-permute-start | bytes 786440 | tf_op jit(solution)/shard_map/ppermute | solution.py:55
  20.2 13.4 %collective-permute-start.4 = (bf16[128,1024]{1,0:T(8,128)(2,1)}, bf16[128,1024]{1,0:T(8,128)(2,1)S(1)}, u32[]{:S(2)}, u32[]{:S(2)}) collective-permute-start(bf16[128,1024]{1,0:T(8,128)(2,1)} %get-tuple-element.38), channel_id=1, source_target_pairs={{0,32},{1,65},{32,0},{33,97},{64,96},{65,129},{96,64},{97,161},{12... | collective-permute-start | bytes 786440 | tf_op jit(solution)/shard_map/ppermute | solution.py:55
  24.6 10.0 %collective-permute-start.5 = (bf16[128,1024]{1,0:T(8,128)(2,1)}, bf16[128,1024]{1,0:T(8,128)(2,1)S(1)}, u32[]{:S(2)}, u32[]{:S(2)}) collective-permute-start(bf16[128,1024]{1,0:T(8,128)(2,1)} %get-tuple-element.39), channel_id=1, source_target_pairs={{0,64},{1,33},{32,96},{33,1},{64,128},{65,97},{96,160},{97,65},{12... | collective-permute-start | bytes 786440 | tf_op jit(solution)/shard_map/ppermute | solution.py:55
  25.4 9.5 %collective-permute-start.6 = (bf16[128,1024]{1,0:T(8,128)(2,1)}, bf16[128,1024]{1,0:T(8,128)(2,1)S(1)}, u32[]{:S(2)}, u32[]{:S(2)}) collective-permute-start(bf16[128,1024]{1,0:T(8,128)(2,1)} %get-tuple-element.40), channel_id=1, source_target_pairs={{0,192},{1,193},{32,224},{33,225},{64,0},{65,1},{96,32},{97,33},{1... | collective-permute-start | bytes 786440 | tf_op jit(solution)/shard_map/ppermute | solution.py:55
  37.6 14.4 %collective-permute-start.7 = (bf16[128,1024]{1,0:T(8,128)(2,1)S(1)}, bf16[128,1024]{1,0:T(8,128)(2,1)S(1)}, u32[]{:S(2)}, u32[]{:S(2)}) collective-permute-start(bf16[128,1024]{1,0:T(8,128)(2,1)S(1)} %fusion.2), channel_id=1, source_target_pairs={{192,0},{193,1},{224,32},{225,33},{0,64},{1,65},{32,96},{33,97},{6... | collective-permute-start | bytes 786440 | tf_op jit(solution)/shard_map/ppermute | solution.py:55
  39.2 14.8 %collective-permute-start.9 = (bf16[128,1024]{1,0:T(8,128)(2,1)S(1)}, bf16[128,1024]{1,0:T(8,128)(2,1)S(1)}, u32[]{:S(2)}, u32[]{:S(2)}) collective-permute-start(bf16[128,1024]{1,0:T(8,128)(2,1)S(1)} %fusion.2), channel_id=1, source_target_pairs={{64,0},{33,1},{96,32},{1,33},{128,64},{97,65},{160,96},{65,97},{19... | collective-permute-start | bytes 786440 | tf_op jit(solution)/shard_map/ppermute | solution.py:55
  40.9 15.9 %collective-permute-start.12 = (bf16[128,1024]{1,0:T(8,128)(2,1)S(1)}, bf16[128,1024]{1,0:T(8,128)(2,1)S(1)}, u32[]{:S(2)}, u32[]{:S(2)}) collective-permute-start(bf16[128,1024]{1,0:T(8,128)(2,1)S(1)} %fusion.2), channel_id=1, source_target_pairs={{224,0},{161,1},{192,32},{129,33},{32,64},{225,65},{0,96},{193,97}... | collective-permute-start | bytes 786440 | tf_op jit(solution)/shard_map/ppermute | solution.py:55
  42.3 19.5 %collective-permute-start.11 = (bf16[128,1024]{1,0:T(8,128)(2,1)S(1)}, bf16[128,1024]{1,0:T(8,128)(2,1)S(1)}, u32[]{:S(2)}, u32[]{:S(2)}) collective-permute-start(bf16[128,1024]{1,0:T(8,128)(2,1)S(1)} %fusion.2), channel_id=1, source_target_pairs={{128,0},{97,1},{160,32},{65,33},{192,64},{161,65},{224,96},{129,97... | collective-permute-start | bytes 786440 | tf_op jit(solution)/shard_map/ppermute | solution.py:55
  44.7 17.0 %collective-permute-start.14 = (bf16[128,1024]{1,0:T(8,128)(2,1)S(1)}, bf16[128,1024]{1,0:T(8,128)(2,1)S(1)}, u32[]{:S(2)}, u32[]{:S(2)}) collective-permute-start(bf16[128,1024]{1,0:T(8,128)(2,1)S(1)} %fusion.2), channel_id=1, source_target_pairs={{160,0},{225,1},{128,32},{193,33},{224,64},{33,65},{192,96},{1,97}... | collective-permute-start | bytes 786440 | tf_op jit(solution)/shard_map/ppermute | solution.py:55
  52.0 9.7 %collective-permute-start.8 = (bf16[128,1024]{1,0:T(8,128)(2,1)S(1)}, bf16[128,1024]{1,0:T(8,128)(2,1)S(1)}, u32[]{:S(2)}, u32[]{:S(2)}) collective-permute-start(bf16[128,1024]{1,0:T(8,128)(2,1)S(1)} %fusion.2), channel_id=1, source_target_pairs={{32,0},{65,1},{0,32},{97,33},{96,64},{129,65},{64,96},{161,97},{16... | collective-permute-start | bytes 786440 | tf_op jit(solution)/shard_map/ppermute | solution.py:55
  54.1 10.5 %collective-permute-start.13 = (bf16[128,1024]{1,0:T(8,128)(2,1)S(1)}, bf16[128,1024]{1,0:T(8,128)(2,1)S(1)}, u32[]{:S(2)}, u32[]{:S(2)}) collective-permute-start(bf16[128,1024]{1,0:T(8,128)(2,1)S(1)} %fusion.2), channel_id=1, source_target_pairs={{96,0},{129,1},{64,32},{161,33},{160,64},{193,65},{128,96},{225,97... | collective-permute-start | bytes 786440 | tf_op jit(solution)/shard_map/ppermute | solution.py:55
  56.9 8.6 %collective-permute-start.10 = (bf16[256,1024]{1,0:T(8,128)(2,1)S(1)}, bf16[256,1024]{1,0:T(8,128)(2,1)S(1)}, u32[]{:S(2)}, u32[]{:S(2)}) collective-permute-start(bf16[256,1024]{1,0:T(8,128)(2,1)S(1)} %convolution_convert_fusion.1), channel_id=1, source_target_pairs={{0,1},{1,0},{2,3},{3,2},{4,5},{5,4},{6,7},{7,6},{8,9},{9,8},{10,11... | collective-permute-start | bytes 1572872 | tf_op jit(solution)/shard_map/ppermute | solution.py:35
  69.1 39.2 %all-to-all-start = ((bf16[16,32,1024]{2,1,0:T(8,128)(2,1)}), bf16[16,32,1024]{2,1,0:T(8,128)(2,1)S(1)}, u32[]{:S(2)}, u32[]{:S(2)}) async-start(bf16[16,32,1024]{2,1,0:T(8,128)(2,1)} %bitcast.117), calls=%async_computation | async-start | bytes 2097152 | tf_op jit(solution)/shard_map/all_to_all | solution.py:272
  110.5 33.3 %all-to-all-start.1 = ((bf16[16,32,1024]{2,1,0:T(8,128)(2,1)}), bf16[16,32,1024]{2,1,0:T(8,128)(2,1)S(1)}, u32[]{:S(2)}, u32[]{:S(2)}) async-start(bf16[16,32,1024]{2,1,0:T(8,128)(2,1)} %broadcast_in_dim.5), calls=%async_computation.1 | async-start | bytes 2097152 | tf_op jit(solution)/shard_map/all_to_all | solution.py:293
  143.7 13.3 %collective-permute-start.19 = (bf16[4,128,1024]{2,1,0:T(8,128)(2,1)S(1)}, bf16[4,128,1024]{2,1,0:T(8,128)(2,1)S(1)}, u32[]{:S(2)}, u32[]{:S(2)}) collective-permute-start(bf16[4,128,1024]{2,1,0:T(8,128)(2,1)S(1)} %bitcast.118), channel_id=1, source_target_pairs={{0,1},{1,0},{2,3},{3,2},{4,5},{5,4},{6,7},{7,6},{8,9},{9,8},{10,11... | collective-permute-start | bytes 3145736 | tf_op jit(solution)/shard_map/ppermute | solution.py:35
  149.5 16.5 %collective-permute-start.20 = (bf16[128,1024]{1,0:T(8,128)(2,1)}, bf16[128,1024]{1,0:T(8,128)(2,1)S(1)}, u32[]{:S(2)}, u32[]{:S(2)}) collective-permute-start(bf16[128,1024]{1,0:T(8,128)(2,1)} %get-tuple-element.54), channel_id=1, source_target_pairs={{0,128},{1,97},{32,160},{33,65},{64,192},{65,161},{96,224},{97,129... | collective-permute-start | bytes 786440 | tf_op jit(solution)/shard_map/ppermute | solution.py:55
  152.8 15.8 %collective-permute-start.21 = (bf16[128,1024]{1,0:T(8,128)(2,1)}, bf16[128,1024]{1,0:T(8,128)(2,1)S(1)}, u32[]{:S(2)}, u32[]{:S(2)}) collective-permute-start(bf16[128,1024]{1,0:T(8,128)(2,1)} %get-tuple-element.55), channel_id=1, source_target_pairs={{0,224},{1,161},{32,192},{33,129},{64,32},{65,225},{96,0},{97,193}... | collective-permute-start | bytes 786440 | tf_op jit(solution)/shard_map/ppermute | solution.py:55
  155.6 22.0 %collective-permute-start.24 = (bf16[128,1024]{1,0:T(8,128)(2,1)}, bf16[128,1024]{1,0:T(8,128)(2,1)S(1)}, u32[]{:S(2)}, u32[]{:S(2)}) collective-permute-start(bf16[128,1024]{1,0:T(8,128)(2,1)} %get-tuple-element.58), channel_id=1, source_target_pairs={{0,32},{1,65},{32,0},{33,97},{64,96},{65,129},{96,64},{97,161},{12... | collective-permute-start | bytes 786440 | tf_op jit(solution)/shard_map/ppermute | solution.py:55
  163.8 14.3 %collective-permute-start.26 = (bf16[128,1024]{1,0:T(8,128)(2,1)S(1)}, bf16[128,1024]{1,0:T(8,128)(2,1)S(1)}, u32[]{:S(2)}, u32[]{:S(2)}) collective-permute-start(bf16[128,1024]{1,0:T(8,128)(2,1)S(1)} %broadcast_select_fusion.2), channel_id=1, source_target_pairs={{0,192},{1,193},{32,224},{33,225},{64,0},{65,1},{96,32},{97,33},{1... | collective-permute-start | bytes 786440 | tf_op jit(solution)/shard_map/ppermute | solution.py:55
  163.9 14.2 %collective-permute-start.22 = (bf16[128,1024]{1,0:T(8,128)(2,1)}, bf16[128,1024]{1,0:T(8,128)(2,1)S(1)}, u32[]{:S(2)}, u32[]{:S(2)}) collective-permute-start(bf16[128,1024]{1,0:T(8,128)(2,1)} %get-tuple-element.56), channel_id=1, source_target_pairs={{0,96},{1,129},{32,64},{33,161},{64,160},{65,193},{96,128},{97,225... | collective-permute-start | bytes 786440 | tf_op jit(solution)/shard_map/ppermute | solution.py:55
  166.0 13.8 %collective-permute-start.23 = (bf16[128,1024]{1,0:T(8,128)(2,1)}, bf16[128,1024]{1,0:T(8,128)(2,1)S(1)}, u32[]{:S(2)}, u32[]{:S(2)}) collective-permute-start(bf16[128,1024]{1,0:T(8,128)(2,1)} %get-tuple-element.57), channel_id=1, source_target_pairs={{0,160},{1,225},{32,128},{33,193},{64,224},{65,33},{96,192},{97,1}... | collective-permute-start | bytes 786440 | tf_op jit(solution)/shard_map/ppermute | solution.py:55
  168.6 11.7 %collective-permute-start.25 = (bf16[128,1024]{1,0:T(8,128)(2,1)}, bf16[128,1024]{1,0:T(8,128)(2,1)S(1)}, u32[]{:S(2)}, u32[]{:S(2)}) collective-permute-start(bf16[128,1024]{1,0:T(8,128)(2,1)} %get-tuple-element.59), channel_id=1, source_target_pairs={{0,64},{1,33},{32,96},{33,1},{64,128},{65,97},{96,160},{97,65},{12... | collective-permute-start | bytes 786440 | tf_op jit(solution)/shard_map/ppermute | solution.py:55
  180.7 9.3 %collective-permute-start.32 = (bf16[128,1024]{1,0:T(8,128)(2,1)S(1)}, bf16[128,1024]{1,0:T(8,128)(2,1)S(1)}, u32[]{:S(2)}, u32[]{:S(2)}) collective-permute-start(bf16[128,1024]{1,0:T(8,128)(2,1)S(1)} %multiply_convert_fusion), channel_id=1, source_target_pairs={{32,0},{65,1},{0,32},{97,33},{96,64},{129,65},{64,96},{161,97},{16... | collective-permute-start | bytes 786440 | tf_op jit(solution)/shard_map/ppermute | solution.py:55
  181.7 18.9 %collective-permute-start.31 = (bf16[128,1024]{1,0:T(8,128)(2,1)S(1)}, bf16[128,1024]{1,0:T(8,128)(2,1)S(1)}, u32[]{:S(2)}, u32[]{:S(2)}) collective-permute-start(bf16[128,1024]{1,0:T(8,128)(2,1)S(1)} %multiply_convert_fusion), channel_id=1, source_target_pairs={{192,0},{193,1},{224,32},{225,33},{0,64},{1,65},{32,96},{33,97},{6... | collective-permute-start | bytes 786440 | tf_op jit(solution)/shard_map/ppermute | solution.py:55
  182.4 19.0 %collective-permute-start.33 = (bf16[128,1024]{1,0:T(8,128)(2,1)S(1)}, bf16[128,1024]{1,0:T(8,128)(2,1)S(1)}, u32[]{:S(2)}, u32[]{:S(2)}) collective-permute-start(bf16[128,1024]{1,0:T(8,128)(2,1)S(1)} %multiply_convert_fusion), channel_id=1, source_target_pairs={{64,0},{33,1},{96,32},{1,33},{128,64},{97,65},{160,96},{65,97},{19... | collective-permute-start | bytes 786440 | tf_op jit(solution)/shard_map/ppermute | solution.py:55
  184.9 22.4 %collective-permute-start.30 = (bf16[128,1024]{1,0:T(8,128)(2,1)S(1)}, bf16[128,1024]{1,0:T(8,128)(2,1)S(1)}, u32[]{:S(2)}, u32[]{:S(2)}) collective-permute-start(bf16[128,1024]{1,0:T(8,128)(2,1)S(1)} %multiply_convert_fusion), channel_id=1, source_target_pairs={{160,0},{225,1},{128,32},{193,33},{224,64},{33,65},{192,96},{1,97}... | collective-permute-start | bytes 786440 | tf_op jit(solution)/shard_map/ppermute | solution.py:55
  186.2 21.1 %collective-permute-start.29 = (bf16[128,1024]{1,0:T(8,128)(2,1)S(1)}, bf16[128,1024]{1,0:T(8,128)(2,1)S(1)}, u32[]{:S(2)}, u32[]{:S(2)}) collective-permute-start(bf16[128,1024]{1,0:T(8,128)(2,1)S(1)} %multiply_convert_fusion), channel_id=1, source_target_pairs={{96,0},{129,1},{64,32},{161,33},{160,64},{193,65},{128,96},{225,97... | collective-permute-start | bytes 786440 | tf_op jit(solution)/shard_map/ppermute | solution.py:55
  190.0 17.5 %collective-permute-start.28 = (bf16[128,1024]{1,0:T(8,128)(2,1)S(1)}, bf16[128,1024]{1,0:T(8,128)(2,1)S(1)}, u32[]{:S(2)}, u32[]{:S(2)}) collective-permute-start(bf16[128,1024]{1,0:T(8,128)(2,1)S(1)} %multiply_convert_fusion), channel_id=1, source_target_pairs={{224,0},{161,1},{192,32},{129,33},{32,64},{225,65},{0,96},{193,97}... | collective-permute-start | bytes 786440 | tf_op jit(solution)/shard_map/ppermute | solution.py:55
  200.6 9.8 %collective-permute-start.27 = (bf16[128,1024]{1,0:T(8,128)(2,1)S(1)}, bf16[128,1024]{1,0:T(8,128)(2,1)S(1)}, u32[]{:S(2)}, u32[]{:S(2)}) collective-permute-start(bf16[128,1024]{1,0:T(8,128)(2,1)S(1)} %multiply_convert_fusion), channel_id=1, source_target_pairs={{128,0},{97,1},{160,32},{65,33},{192,64},{161,65},{224,96},{129,97... | collective-permute-start | bytes 786440 | tf_op jit(solution)/shard_map/ppermute | solution.py:55
  (24 other events, 203.5 us)

commit v5 on v4

--- a/solution.py
+++ b/solution.py
@@ -219,6 +219,7 @@
         return lax.dynamic_slice_in_dim(residual_rows, start, count, 0)
 
     twin = (NEAR[2],) * 4
+    own_row = (y * N_XL + x) * block
 
     def sum_src(far_parts, near_parts):
         near1, near3, sent, kept = near_parts
@@ -229,16 +230,22 @@
             total = total + part.astype(f32)
         return total
 
-    def gather_src(shard):
-        far = [move(shard, FAR, slot, False) for slot in (3, 2, 1, 0)][::-1]
+    def gather_src(shard, work=None, seed=None):
         near3, near1 = (move(shard, NEAR, slot, False) for slot in (3, 1))
         mate = move(shard, twin, 0, False)
+        late, done = shard, None
+        if work is not None:
+            near1, seed = lax.optimization_barrier((near1, seed))
+            done = work(seed)
+            late, done = lax.optimization_barrier((shard, done))
+        far = [
+            move(late if slot > 1 else shard, FAR, slot, False) for slot in (3, 2, 1, 0)
+        ][::-1]
         near = [jnp.where(first, shard, mate), near1, jnp.where(first, mate, shard), near3]
-        return near, far
+        return near, far, done
 
     far_rows = [owner_row(FAR, slot) // block for slot in range(4)]
     near_rows = [owner_row(NEAR, slot) // block for slot in range(4)]
-    own_row = (y * N_XL + x) * block
     twin_row = owner_row(twin, 0)
     far_parts = blocks_dot(
         encoder, 0, [bf16] * 4, source=residual_rows, order=jnp.stack(far_rows)
@@ -254,7 +261,7 @@
     latent = (jax.nn.softplus(SHARPNESS * pre_act) / SHARPNESS).astype(bf16)
     slope = jax.nn.sigmoid(SHARPNESS * pre_act)
 
-    near, far = gather_src(latent)
+    near, far, _ = gather_src(latent)
 
     def core_sum(blocks):
         sent = dot(jnp.concatenate(blocks[2:], axis=0), decoder).astype(bf16)
@@ -296,21 +303,24 @@
     near_err = [mine[0], mine[1], theirs[0], theirs[1]]
     far_err = [mine[2], mine[3], theirs[2], theirs[3]]
 
-    types = [bf16] * 4
-    far0, far1, near1, low = blocks_dot(
-        decoder, 1, types, blocks=[far_err[0], far_err[1], near_err[1], near_err[0]]
-    )
-    far2, far3, near3, high = blocks_dot(
-        decoder, 1, types, blocks=[far_err[2], far_err[3], near_err[3], near_err[2]]
+    far0, far1, near1 = (
+        dot_t(e, decoder).astype(bf16) for e in (far_err[0], far_err[1], near_err[1])
+    )
+    far2, far3, near3, high, low = blocks_dot(
+        decoder,
+        1,
+        [bf16] * 5,
+        blocks=[far_err[2], far_err[3], near_err[3], near_err[2], near_err[0]],
     )
     sent, kept = jnp.where(first, high, low), jnp.where(first, low, high)
     act_grad = sum_src([far0, far1, far2, far3], [near1, near3, sent, kept]) + penalty[None, :]
-    grad_decoder = decoder_grad(
-        near + far, near_err + far_err, decoder, jnp.stack([own_norm] * 8), loss_scale
-    )
-    slope, grad_decoder = lax.optimization_barrier((slope, grad_decoder))
     grad_pre = (loss_scale * act_grad * slope).astype(bf16)
-    near_grad, far_grad = gather_src(grad_pre)
+    def work(norms):
+        return decoder_grad(
+            near + far, near_err + far_err, decoder, jnp.stack([norms] * 8), loss_scale
+        )
+
+    near_grad, far_grad, grad_decoder = gather_src(grad_pre, work, own_norm)
 
     grad_encoder = encoder_grad(res_t, near_grad, 0, None)
     grad_encoder = encoder_grad(res_t, far_grad, 1, grad_encoder)

time: 218 us -> 224 us (1.028)
  the two profiles are of different devices: /device:TPU:32 before, /device:TPU:44 now
where the time goes in v5:
time: 224 us; the launch traced here: 223 us
  waiting for transfers between devices  78.8 us (35%)
  starting transfers between devices  76.9 us (34%)
  Pallas kernels  41.2 us (18%)
  other arithmetic  9.98 us (4%)
  local copies, waits for them, and re-layouts  7.43 us (3%)
  matrix products  6.76 us (3%)
    ppermute x28, starting transfers between devices, move(): return lax.ppermute(value, ('y', 'xl', 'core'), pairs)  56.5 us
    ppermute x28, waiting for transfers between devices, move(): return lax.ppermute(value, ('y', 'xl', 'core'), pairs)  36.6 us
    all_to_all x1, waiting for transfers between devices, per_device(): mine = lax.all_to_all(errors, RING, 0, 0).reshape(4, block, -1)  19.6 us
    pallas_call x3, Pallas kernels, blocks_dot(): pl.pallas_call(kernel, grid_spec=pltpu.PrefetchScalarGridSpec(num_scalar_...  16 us
    all_to_all x1, waiting for transfers between devices, per_device(): shares = lax.all_to_all(shares.reshape(N_RING, rows, -1), RING, 0, 0)  13.2 us
    all_to_all x1, starting transfers between devices, per_device(): shares = lax.all_to_all(shares.reshape(N_RING, rows, -1), RING, 0, 0)  11.1 us
    pallas_call x2, Pallas kernels, encoder_grad(): pl.pallas_call(kernel, grid=(feat // tile,), in_specs=[pl.BlockSpec((tile...  10.7 us
    ppermute x6, waiting for transfers between devices, swap(): return lax.ppermute(value, axis, [(i, i ^ mask) for i in range(size)])  9.42 us
  transfers between devices with their start and end apart: 36, of which 17 were waited for; matrix products, arithmetic and copies ran while one was open for 6% of the time, Pallas kernels for 14%

profile of v5, /device:TPU:44, one launch (start us, length us, event | category | flops | bytes accessed | tf_op | source)
XLA Modules:
  0.0 222.9 jit_solution(4749272363392124789)
XLA Ops:
  1.4 5.4 %blocks_dot.4 = (bf16[128,1024]{1,0:T(8,128)(2,1)}, bf16[128,1024]{1,0:T(8,128)(2,1)}, bf16[128,1024]{1,0:T(8,128)(2,1)}, bf16[128,1024]{1,0:T(8,128)(2,1)}) custom-call(s32[4]{0:T(128)} %pad_add_fusion.1.order_ref, bf16[1024,1024]{1,0:T(8,128)(2,1)} %in_ref.1, bf16[1024,1024]{1,0:T(8,128)(2,1)} %in_ref.1, bf16[1024,1024]{1,0:T(8,128)(2,1)} %in_ref.1, ...), custom_call_target="tpu_custom_call" | custom-call | tf_op jit(solution)/shard_map/blocks_dot/pallas_call | solution.py:97
  6.8 2.3 %collective-permute-start = (bf16[128,1024]{1,0:T(8,128)(2,1)}, bf16[128,1024]{1,0:T(8,128)(2,1)S(1)}, u32[]{:S(2)}, u32[]{:S(2)}) collective-permute-start(bf16[128,1024]{1,0:T(8,128)(2,1)} %get-tuple-element.33), channel_id=1, source_target_pairs={{0,128},{1,97},{32,160},{33,65},{64,192},{65,161},{96,224},{97,129... | collective-permute-start | bytes 786440 | tf_op jit(solution)/shard_map/ppermute | solution.py:55
  12.0 3.1 %collective-permute-start.3 = (bf16[128,1024]{1,0:T(8,128)(2,1)}, bf16[128,1024]{1,0:T(8,128)(2,1)S(1)}, u32[]{:S(2)}, u32[]{:S(2)}) collective-permute-start(bf16[128,1024]{1,0:T(8,128)(2,1)} %get-tuple-element.36), channel_id=1, source_target_pairs={{0,160},{1,225},{32,128},{33,193},{64,224},{65,33},{96,192},{97,1}... | collective-permute-start | bytes 786440 | tf_op jit(solution)/shard_map/ppermute | solution.py:55
  15.7 5.5 %blocks_dot.3 = (bf16[128,1024]{1,0:T(8,128)(2,1)}, bf16[128,1024]{1,0:T(8,128)(2,1)}, bf16[128,1024]{1,0:T(8,128)(2,1)}, f32[128,1024]{1,0:T(8,128)}) custom-call(s32[4]{0:T(128)} %pad_add_fusion.order_ref, bf16[1024,1024]{1,0:T(8,128)(2,1)} %in_ref.1, bf16[1024,1024]{1,0:T(8,128)(2,1)} %in_ref.1, bf16[1024,1024]{1,0:T(8,128)(2,1)} %in_ref.1, ...), custom_call_target="tpu_custom_call" | custom-call | tf_op jit(solution)/shard_map/blocks_dot/pallas_call | solution.py:97
  22.1 2.4 %collective-permute-done = bf16[128,1024]{1,0:T(8,128)(2,1)S(1)} collective-permute-done((bf16[128,1024]{1,0:T(8,128)(2,1)}, bf16[128,1024]{1,0:T(8,128)(2,1)S(1)}, u32[]{:S(2)}, u32[]{:S(2)}) %collective-permute-start) | collective-permute-done | bytes 262176 | tf_op jit(solution)/shard_map/ppermute | solution.py:55
  26.5 3.3 %collective-permute-done.3 = bf16[128,1024]{1,0:T(8,128)(2,1)S(1)} collective-permute-done((bf16[128,1024]{1,0:T(8,128)(2,1)}, bf16[128,1024]{1,0:T(8,128)(2,1)S(1)}, u32[]{:S(2)}, u32[]{:S(2)}) %collective-permute-start.3) | collective-permute-done | bytes 262176 | tf_op jit(solution)/shard_map/ppermute | solution.py:55
  29.8 3.1 %collective-permute-done.4 = bf16[128,1024]{1,0:T(8,128)(2,1)S(1)} collective-permute-done((bf16[128,1024]{1,0:T(8,128)(2,1)}, bf16[128,1024]{1,0:T(8,128)(2,1)S(1)}, u32[]{:S(2)}, u32[]{:S(2)}) %collective-permute-start.4) | collective-permute-done | bytes 262176 | tf_op jit(solution)/shard_map/ppermute | solution.py:55
  35.0 2.6 %fusion.2 = (bf16[128,1024]{1,0:T(8,128)(2,1)S(1)}, f32[128,1024]{1,0:T(8,128)}) fusion(f32[1024]{0:T(1024)S(1)} %copy-done.16, bf16[128,1024]{1,0:T(8,128)(2,1)S(1)} %collective-permute-done.6, bf16[128,1024]{1,0:T(8,128)(2,1)S(1)} %collective-permute-done.5, bf16[128,1024]{1,0:T(8,128)(2,1)S(1)} %collective-permute-done.4, ...), kind=kLoop, calls=%fused_computation.12 | loop fusion | flops 3145728 | bytes 3149824 | tf_op jit(solution)/shard_map/convert_element_type | solution.py:261
  39.6 2.3 %collective-permute-start.13 = (bf16[128,1024]{1,0:T(8,128)(2,1)S(1)}, bf16[128,1024]{1,0:T(8,128)(2,1)S(1)}, u32[]{:S(2)}, u32[]{:S(2)}) collective-permute-start(bf16[128,1024]{1,0:T(8,128)(2,1)S(1)} %get-tuple-element.64), channel_id=1, source_target_pairs={{96,0},{129,1},{64,32},{161,33},{160,64},{193,65},{128,96},{225,97... | collective-permute-start | bytes 786440 | tf_op jit(solution)/shard_map/ppermute | solution.py:55
  42.5 3.1 %collective-permute-start.11 = (bf16[128,1024]{1,0:T(8,128)(2,1)S(1)}, bf16[128,1024]{1,0:T(8,128)(2,1)S(1)}, u32[]{:S(2)}, u32[]{:S(2)}) collective-permute-start(bf16[128,1024]{1,0:T(8,128)(2,1)S(1)} %get-tuple-element.64), channel_id=1, source_target_pairs={{128,0},{97,1},{160,32},{65,33},{192,64},{161,65},{224,96},{129,97... | collective-permute-start | bytes 786440 | tf_op jit(solution)/shard_map/ppermute | solution.py:55
  45.5 3.0 %collective-permute-done.7 = bf16[128,1024]{1,0:T(8,128)(2,1)S(1)} collective-permute-done((bf16[128,1024]{1,0:T(8,128)(2,1)S(1)}, bf16[128,1024]{1,0:T(8,128)(2,1)S(1)}, u32[]{:S(2)}, u32[]{:S(2)}) %collective-permute-start.7) | collective-permute-done | bytes 262176 | tf_op jit(solution)/shard_map/ppermute | solution.py:55
  48.5 3.7 %collective-permute-start.14 = (bf16[128,1024]{1,0:T(8,128)(2,1)S(1)}, bf16[128,1024]{1,0:T(8,128)(2,1)S(1)}, u32[]{:S(2)}, u32[]{:S(2)}) collective-permute-start(bf16[128,1024]{1,0:T(8,128)(2,1)S(1)} %get-tuple-element.64), channel_id=1, source_target_pairs={{160,0},{225,1},{128,32},{193,33},{224,64},{33,65},{192,96},{1,97}... | collective-permute-start | bytes 786440 | tf_op jit(solution)/shard_map/ppermute | solution.py:55
  52.3 6.6 %collective-permute-done.9.refs_3_ = bf16[128,1024]{1,0:T(8,128)(2,1)S(1)} collective-permute-done((bf16[128,1024]{1,0:T(8,128)(2,1)S(1)}, bf16[128,1024]{1,0:T(8,128)(2,1)S(1)}, u32[]{:S(2)}, u32[]{:S(2)}) %collective-permute-start.9) | collective-permute-done | bytes 262176 | tf_op jit(solution)/shard_map/ppermute | solution.py:55
  58.9 3.3 %collective-permute-start.8 = (bf16[128,1024]{1,0:T(8,128)(2,1)S(1)}, bf16[128,1024]{1,0:T(8,128)(2,1)S(1)}, u32[]{:S(2)}, u32[]{:S(2)}) collective-permute-start(bf16[128,1024]{1,0:T(8,128)(2,1)S(1)} %get-tuple-element.64), channel_id=1, source_target_pairs={{32,0},{65,1},{0,32},{97,33},{96,64},{129,65},{64,96},{161,97},{16... | collective-permute-start | bytes 786440 | tf_op jit(solution)/shard_map/ppermute | solution.py:55
  71.1 11.1 %all-to-all-start = ((bf16[16,32,1024]{2,1,0:T(8,128)(2,1)}), bf16[16,32,1024]{2,1,0:T(8,128)(2,1)S(1)}, u32[]{:S(2)}, u32[]{:S(2)}) async-start(bf16[16,32,1024]{2,1,0:T(8,128)(2,1)} %bitcast.128), calls=%async_computation | async-start | bytes 2097152 | tf_op jit(solution)/shard_map/all_to_all | solution.py:279
  86.7 3.6 %collective-permute-done.17 = f32[1024]{0:T(1024)S(1)} collective-permute-done((f32[1024]{0:T(1024)S(1)}, f32[1024]{0:T(1024)S(1)}, u32[]{:S(2)}, u32[]{:S(2)}) %collective-permute-start.17) | collective-permute-done | bytes 4128 | tf_op jit(solution)/shard_map/ppermute | solution.py:35
  92.7 2.8 %collective-permute-done.18 = f32[1024]{0:T(1024)S(1)} collective-permute-done((f32[1024]{0:T(1024)S(1)}, f32[1024]{0:T(1024)S(1)}, u32[]{:S(2)}, u32[]{:S(2)}) %collective-permute-start.18) | collective-permute-done | bytes 4128 | tf_op jit(solution)/shard_map/ppermute | solution.py:35
  95.5 13.2 %all-to-all-done = bf16[16,32,1024]{2,1,0:T(8,128)(2,1)S(1)} async-done(((bf16[16,32,1024]{2,1,0:T(8,128)(2,1)}), bf16[16,32,1024]{2,1,0:T(8,128)(2,1)S(1)}, u32[]{:S(2)}, u32[]{:S(2)}) %all-to-all-start) | async-done | bytes 1048608 | tf_op jit(solution)/shard_map/all_to_all | solution.py:279
  110.9 6.8 %all-to-all-start.1 = ((bf16[16,32,1024]{2,1,0:T(8,128)(2,1)}), bf16[16,32,1024]{2,1,0:T(8,128)(2,1)S(1)}, u32[]{:S(2)}, u32[]{:S(2)}) async-start(bf16[16,32,1024]{2,1,0:T(8,128)(2,1)} %broadcast_in_dim.5), calls=%async_computation.1 | async-start | bytes 2097152 | tf_op jit(solution)/shard_map/all_to_all | solution.py:300
  117.7 6.8 %transpose.21.res_ref = bf16[1024,1024]{1,0:T(8,128)(2,1)} custom-call(s32[8]{0:T(128)} %stack.79.order_ref, bf16[1024,1024]{1,0:T(8,128)(2,1)} %in_ref.1), custom_call_target="tpu_custom_call" | custom-call | tf_op jit(solution)/shard_map/transpose/pallas_call | solution.py:156
  124.5 19.6 %all-to-all-done.1 = bf16[16,32,1024]{2,1,0:T(8,128)(2,1)S(1)} async-done(((bf16[16,32,1024]{2,1,0:T(8,128)(2,1)}), bf16[16,32,1024]{2,1,0:T(8,128)(2,1)S(1)}, u32[]{:S(2)}, u32[]{:S(2)}) %all-to-all-start.1) | async-done | bytes 1048608 | tf_op jit(solution)/shard_map/all_to_all | solution.py:300
  152.4 5.0 %blocks_dot.5 = (bf16[128,1024]{1,0:T(8,128)(2,1)}, bf16[128,1024]{1,0:T(8,128)(2,1)}, bf16[128,1024]{1,0:T(8,128)(2,1)}, bf16[128,1024]{1,0:T(8,128)(2,1)}, bf16[128,1024]{1,0:T(8,128)(2,1)}) custom-call(s32[1]{0:T(128)} %constant.215.clone.1.order_ref, bf16[128,1024]{1,0:T(8,128)(2,1)} %get-tuple-element.73.refs_0_.refs_14_, ...), custom_call_target="tpu_custom_call" | custom-call | tf_op jit(solution)/shard_map/blocks_dot/pallas_call | solution.py:97
  158.5 4.1 %collective-permute-start.26 = (bf16[128,1024]{1,0:T(8,128)(2,1)S(1)}, bf16[128,1024]{1,0:T(8,128)(2,1)S(1)}, u32[]{:S(2)}, u32[]{:S(2)}) collective-permute-start(bf16[128,1024]{1,0:T(8,128)(2,1)S(1)} %broadcast_select_fusion.2), channel_id=1, source_target_pairs={{0,192},{1,193},{32,224},{33,225},{64,0},{65,1},{96,32},{97,33},{1... | collective-permute-start | bytes 786440 | tf_op jit(solution)/shard_map/ppermute | solution.py:55
  162.6 3.5 %collective-permute-start.23 = (bf16[128,1024]{1,0:T(8,128)(2,1)}, bf16[128,1024]{1,0:T(8,128)(2,1)S(1)}, u32[]{:S(2)}, u32[]{:S(2)}) collective-permute-start(bf16[128,1024]{1,0:T(8,128)(2,1)} %get-tuple-element.54), channel_id=1, source_target_pairs={{0,160},{1,225},{32,128},{33,193},{64,224},{65,33},{96,192},{97,1}... | collective-permute-start | bytes 786440 | tf_op jit(solution)/shard_map/ppermute | solution.py:55
  167.0 6.1 %collective-permute-done.26 = bf16[128,1024]{1,0:T(8,128)(2,1)S(1)} collective-permute-done((bf16[128,1024]{1,0:T(8,128)(2,1)S(1)}, bf16[128,1024]{1,0:T(8,128)(2,1)S(1)}, u32[]{:S(2)}, u32[]{:S(2)}) %collective-permute-start.26) | collective-permute-done | bytes 262176 | tf_op jit(solution)/shard_map/ppermute | solution.py:55
  173.1 5.6 %collective-permute-done.23 = bf16[128,1024]{1,0:T(8,128)(2,1)S(1)} collective-permute-done((bf16[128,1024]{1,0:T(8,128)(2,1)}, bf16[128,1024]{1,0:T(8,128)(2,1)S(1)}, u32[]{:S(2)}, u32[]{:S(2)}) %collective-permute-start.23) | collective-permute-done | bytes 262176 | tf_op jit(solution)/shard_map/ppermute | solution.py:55
  180.5 2.6 %collective-permute-start.32 = (bf16[128,1024]{1,0:T(8,128)(2,1)S(1)}, bf16[128,1024]{1,0:T(8,128)(2,1)S(1)}, u32[]{:S(2)}, u32[]{:S(2)}) collective-permute-start(bf16[128,1024]{1,0:T(8,128)(2,1)S(1)} %multiply_convert_fusion), channel_id=1, source_target_pairs={{192,0},{193,1},{224,32},{225,33},{0,64},{1,65},{32,96},{33,97},{6... | collective-permute-start | bytes 786440 | tf_op jit(solution)/shard_map/ppermute | solution.py:55
  184.6 3.9 %collective-permute-start.27 = (bf16[128,1024]{1,0:T(8,128)(2,1)S(1)}, bf16[128,1024]{1,0:T(8,128)(2,1)S(1)}, u32[]{:S(2)}, u32[]{:S(2)}) collective-permute-start(bf16[128,1024]{1,0:T(8,128)(2,1)S(1)} %multiply_convert_fusion), channel_id=1, source_target_pairs={{128,0},{97,1},{160,32},{65,33},{192,64},{161,65},{224,96},{129,97... | collective-permute-start | bytes 786440 | tf_op jit(solution)/shard_map/ppermute | solution.py:55
  190.2 7.7 %decoder_grad.1 = bf16[1024,1024]{1,0:T(8,128)(2,1)} custom-call(bf16[128,1024]{1,0:T(8,128)(2,1)} %copy-done.2, bf16[128,1024]{1,0:T(8,128)(2,1)} %copy-done.9, bf16[128,1024]{1,0:T(8,128)(2,1)} %copy-done.3, bf16[128,1024]{1,0:T(8,128)(2,1)} %copy-done.4, bf16[128,1024]{1,0:T(8,128)(2,1)} %copy-done.7, bf16[128,1024]{1,0:T(8,128)(2,1)} %copy-done.6, ...), custom_call_target="tpu_custom_call" | custom-call | tf_op jit(solution)/shard_map/decoder_grad/pallas_call | solution.py:134
  198.4 10.6 %collective-permute-start.30 = (bf16[128,1024]{1,0:T(8,128)(2,1)S(1)}, bf16[128,1024]{1,0:T(8,128)(2,1)S(1)}, u32[]{:S(2)}, u32[]{:S(2)}) collective-permute-start(bf16[128,1024]{1,0:T(8,128)(2,1)S(1)} %multiply_convert_fusion), channel_id=1, source_target_pairs={{96,0},{129,1},{64,32},{161,33},{160,64},{193,65},{128,96},{225,97... | collective-permute-start | bytes 786440 | tf_op jit(solution)/shard_map/ppermute | solution.py:55
  210.5 5.2 %encoder_grad.2.refs_4_ = f32[1024,1024]{1,0:T(8,128)} custom-call(bf16[1024,1024]{1,0:T(8,128)(2,1)} %transpose.21.res_ref, bf16[128,1024]{1,0:T(8,128)(2,1)} %get-tuple-element.75.refs_0_, bf16[128,1024]{1,0:T(8,128)(2,1)} %copy-done.12, bf16[128,1024]{1,0:T(8,128)(2,1)} %get-tuple-element.74.refs_2_, bf16[128,1024]{1,0:T(8,128)(2,1)} %copy-done.13), custom_call_target="tpu_custom_call" | custom-call | tf_op jit(solution)/shard_map/encoder_grad/pallas_call | solution.py:190
  217.4 5.5 %encoder_grad.3 = bf16[1024,1024]{1,0:T(8,128)(2,1)} custom-call(bf16[1024,1024]{1,0:T(8,128)(2,1)} %transpose.21.res_ref, bf16[128,1024]{1,0:T(8,128)(2,1)} %copy-done.11, bf16[128,1024]{1,0:T(8,128)(2,1)} %copy-done.10, bf16[128,1024]{1,0:T(8,128)(2,1)} %copy-done.15, bf16[128,1024]{1,0:T(8,128)(2,1)} %copy-done.14, f32[1024,1024]{1,0:T(8,128)} %encoder_grad.2.refs_4_), custom_call_target="tpu_custom_call" | custom-call | tf_op jit(solution)/shard_map/encoder_grad/pallas_call | solution.py:190
  (110 shorter events, 47.9 us)
Async XLA Ops:
  6.8 17.7 %collective-permute-start = (bf16[128,1024]{1,0:T(8,128)(2,1)}, bf16[128,1024]{1,0:T(8,128)(2,1)S(1)}, u32[]{:S(2)}, u32[]{:S(2)}) collective-permute-start(bf16[128,1024]{1,0:T(8,128)(2,1)} %get-tuple-element.33), channel_id=1, source_target_pairs={{0,128},{1,97},{32,160},{33,65},{64,192},{65,161},{96,224},{97,129... | collective-permute-start | bytes 786440 | tf_op jit(solution)/shard_map/ppermute | solution.py:55
  9.1 15.8 %collective-permute-start.1 = (bf16[128,1024]{1,0:T(8,128)(2,1)}, bf16[128,1024]{1,0:T(8,128)(2,1)S(1)}, u32[]{:S(2)}, u32[]{:S(2)}) collective-permute-start(bf16[128,1024]{1,0:T(8,128)(2,1)} %get-tuple-element.34), channel_id=1, source_target_pairs={{0,224},{1,161},{32,192},{33,129},{64,32},{65,225},{96,0},{97,193}... | collective-permute-start | bytes 786440 | tf_op jit(solution)/shard_map/ppermute | solution.py:55
  11.0 15.5 %collective-permute-start.2 = (bf16[128,1024]{1,0:T(8,128)(2,1)}, bf16[128,1024]{1,0:T(8,128)(2,1)S(1)}, u32[]{:S(2)}, u32[]{:S(2)}) collective-permute-start(bf16[128,1024]{1,0:T(8,128)(2,1)} %get-tuple-element.35), channel_id=1, source_target_pairs={{0,96},{1,129},{32,64},{33,161},{64,160},{65,193},{96,128},{97,225... | collective-permute-start | bytes 786440 | tf_op jit(solution)/shard_map/ppermute | solution.py:55
  12.0 17.8 %collective-permute-start.3 = (bf16[128,1024]{1,0:T(8,128)(2,1)}, bf16[128,1024]{1,0:T(8,128)(2,1)S(1)}, u32[]{:S(2)}, u32[]{:S(2)}) collective-permute-start(bf16[128,1024]{1,0:T(8,128)(2,1)} %get-tuple-element.36), channel_id=1, source_target_pairs={{0,160},{1,225},{32,128},{33,193},{64,224},{65,33},{96,192},{97,1}... | collective-permute-start | bytes 786440 | tf_op jit(solution)/shard_map/ppermute | solution.py:55
  21.3 11.7 %collective-permute-start.4 = (bf16[128,1024]{1,0:T(8,128)(2,1)}, bf16[128,1024]{1,0:T(8,128)(2,1)S(1)}, u32[]{:S(2)}, u32[]{:S(2)}) collective-permute-start(bf16[128,1024]{1,0:T(8,128)(2,1)} %get-tuple-element.37), channel_id=1, source_target_pairs={{0,32},{1,65},{32,0},{33,97},{64,96},{65,129},{96,64},{97,161},{12... | collective-permute-start | bytes 786440 | tf_op jit(solution)/shard_map/ppermute | solution.py:55
  24.5 8.4 %collective-permute-start.5 = (bf16[128,1024]{1,0:T(8,128)(2,1)}, bf16[128,1024]{1,0:T(8,128)(2,1)S(1)}, u32[]{:S(2)}, u32[]{:S(2)}) collective-permute-start(bf16[128,1024]{1,0:T(8,128)(2,1)} %get-tuple-element.38), channel_id=1, source_target_pairs={{0,64},{1,33},{32,96},{33,1},{64,128},{65,97},{96,160},{97,65},{12... | collective-permute-start | bytes 786440 | tf_op jit(solution)/shard_map/ppermute | solution.py:55
  24.8 10.1 %collective-permute-start.6 = (bf16[128,1024]{1,0:T(8,128)(2,1)}, bf16[128,1024]{1,0:T(8,128)(2,1)S(1)}, u32[]{:S(2)}, u32[]{:S(2)}) collective-permute-start(bf16[128,1024]{1,0:T(8,128)(2,1)} %get-tuple-element.39), channel_id=1, source_target_pairs={{0,192},{1,193},{32,224},{33,225},{64,0},{65,1},{96,32},{97,33},{1... | collective-permute-start | bytes 786440 | tf_op jit(solution)/shard_map/ppermute | solution.py:55
  37.5 11.0 %collective-permute-start.7 = (bf16[128,1024]{1,0:T(8,128)(2,1)S(1)}, bf16[128,1024]{1,0:T(8,128)(2,1)S(1)}, u32[]{:S(2)}, u32[]{:S(2)}) collective-permute-start(bf16[128,1024]{1,0:T(8,128)(2,1)S(1)} %get-tuple-element.64), channel_id=1, source_target_pairs={{192,0},{193,1},{224,32},{225,33},{0,64},{1,65},{32,96},{33,97},{6... | collective-permute-start | bytes 786440 | tf_op jit(solution)/shard_map/ppermute | solution.py:55
  38.1 20.7 %collective-permute-start.9 = (bf16[128,1024]{1,0:T(8,128)(2,1)S(1)}, bf16[128,1024]{1,0:T(8,128)(2,1)S(1)}, u32[]{:S(2)}, u32[]{:S(2)}) collective-permute-start(bf16[128,1024]{1,0:T(8,128)(2,1)S(1)} %get-tuple-element.64), channel_id=1, source_target_pairs={{64,0},{33,1},{96,32},{1,33},{128,64},{97,65},{160,96},{65,97},{19... | collective-permute-start | bytes 786440 | tf_op jit(solution)/shard_map/ppermute | solution.py:55
  39.6 23.4 %collective-permute-start.13 = (bf16[128,1024]{1,0:T(8,128)(2,1)S(1)}, bf16[128,1024]{1,0:T(8,128)(2,1)S(1)}, u32[]{:S(2)}, u32[]{:S(2)}) collective-permute-start(bf16[128,1024]{1,0:T(8,128)(2,1)S(1)} %get-tuple-element.64), channel_id=1, source_target_pairs={{96,0},{129,1},{64,32},{161,33},{160,64},{193,65},{128,96},{225,97... | collective-permute-start | bytes 786440 | tf_op jit(solution)/shard_map/ppermute | solution.py:55
  41.8 21.2 %collective-permute-start.12 = (bf16[128,1024]{1,0:T(8,128)(2,1)S(1)}, bf16[128,1024]{1,0:T(8,128)(2,1)S(1)}, u32[]{:S(2)}, u32[]{:S(2)}) collective-permute-start(bf16[128,1024]{1,0:T(8,128)(2,1)S(1)} %get-tuple-element.64), channel_id=1, source_target_pairs={{224,0},{161,1},{192,32},{129,33},{32,64},{225,65},{0,96},{193,97}... | collective-permute-start | bytes 786440 | tf_op jit(solution)/shard_map/ppermute | solution.py:55
  42.5 22.6 %collective-permute-start.11 = (bf16[128,1024]{1,0:T(8,128)(2,1)S(1)}, bf16[128,1024]{1,0:T(8,128)(2,1)S(1)}, u32[]{:S(2)}, u32[]{:S(2)}) collective-permute-start(bf16[128,1024]{1,0:T(8,128)(2,1)S(1)} %get-tuple-element.64), channel_id=1, source_target_pairs={{128,0},{97,1},{160,32},{65,33},{192,64},{161,65},{224,96},{129,97... | collective-permute-start | bytes 786440 | tf_op jit(solution)/shard_map/ppermute | solution.py:55
  48.5 16.5 %collective-permute-start.14 = (bf16[128,1024]{1,0:T(8,128)(2,1)S(1)}, bf16[128,1024]{1,0:T(8,128)(2,1)S(1)}, u32[]{:S(2)}, u32[]{:S(2)}) collective-permute-start(bf16[128,1024]{1,0:T(8,128)(2,1)S(1)} %get-tuple-element.64), channel_id=1, source_target_pairs={{160,0},{225,1},{128,32},{193,33},{224,64},{33,65},{192,96},{1,97}... | collective-permute-start | bytes 786440 | tf_op jit(solution)/shard_map/ppermute | solution.py:55
  58.9 7.7 %collective-permute-start.8 = (bf16[128,1024]{1,0:T(8,128)(2,1)S(1)}, bf16[128,1024]{1,0:T(8,128)(2,1)S(1)}, u32[]{:S(2)}, u32[]{:S(2)}) collective-permute-start(bf16[128,1024]{1,0:T(8,128)(2,1)S(1)} %get-tuple-element.64), channel_id=1, source_target_pairs={{32,0},{65,1},{0,32},{97,33},{96,64},{129,65},{64,96},{161,97},{16... | collective-permute-start | bytes 786440 | tf_op jit(solution)/shard_map/ppermute | solution.py:55
  71.1 37.6 %all-to-all-start = ((bf16[16,32,1024]{2,1,0:T(8,128)(2,1)}), bf16[16,32,1024]{2,1,0:T(8,128)(2,1)S(1)}, u32[]{:S(2)}, u32[]{:S(2)}) async-start(bf16[16,32,1024]{2,1,0:T(8,128)(2,1)} %bitcast.128), calls=%async_computation | async-start | bytes 2097152 | tf_op jit(solution)/shard_map/all_to_all | solution.py:279
  90.3 5.1 %collective-permute-start.18 = (f32[1024]{0:T(1024)S(1)}, f32[1024]{0:T(1024)S(1)}, u32[]{:S(2)}, u32[]{:S(2)}) collective-permute-start(f32[1024]{0:T(1024)S(1)} %get-tuple-element.63), channel_id=1, source_target_pairs={{0,128},{64,192},{128,0},{192,64},{1,129},{65,193},{129,1},{193,65... | collective-permute-start | bytes 12296 | tf_op jit(solution)/shard_map/ppermute | solution.py:35
  110.9 33.2 %all-to-all-start.1 = ((bf16[16,32,1024]{2,1,0:T(8,128)(2,1)}), bf16[16,32,1024]{2,1,0:T(8,128)(2,1)S(1)}, u32[]{:S(2)}, u32[]{:S(2)}) async-start(bf16[16,32,1024]{2,1,0:T(8,128)(2,1)} %broadcast_in_dim.5), calls=%async_computation.1 | async-start | bytes 2097152 | tf_op jit(solution)/shard_map/all_to_all | solution.py:300
  144.0 7.4 %collective-permute-start.19 = (bf16[4,128,1024]{2,1,0:T(8,128)(2,1)S(1)}, bf16[4,128,1024]{2,1,0:T(8,128)(2,1)S(1)}, u32[]{:S(2)}, u32[]{:S(2)}) collective-permute-start(bf16[4,128,1024]{2,1,0:T(8,128)(2,1)S(1)} %bitcast.123), channel_id=1, source_target_pairs={{0,1},{1,0},{2,3},{3,2},{4,5},{5,4},{6,7},{7,6},{8,9},{9,8},{10,11... | collective-permute-start | bytes 3145736 | tf_op jit(solution)/shard_map/ppermute | solution.py:35
  145.6 17.0 %collective-permute-start.20 = (bf16[128,1024]{1,0:T(8,128)(2,1)}, bf16[128,1024]{1,0:T(8,128)(2,1)}, u32[]{:S(2)}, u32[]{:S(2)}) collective-permute-start(bf16[128,1024]{1,0:T(8,128)(2,1)} %convolution_convert_fusion.4), channel_id=1, source_target_pairs={{0,128},{1,97},{32,160},{33,65},{64,192},{65,161},{96,224},{97,129... | collective-permute-start | bytes 786440 | tf_op jit(solution)/shard_map/ppermute | solution.py:55
  147.7 18.4 %collective-permute-start.21 = (bf16[128,1024]{1,0:T(8,128)(2,1)}, bf16[128,1024]{1,0:T(8,128)(2,1)}, u32[]{:S(2)}, u32[]{:S(2)}) collective-permute-start(bf16[128,1024]{1,0:T(8,128)(2,1)} %convolution_convert_fusion.3), channel_id=1, source_target_pairs={{0,224},{1,161},{32,192},{33,129},{64,32},{65,225},{96,0},{97,193}... | collective-permute-start | bytes 786440 | tf_op jit(solution)/shard_map/ppermute | solution.py:55
  150.0 17.0 %collective-permute-start.24 = (bf16[128,1024]{1,0:T(8,128)(2,1)S(1)}, bf16[128,1024]{1,0:T(8,128)(2,1)S(1)}, u32[]{:S(2)}, u32[]{:S(2)}) collective-permute-start(bf16[128,1024]{1,0:T(8,128)(2,1)S(1)} %convolution_convert_fusion.2), channel_id=1, source_target_pairs={{0,32},{1,65},{32,0},{33,97},{64,96},{65,129},{96,64},{97,161},{12... | collective-permute-start | bytes 786440 | tf_op jit(solution)/shard_map/ppermute | solution.py:55
  158.5 14.6 %collective-permute-start.26 = (bf16[128,1024]{1,0:T(8,128)(2,1)S(1)}, bf16[128,1024]{1,0:T(8,128)(2,1)S(1)}, u32[]{:S(2)}, u32[]{:S(2)}) collective-permute-start(bf16[128,1024]{1,0:T(8,128)(2,1)S(1)} %broadcast_select_fusion.2), channel_id=1, source_target_pairs={{0,192},{1,193},{32,224},{33,225},{64,0},{65,1},{96,32},{97,33},{1... | collective-permute-start | bytes 786440 | tf_op jit(solution)/shard_map/ppermute | solution.py:55
  162.6 10.5 %collective-permute-start.22 = (bf16[128,1024]{1,0:T(8,128)(2,1)}, bf16[128,1024]{1,0:T(8,128)(2,1)S(1)}, u32[]{:S(2)}, u32[]{:S(2)}) collective-permute-start(bf16[128,1024]{1,0:T(8,128)(2,1)} %get-tuple-element.53), channel_id=1, source_target_pairs={{0,96},{1,129},{32,64},{33,161},{64,160},{65,193},{96,128},{97,225... | collective-permute-start | bytes 786440 | tf_op jit(solution)/shard_map/ppermute | solution.py:55
  162.6 16.1 %collective-permute-start.23 = (bf16[128,1024]{1,0:T(8,128)(2,1)}, bf16[128,1024]{1,0:T(8,128)(2,1)S(1)}, u32[]{:S(2)}, u32[]{:S(2)}) collective-permute-start(bf16[128,1024]{1,0:T(8,128)(2,1)} %get-tuple-element.54), channel_id=1, source_target_pairs={{0,160},{1,225},{32,128},{33,193},{64,224},{65,33},{96,192},{97,1}... | collective-permute-start | bytes 786440 | tf_op jit(solution)/shard_map/ppermute | solution.py:55
  166.1 12.6 %collective-permute-start.25 = (bf16[128,1024]{1,0:T(8,128)(2,1)}, bf16[128,1024]{1,0:T(8,128)(2,1)S(1)}, u32[]{:S(2)}, u32[]{:S(2)}) collective-permute-start(bf16[128,1024]{1,0:T(8,128)(2,1)} %get-tuple-element.55), channel_id=1, source_target_pairs={{0,64},{1,33},{32,96},{33,1},{64,128},{65,97},{96,160},{97,65},{12... | collective-permute-start | bytes 786440 | tf_op jit(solution)/shard_map/ppermute | solution.py:55
  180.3 9.2 %collective-permute-start.29 = (bf16[128,1024]{1,0:T(8,128)(2,1)S(1)}, bf16[128,1024]{1,0:T(8,128)(2,1)S(1)}, u32[]{:S(2)}, u32[]{:S(2)}) collective-permute-start(bf16[128,1024]{1,0:T(8,128)(2,1)S(1)} %multiply_convert_fusion), channel_id=1, source_target_pairs={{32,0},{65,1},{0,32},{97,33},{96,64},{129,65},{64,96},{161,97},{16... | collective-permute-start | bytes 786440 | tf_op jit(solution)/shard_map/ppermute | solution.py:55
  180.5 17.9 %collective-permute-start.32 = (bf16[128,1024]{1,0:T(8,128)(2,1)S(1)}, bf16[128,1024]{1,0:T(8,128)(2,1)S(1)}, u32[]{:S(2)}, u32[]{:S(2)}) collective-permute-start(bf16[128,1024]{1,0:T(8,128)(2,1)S(1)} %multiply_convert_fusion), channel_id=1, source_target_pairs={{192,0},{193,1},{224,32},{225,33},{0,64},{1,65},{32,96},{33,97},{6... | collective-permute-start | bytes 786440 | tf_op jit(solution)/shard_map/ppermute | solution.py:55
  183.1 26.8 %collective-permute-start.33 = (bf16[128,1024]{1,0:T(8,128)(2,1)S(1)}, bf16[128,1024]{1,0:T(8,128)(2,1)S(1)}, u32[]{:S(2)}, u32[]{:S(2)}) collective-permute-start(bf16[128,1024]{1,0:T(8,128)(2,1)S(1)} %multiply_convert_fusion), channel_id=1, source_target_pairs={{64,0},{33,1},{96,32},{1,33},{128,64},{97,65},{160,96},{65,97},{19... | collective-permute-start | bytes 786440 | tf_op jit(solution)/shard_map/ppermute | solution.py:55
  183.1 32.7 %collective-permute-start.28 = (bf16[128,1024]{1,0:T(8,128)(2,1)S(1)}, bf16[128,1024]{1,0:T(8,128)(2,1)S(1)}, u32[]{:S(2)}, u32[]{:S(2)}) collective-permute-start(bf16[128,1024]{1,0:T(8,128)(2,1)S(1)} %multiply_convert_fusion), channel_id=1, source_target_pairs={{224,0},{161,1},{192,32},{129,33},{32,64},{225,65},{0,96},{193,97}... | collective-permute-start | bytes 786440 | tf_op jit(solution)/shard_map/ppermute | solution.py:55
  184.6 31.1 %collective-permute-start.27 = (bf16[128,1024]{1,0:T(8,128)(2,1)S(1)}, bf16[128,1024]{1,0:T(8,128)(2,1)S(1)}, u32[]{:S(2)}, u32[]{:S(2)}) collective-permute-start(bf16[128,1024]{1,0:T(8,128)(2,1)S(1)} %multiply_convert_fusion), channel_id=1, source_target_pairs={{128,0},{97,1},{160,32},{65,33},{192,64},{161,65},{224,96},{129,97... | collective-permute-start | bytes 786440 | tf_op jit(solution)/shard_map/ppermute | solution.py:55
  197.9 17.9 %collective-permute-start.31 = (bf16[128,1024]{1,0:T(8,128)(2,1)S(1)}, bf16[128,1024]{1,0:T(8,128)(2,1)S(1)}, u32[]{:S(2)}, u32[]{:S(2)}) collective-permute-start(bf16[128,1024]{1,0:T(8,128)(2,1)S(1)} %multiply_convert_fusion), channel_id=1, source_target_pairs={{160,0},{225,1},{128,32},{193,33},{224,64},{33,65},{192,96},{1,97}... | collective-permute-start | bytes 786440 | tf_op jit(solution)/shard_map/ppermute | solution.py:55
  198.4 17.4 %collective-permute-start.30 = (bf16[128,1024]{1,0:T(8,128)(2,1)S(1)}, bf16[128,1024]{1,0:T(8,128)(2,1)S(1)}, u32[]{:S(2)}, u32[]{:S(2)}) collective-permute-start(bf16[128,1024]{1,0:T(8,128)(2,1)S(1)} %multiply_convert_fusion), channel_id=1, source_target_pairs={{96,0},{129,1},{64,32},{161,33},{160,64},{193,65},{128,96},{225,97... | collective-permute-start | bytes 786440 | tf_op jit(solution)/shard_map/ppermute | solution.py:55
  (22 other events, 195.6 us)

commit v6 on v4

--- a/solution.py
+++ b/solution.py
@@ -113,36 +113,46 @@
     width, feat = decoder.shape
     block = latents[0].shape[0]
     rows = n * block
-    tile = 256
+    tile, span = 256, 512
 
     def kernel(*refs):
         lat, err = refs[:n], refs[n : 2 * n]
-        dec_ref, norm_ref, out_ref, err_all = refs[2 * n :]
-
-        @pl.when(pl.program_id(0) == 0)
+        dec_ref, norm_ref, out_ref, err_all, tall_ref, shrink_ref = refs[2 * n :]
+
+        @pl.when((pl.program_id(0) == 0) & (pl.program_id(1) == 0))
         def _():
             for i in range(n):
                 err_all[i * block : (i + 1) * block] = err[i][...]
 
-        tall = jnp.concatenate([l_ref[...] for l_ref in lat], axis=0).T
-        outer = jnp.dot(tall, err_all[...], preferred_element_type=f32)
-        ones = jnp.ones((rows, 128), bf16)
-        sums = jnp.dot(tall, ones, preferred_element_type=f32)[:, :1]
-        shrink = loss_scale * PENALTY * sums / norm_ref[...].T[:, :1]
-        out_ref[...] = (loss_scale * outer + shrink * dec_ref[...].astype(f32)).astype(bf16)
+        @pl.when(pl.program_id(1) == 0)
+        def _():
+            tall_ref[...] = jnp.concatenate([l_ref[...] for l_ref in lat], axis=0).T
+            ones = jnp.ones((rows, 128), bf16)
+            sums = jnp.dot(tall_ref[...], ones, preferred_element_type=f32)
+            shrink_ref[...] = loss_scale * PENALTY * sums / norm_ref[...].T[:, :1]
+
+        cols = pl.ds(pl.multiple_of(pl.program_id(1) * span, span), span)
+        outer = jnp.dot(tall_ref[...], err_all[:, cols], preferred_element_type=f32)
+        out_ref[...] = (
+            loss_scale * outer + shrink_ref[:, :1] * dec_ref[...].astype(f32)
+        ).astype(bf16)
 
     return pl.pallas_call(
         kernel,
-        grid=(width // tile,),
-        in_specs=[pl.BlockSpec((block, tile), lambda i: (0, i))] * n
-        + [pl.BlockSpec((block, feat), lambda i: (0, 0))] * n
+        grid=(width // tile, feat // span),
+        in_specs=[pl.BlockSpec((block, tile), lambda i, k: (0, i))] * n
+        + [pl.BlockSpec((block, feat), lambda i, k: (0, 0))] * n
         + [
-            pl.BlockSpec((tile, feat), lambda i: (i, 0)),
-            pl.BlockSpec((8, tile), lambda i: (0, i)),
+            pl.BlockSpec((tile, span), lambda i, k: (i, k)),
+            pl.BlockSpec((8, tile), lambda i, k: (0, i)),
         ],
-        out_specs=pl.BlockSpec((tile, feat), lambda i: (i, 0)),
+        out_specs=pl.BlockSpec((tile, span), lambda i, k: (i, k)),
         out_shape=jax.ShapeDtypeStruct(decoder.shape, bf16),
-        scratch_shapes=[pltpu.VMEM((rows, feat), bf16)],
+        scratch_shapes=[
+            pltpu.VMEM((rows, feat), bf16),
+            pltpu.VMEM((tile, rows), bf16),
+            pltpu.VMEM((tile, 128), f32),
+        ],
         name="decoder_grad",
     )(*latents, *errors, decoder, norms)
 
@@ -296,15 +306,16 @@
     near_err = [mine[0], mine[1], theirs[0], theirs[1]]
     far_err = [mine[2], mine[3], theirs[2], theirs[3]]
 
-    types = [bf16] * 4
-    far0, far1, near1, low = blocks_dot(
-        decoder, 1, types, blocks=[far_err[0], far_err[1], near_err[1], near_err[0]]
-    )
-    far2, far3, near3, high = blocks_dot(
-        decoder, 1, types, blocks=[far_err[2], far_err[3], near_err[3], near_err[2]]
-    )
-    sent, kept = jnp.where(first, high, low), jnp.where(first, low, high)
-    act_grad = sum_src([far0, far1, far2, far3], [near1, near3, sent, kept]) + penalty[None, :]
+    sent = jnp.where(first, near_err[2], near_err[0])
+    kept = jnp.where(first, near_err[0], near_err[2])
+    far_back = [dot_t(e, decoder).astype(bf16) for e in far_err]
+    near1 = dot_t(near_err[1], decoder).astype(bf16)
+    sent, far_back[2], far_back[3] = lax.optimization_barrier((sent, far_back[2], far_back[3]))
+    near3, sent, kept = blocks_dot(
+        decoder, 1, [bf16, bf16, f32], blocks=[near_err[3], sent, kept]
+    )
+    near_back = [near1, near3, sent, kept]
+    act_grad = sum_src(far_back, near_back) + penalty[None, :]
     grad_decoder = decoder_grad(
         near + far, near_err + far_err, decoder, jnp.stack([own_norm] * 8), loss_scale
     )

time: 218 us -> 223 us (1.023)
  matrix products: 2.85 us -> 10.5 us
  waiting for transfers between devices: 83.5 us -> 77.8 us
  starting transfers between devices: 67.3 us -> 70.1 us
    dot_general x0 -> x5, matrix products: none -> 7.69 us  [dot_t(): return jnp.einsum('bk,jk->bj', a, b, preferred_element_type=f32)]
    ppermute x28, waiting for transfers between devices: 41.6 us -> 36.1 us  [move(): return lax.ppermute(value, ('y', 'xl', 'core'), pairs)]
    pallas_call x4 -> x3, Pallas kernels: 20.4 us -> 15.5 us  [blocks_dot(): pl.pallas_call(kernel, grid_spec=pltpu.PrefetchScalarGridSpec(num_scalar_...]
    pallas_call x1, Pallas kernels: 7.73 us -> 10.7 us  [decoder_grad(): pl.pallas_call(kernel, grid=(width // tile, feat // span), in_specs=[pl.B...]
    ppermute x28, starting transfers between devices: 44.6 us -> 47.4 us  [move(): return lax.ppermute(value, ('y', 'xl', 'core'), pairs)]
  transfers between devices with their start and end apart: 36 -> 36, of which waited for: 21 -> 17; matrix products, arithmetic and copies ran while one was open for 4% -> 8% of each run, Pallas kernels for 16% -> 15%
where the time goes in v6:
time: 223 us; the launch traced here: 221 us
  waiting for transfers between devices  77.8 us (35%)
  starting transfers between devices  70.1 us (31%)
  Pallas kernels  43.6 us (20%)
  matrix products  10.5 us (5%)
  other arithmetic  10.2 us (5%)
  local copies, waits for them, and re-layouts  6.61 us (3%)
    ppermute x28, starting transfers between devices, move(): return lax.ppermute(value, ('y', 'xl', 'core'), pairs)  47.4 us
    ppermute x28, waiting for transfers between devices, move(): return lax.ppermute(value, ('y', 'xl', 'core'), pairs)  36.1 us
    all_to_all x1, waiting for transfers between devices, per_device(): mine = lax.all_to_all(errors, RING, 0, 0).reshape(4, block, -1)  21.1 us
    pallas_call x3, Pallas kernels, blocks_dot(): pl.pallas_call(kernel, grid_spec=pltpu.PrefetchScalarGridSpec(num_scalar_...  15.5 us
    all_to_all x1, waiting for transfers between devices, per_device(): shares = lax.all_to_all(shares.reshape(N_RING, rows, -1), RING, 0, 0)  13.7 us
    all_to_all x1, starting transfers between devices, per_device(): shares = lax.all_to_all(shares.reshape(N_RING, rows, -1), RING, 0, 0)  11.3 us
    pallas_call x2, Pallas kernels, encoder_grad(): pl.pallas_call(kernel, grid=(feat // tile,), in_specs=[pl.BlockSpec((tile...  10.7 us
    pallas_call x1, Pallas kernels, decoder_grad(): pl.pallas_call(kernel, grid=(width // tile, feat // span), in_specs=[pl.B...  10.7 us
  transfers between devices with their start and end apart: 36, of which 17 were waited for; matrix products, arithmetic and copies ran while one was open for 8% of the time, Pallas kernels for 15%

profile of v6, /device:TPU:32, one launch (start us, length us, event | category | flops | bytes accessed | tf_op | source)
XLA Modules:
  0.0 220.7 jit_solution(10064807171596746131)
XLA Ops:
  1.4 5.4 %blocks_dot.4 = (bf16[128,1024]{1,0:T(8,128)(2,1)}, bf16[128,1024]{1,0:T(8,128)(2,1)}, bf16[128,1024]{1,0:T(8,128)(2,1)}, bf16[128,1024]{1,0:T(8,128)(2,1)}) custom-call(s32[4]{0:T(128)} %pad_add_fusion.1.order_ref, bf16[1024,1024]{1,0:T(8,128)(2,1)} %in_ref.1, bf16[1024,1024]{1,0:T(8,128)(2,1)} %in_ref.1, bf16[1024,1024]{1,0:T(8,128)(2,1)} %in_ref.1, ...), custom_call_target="tpu_custom_call" | custom-call | tf_op jit(solution)/shard_map/blocks_dot/pallas_call | solution.py:97
  6.8 3.2 %collective-permute-start = (bf16[128,1024]{1,0:T(8,128)(2,1)}, bf16[128,1024]{1,0:T(8,128)(2,1)S(1)}, u32[]{:S(2)}, u32[]{:S(2)}) collective-permute-start(bf16[128,1024]{1,0:T(8,128)(2,1)} %get-tuple-element.32), channel_id=1, source_target_pairs={{0,128},{1,97},{32,160},{33,65},{64,192},{65,161},{96,224},{97,129... | collective-permute-start | bytes 786440 | tf_op jit(solution)/shard_map/ppermute | solution.py:55
  14.8 5.5 %blocks_dot.3 = (bf16[128,1024]{1,0:T(8,128)(2,1)}, bf16[128,1024]{1,0:T(8,128)(2,1)}, bf16[128,1024]{1,0:T(8,128)(2,1)}, f32[128,1024]{1,0:T(8,128)}) custom-call(s32[4]{0:T(128)} %pad_add_fusion.order_ref, bf16[1024,1024]{1,0:T(8,128)(2,1)} %in_ref.1, bf16[1024,1024]{1,0:T(8,128)(2,1)} %in_ref.1, bf16[1024,1024]{1,0:T(8,128)(2,1)} %in_ref.1, ...), custom_call_target="tpu_custom_call" | custom-call | tf_op jit(solution)/shard_map/blocks_dot/pallas_call | solution.py:97
  21.3 3.3 %collective-permute-done = bf16[128,1024]{1,0:T(8,128)(2,1)S(1)} collective-permute-done((bf16[128,1024]{1,0:T(8,128)(2,1)}, bf16[128,1024]{1,0:T(8,128)(2,1)S(1)}, u32[]{:S(2)}, u32[]{:S(2)}) %collective-permute-start) | collective-permute-done | bytes 262176 | tf_op jit(solution)/shard_map/ppermute | solution.py:55
  25.4 2.4 %collective-permute-start.6 = (bf16[128,1024]{1,0:T(8,128)(2,1)}, bf16[128,1024]{1,0:T(8,128)(2,1)S(1)}, u32[]{:S(2)}, u32[]{:S(2)}) collective-permute-start(bf16[128,1024]{1,0:T(8,128)(2,1)} %get-tuple-element.38), channel_id=1, source_target_pairs={{0,192},{1,193},{32,224},{33,225},{64,0},{65,1},{96,32},{97,33},{1... | collective-permute-start | bytes 786440 | tf_op jit(solution)/shard_map/ppermute | solution.py:55
  27.8 4.5 %collective-permute-done.3 = bf16[128,1024]{1,0:T(8,128)(2,1)S(1)} collective-permute-done((bf16[128,1024]{1,0:T(8,128)(2,1)}, bf16[128,1024]{1,0:T(8,128)(2,1)S(1)}, u32[]{:S(2)}, u32[]{:S(2)}) %collective-permute-start.3) | collective-permute-done | bytes 262176 | tf_op jit(solution)/shard_map/ppermute | solution.py:55
  34.9 2.4 %add_divide_fusion = (f32[128,1024]{1,0:T(8,128)}, f32[128,1024]{1,0:T(8,128)S(1)}) fusion(f32[1024]{0:T(1024)S(1)} %copy-done.19, bf16[128,1024]{1,0:T(8,128)(2,1)S(1)} %collective-permute-done.6, bf16[128,1024]{1,0:T(8,128)(2,1)S(1)} %collective-permute-done.5, bf16[128,1024]{1,0:T(8,128)(2,1)S(1)} %collective-permute-done.4, ...), kind=kLoop, calls=%fused_computation.29 | loop fusion | flops 2490368 | bytes 3411968 | tf_op jit(solution)/shard_map/div | solution.py:265
  42.3 2.5 %collective-permute-start.11 = (bf16[128,1024]{1,0:T(8,128)(2,1)S(1)}, bf16[128,1024]{1,0:T(8,128)(2,1)S(1)}, u32[]{:S(2)}, u32[]{:S(2)}) collective-permute-start(bf16[128,1024]{1,0:T(8,128)(2,1)S(1)} %fusion.2), channel_id=1, source_target_pairs={{128,0},{97,1},{160,32},{65,33},{192,64},{161,65},{224,96},{129,97... | collective-permute-start | bytes 786440 | tf_op jit(solution)/shard_map/ppermute | solution.py:55
  45.7 6.4 %collective-permute-done.7 = bf16[128,1024]{1,0:T(8,128)(2,1)S(1)} collective-permute-done((bf16[128,1024]{1,0:T(8,128)(2,1)S(1)}, bf16[128,1024]{1,0:T(8,128)(2,1)S(1)}, u32[]{:S(2)}, u32[]{:S(2)}) %collective-permute-start.7) | collective-permute-done | bytes 262176 | tf_op jit(solution)/shard_map/ppermute | solution.py:55
  54.1 2.0 collective-permute-start.13
  56.9 4.8 %collective-permute-done.11.refs_4_ = bf16[128,1024]{1,0:T(8,128)(2,1)S(1)} collective-permute-done((bf16[128,1024]{1,0:T(8,128)(2,1)S(1)}, bf16[128,1024]{1,0:T(8,128)(2,1)S(1)}, u32[]{:S(2)}, u32[]{:S(2)}) %collective-permute-start.11) | collective-permute-done | bytes 262176 | tf_op jit(solution)/shard_map/ppermute | solution.py:55
  61.8 2.8 %collective-permute-done.13.refs_6_ = bf16[128,1024]{1,0:T(8,128)(2,1)S(1)} collective-permute-done((bf16[128,1024]{1,0:T(8,128)(2,1)S(1)}, bf16[128,1024]{1,0:T(8,128)(2,1)S(1)}, u32[]{:S(2)}, u32[]{:S(2)}) %collective-permute-start.13) | collective-permute-done | bytes 262176 | tf_op jit(solution)/shard_map/ppermute | solution.py:55
  69.1 11.3 %all-to-all-start = ((bf16[16,32,1024]{2,1,0:T(8,128)(2,1)}), bf16[16,32,1024]{2,1,0:T(8,128)(2,1)S(1)}, u32[]{:S(2)}, u32[]{:S(2)}) async-start(bf16[16,32,1024]{2,1,0:T(8,128)(2,1)} %bitcast.141), calls=%async_computation | async-start | bytes 2097152 | tf_op jit(solution)/shard_map/all_to_all | solution.py:282
  81.6 3.1 %collective-permute-done.16 = f32[1024]{0:T(1024)S(1)} collective-permute-done((f32[1024]{0:T(1024)S(1)}, f32[1024]{0:T(1024)S(1)}, u32[]{:S(2)}, u32[]{:S(2)}) %collective-permute-start.16) | collective-permute-done | bytes 4128 | tf_op jit(solution)/shard_map/ppermute | solution.py:35
  84.7 3.2 %collective-permute-start.17 = (f32[1024]{0:T(1024)S(1)}, f32[1024]{0:T(1024)S(1)}, u32[]{:S(2)}, u32[]{:S(2)}) collective-permute-start(f32[1024]{0:T(1024)S(1)} %add.269), channel_id=1, source_target_pairs={{0,64},{64,0},{128,192},{192,128},{1,65},{65,1},{129,193},{193,129... | collective-permute-start | bytes 12296 | tf_op jit(solution)/shard_map/ppermute | solution.py:35
  94.6 13.7 %all-to-all-done = bf16[16,32,1024]{2,1,0:T(8,128)(2,1)S(1)} async-done(((bf16[16,32,1024]{2,1,0:T(8,128)(2,1)}), bf16[16,32,1024]{2,1,0:T(8,128)(2,1)S(1)}, u32[]{:S(2)}, u32[]{:S(2)}) %all-to-all-start) | async-done | bytes 1048608 | tf_op jit(solution)/shard_map/all_to_all | solution.py:282
  110.5 5.4 %all-to-all-start.1 = ((bf16[16,32,1024]{2,1,0:T(8,128)(2,1)}), bf16[16,32,1024]{2,1,0:T(8,128)(2,1)S(1)}, u32[]{:S(2)}, u32[]{:S(2)}) async-start(bf16[16,32,1024]{2,1,0:T(8,128)(2,1)} %broadcast_in_dim.5), calls=%async_computation.1 | async-start | bytes 2097152 | tf_op jit(solution)/shard_map/all_to_all | solution.py:303
  115.9 6.8 %transpose.21.res_ref = bf16[1024,1024]{1,0:T(8,128)(2,1)} custom-call(s32[8]{0:T(128)} %stack.79.order_ref, bf16[1024,1024]{1,0:T(8,128)(2,1)} %in_ref.1), custom_call_target="tpu_custom_call" | custom-call | tf_op jit(solution)/shard_map/transpose/pallas_call | solution.py:166
  122.7 21.1 %all-to-all-done.1 = bf16[16,32,1024]{2,1,0:T(8,128)(2,1)S(1)} async-done(((bf16[16,32,1024]{2,1,0:T(8,128)(2,1)}), bf16[16,32,1024]{2,1,0:T(8,128)(2,1)S(1)}, u32[]{:S(2)}, u32[]{:S(2)}) %all-to-all-start.1) | async-done | bytes 1048608 | tf_op jit(solution)/shard_map/all_to_all | solution.py:303
  145.3 3.3 %collective-permute-start.21 = (bf16[128,1024]{1,0:T(8,128)(2,1)}, bf16[128,1024]{1,0:T(8,128)(2,1)S(1)}, u32[]{:S(2)}, u32[]{:S(2)}) collective-permute-start(bf16[128,1024]{1,0:T(8,128)(2,1)} %convolution_convert_fusion.3), channel_id=1, source_target_pairs={{0,224},{1,161},{32,192},{33,129},{64,32},{65,225},{96,0},{97,193}... | collective-permute-start | bytes 786440 | tf_op jit(solution)/shard_map/ppermute | solution.py:55
  153.0 2.2 %collective-permute-start.20 = (bf16[128,1024]{1,0:T(8,128)(2,1)}, bf16[128,1024]{1,0:T(8,128)(2,1)}, u32[]{:S(2)}, u32[]{:S(2)}) collective-permute-start(bf16[128,1024]{1,0:T(8,128)(2,1)} %convolution_convert_fusion.4), channel_id=1, source_target_pairs={{0,128},{1,97},{32,160},{33,65},{64,192},{65,161},{96,224},{97,129... | collective-permute-start | bytes 786440 | tf_op jit(solution)/shard_map/ppermute | solution.py:55
  160.3 4.6 %blocks_dot.5 = (bf16[128,1024]{1,0:T(8,128)(2,1)}, bf16[128,1024]{1,0:T(8,128)(2,1)}, f32[128,1024]{1,0:T(8,128)}) custom-call(s32[1]{0:T(128)} %constant.215.clone.1.order_ref, bf16[128,1024]{1,0:T(8,128)(2,1)} %get-tuple-element.69.refs_0_.refs_11_, bf16[128,1024]{1,0:T(8,128)(2,1)} %get-tuple-element.50.refs_1_, ...), custom_call_target="tpu_custom_call" | custom-call | tf_op jit(solution)/shard_map/blocks_dot/pallas_call | solution.py:97
  164.8 3.2 %collective-permute-start.26 = (bf16[128,1024]{1,0:T(8,128)(2,1)}, bf16[128,1024]{1,0:T(8,128)(2,1)S(1)}, u32[]{:S(2)}, u32[]{:S(2)}) collective-permute-start(bf16[128,1024]{1,0:T(8,128)(2,1)} %get-tuple-element.55), channel_id=1, source_target_pairs={{0,192},{1,193},{32,224},{33,225},{64,0},{65,1},{96,32},{97,33},{1... | collective-permute-start | bytes 786440 | tf_op jit(solution)/shard_map/ppermute | solution.py:55
  168.1 2.4 %collective-permute-start.23 = (bf16[128,1024]{1,0:T(8,128)(2,1)S(1)}, bf16[128,1024]{1,0:T(8,128)(2,1)}, u32[]{:S(2)}, u32[]{:S(2)}) collective-permute-start(bf16[128,1024]{1,0:T(8,128)(2,1)S(1)} %copy-done.11), channel_id=1, source_target_pairs={{0,160},{1,225},{32,128},{33,193},{64,224},{65,33},{96,192},{97,1}... | collective-permute-start | bytes 786440 | tf_op jit(solution)/shard_map/ppermute | solution.py:55
  172.2 10.7 %decoder_grad.1 = bf16[1024,1024]{1,0:T(8,128)(2,1)} custom-call(bf16[128,1024]{1,0:T(8,128)(2,1)} %copy-done.2, bf16[128,1024]{1,0:T(8,128)(2,1)} %copy-done.9, bf16[128,1024]{1,0:T(8,128)(2,1)} %copy-done.3, bf16[128,1024]{1,0:T(8,128)(2,1)} %copy-done.5, bf16[128,1024]{1,0:T(8,128)(2,1)} %copy-done.7, bf16[128,1024]{1,0:T(8,128)(2,1)} %copy-done.6, ...), custom_call_target="tpu_custom_call" | custom-call | tf_op jit(solution)/shard_map/decoder_grad/pallas_call | solution.py:140
  185.2 2.6 %collective-permute-start.31 = (bf16[128,1024]{1,0:T(8,128)(2,1)S(1)}, bf16[128,1024]{1,0:T(8,128)(2,1)S(1)}, u32[]{:S(2)}, u32[]{:S(2)}) collective-permute-start(bf16[128,1024]{1,0:T(8,128)(2,1)S(1)} %multiply_convert_fusion), channel_id=1, source_target_pairs={{192,0},{193,1},{224,32},{225,33},{0,64},{1,65},{32,96},{33,97},{6... | collective-permute-start | bytes 786440 | tf_op jit(solution)/shard_map/ppermute | solution.py:55
  188.4 2.2 %collective-permute-start.30 = (bf16[128,1024]{1,0:T(8,128)(2,1)S(1)}, bf16[128,1024]{1,0:T(8,128)(2,1)S(1)}, u32[]{:S(2)}, u32[]{:S(2)}) collective-permute-start(bf16[128,1024]{1,0:T(8,128)(2,1)S(1)} %multiply_convert_fusion), channel_id=1, source_target_pairs={{160,0},{225,1},{128,32},{193,33},{224,64},{33,65},{192,96},{1,97}... | collective-permute-start | bytes 786440 | tf_op jit(solution)/shard_map/ppermute | solution.py:55
  190.7 2.7 %collective-permute-start.29 = (bf16[128,1024]{1,0:T(8,128)(2,1)S(1)}, bf16[128,1024]{1,0:T(8,128)(2,1)S(1)}, u32[]{:S(2)}, u32[]{:S(2)}) collective-permute-start(bf16[128,1024]{1,0:T(8,128)(2,1)S(1)} %multiply_convert_fusion), channel_id=1, source_target_pairs={{96,0},{129,1},{64,32},{161,33},{160,64},{193,65},{128,96},{225,97... | collective-permute-start | bytes 786440 | tf_op jit(solution)/shard_map/ppermute | solution.py:55
  193.8 2.6 %collective-permute-start.28 = (bf16[128,1024]{1,0:T(8,128)(2,1)S(1)}, bf16[128,1024]{1,0:T(8,128)(2,1)S(1)}, u32[]{:S(2)}, u32[]{:S(2)}) collective-permute-start(bf16[128,1024]{1,0:T(8,128)(2,1)S(1)} %multiply_convert_fusion), channel_id=1, source_target_pairs={{224,0},{161,1},{192,32},{129,33},{32,64},{225,65},{0,96},{193,97}... | collective-permute-start | bytes 786440 | tf_op jit(solution)/shard_map/ppermute | solution.py:55
  196.4 10.2 %collective-permute-done.31 = bf16[128,1024]{1,0:T(8,128)(2,1)S(1)} collective-permute-done((bf16[128,1024]{1,0:T(8,128)(2,1)S(1)}, bf16[128,1024]{1,0:T(8,128)(2,1)S(1)}, u32[]{:S(2)}, u32[]{:S(2)}) %collective-permute-start.31) | collective-permute-done | bytes 262176 | tf_op jit(solution)/shard_map/ppermute | solution.py:55
  208.1 5.2 %encoder_grad.2.refs_4_ = f32[1024,1024]{1,0:T(8,128)} custom-call(bf16[1024,1024]{1,0:T(8,128)(2,1)} %transpose.21.res_ref, bf16[128,1024]{1,0:T(8,128)(2,1)} %get-tuple-element.75.refs_0_, bf16[128,1024]{1,0:T(8,128)(2,1)} %copy-done.15, bf16[128,1024]{1,0:T(8,128)(2,1)} %get-tuple-element.74.refs_2_, bf16[128,1024]{1,0:T(8,128)(2,1)} %copy-done.17), custom_call_target="tpu_custom_call" | custom-call | tf_op jit(solution)/shard_map/encoder_grad/pallas_call | solution.py:200
  215.2 5.5 %encoder_grad.3 = bf16[1024,1024]{1,0:T(8,128)(2,1)} custom-call(bf16[1024,1024]{1,0:T(8,128)(2,1)} %transpose.21.res_ref, bf16[128,1024]{1,0:T(8,128)(2,1)} %copy-done.18, bf16[128,1024]{1,0:T(8,128)(2,1)} %copy-done.16, bf16[128,1024]{1,0:T(8,128)(2,1)} %copy-done.14, bf16[128,1024]{1,0:T(8,128)(2,1)} %copy-done.13, f32[1024,1024]{1,0:T(8,128)} %encoder_grad.2.refs_4_), custom_call_target="tpu_custom_call" | custom-call | tf_op jit(solution)/shard_map/encoder_grad/pallas_call | solution.py:200
  (119 shorter events, 51.8 us)
Async XLA Ops:
  6.8 17.8 %collective-permute-start = (bf16[128,1024]{1,0:T(8,128)(2,1)}, bf16[128,1024]{1,0:T(8,128)(2,1)S(1)}, u32[]{:S(2)}, u32[]{:S(2)}) collective-permute-start(bf16[128,1024]{1,0:T(8,128)(2,1)} %get-tuple-element.32), channel_id=1, source_target_pairs={{0,128},{1,97},{32,160},{33,65},{64,192},{65,161},{96,224},{97,129... | collective-permute-start | bytes 786440 | tf_op jit(solution)/shard_map/ppermute | solution.py:55
  10.0 15.4 %collective-permute-start.1 = (bf16[128,1024]{1,0:T(8,128)(2,1)}, bf16[128,1024]{1,0:T(8,128)(2,1)S(1)}, u32[]{:S(2)}, u32[]{:S(2)}) collective-permute-start(bf16[128,1024]{1,0:T(8,128)(2,1)} %get-tuple-element.33), channel_id=1, source_target_pairs={{0,224},{1,161},{32,192},{33,129},{64,32},{65,225},{96,0},{97,193}... | collective-permute-start | bytes 786440 | tf_op jit(solution)/shard_map/ppermute | solution.py:55
  11.9 15.9 %collective-permute-start.2 = (bf16[128,1024]{1,0:T(8,128)(2,1)}, bf16[128,1024]{1,0:T(8,128)(2,1)S(1)}, u32[]{:S(2)}, u32[]{:S(2)}) collective-permute-start(bf16[128,1024]{1,0:T(8,128)(2,1)} %get-tuple-element.34), channel_id=1, source_target_pairs={{0,96},{1,129},{32,64},{33,161},{64,160},{65,193},{96,128},{97,225... | collective-permute-start | bytes 786440 | tf_op jit(solution)/shard_map/ppermute | solution.py:55
  12.9 19.4 %collective-permute-start.3 = (bf16[128,1024]{1,0:T(8,128)(2,1)}, bf16[128,1024]{1,0:T(8,128)(2,1)S(1)}, u32[]{:S(2)}, u32[]{:S(2)}) collective-permute-start(bf16[128,1024]{1,0:T(8,128)(2,1)} %get-tuple-element.35), channel_id=1, source_target_pairs={{0,160},{1,225},{32,128},{33,193},{64,224},{65,33},{96,192},{97,1}... | collective-permute-start | bytes 786440 | tf_op jit(solution)/shard_map/ppermute | solution.py:55
  20.3 13.3 %collective-permute-start.4 = (bf16[128,1024]{1,0:T(8,128)(2,1)}, bf16[128,1024]{1,0:T(8,128)(2,1)S(1)}, u32[]{:S(2)}, u32[]{:S(2)}) collective-permute-start(bf16[128,1024]{1,0:T(8,128)(2,1)} %get-tuple-element.36), channel_id=1, source_target_pairs={{0,32},{1,65},{32,0},{33,97},{64,96},{65,129},{96,64},{97,161},{12... | collective-permute-start | bytes 786440 | tf_op jit(solution)/shard_map/ppermute | solution.py:55
  24.6 10.0 %collective-permute-start.5 = (bf16[128,1024]{1,0:T(8,128)(2,1)}, bf16[128,1024]{1,0:T(8,128)(2,1)S(1)}, u32[]{:S(2)}, u32[]{:S(2)}) collective-permute-start(bf16[128,1024]{1,0:T(8,128)(2,1)} %get-tuple-element.37), channel_id=1, source_target_pairs={{0,64},{1,33},{32,96},{33,1},{64,128},{65,97},{96,160},{97,65},{12... | collective-permute-start | bytes 786440 | tf_op jit(solution)/shard_map/ppermute | solution.py:55
  25.4 9.5 %collective-permute-start.6 = (bf16[128,1024]{1,0:T(8,128)(2,1)}, bf16[128,1024]{1,0:T(8,128)(2,1)S(1)}, u32[]{:S(2)}, u32[]{:S(2)}) collective-permute-start(bf16[128,1024]{1,0:T(8,128)(2,1)} %get-tuple-element.38), channel_id=1, source_target_pairs={{0,192},{1,193},{32,224},{33,225},{64,0},{65,1},{96,32},{97,33},{1... | collective-permute-start | bytes 786440 | tf_op jit(solution)/shard_map/ppermute | solution.py:55
  37.6 14.4 %collective-permute-start.7 = (bf16[128,1024]{1,0:T(8,128)(2,1)S(1)}, bf16[128,1024]{1,0:T(8,128)(2,1)S(1)}, u32[]{:S(2)}, u32[]{:S(2)}) collective-permute-start(bf16[128,1024]{1,0:T(8,128)(2,1)S(1)} %fusion.2), channel_id=1, source_target_pairs={{192,0},{193,1},{224,32},{225,33},{0,64},{1,65},{32,96},{33,97},{6... | collective-permute-start | bytes 786440 | tf_op jit(solution)/shard_map/ppermute | solution.py:55
  39.2 14.8 %collective-permute-start.9 = (bf16[128,1024]{1,0:T(8,128)(2,1)S(1)}, bf16[128,1024]{1,0:T(8,128)(2,1)S(1)}, u32[]{:S(2)}, u32[]{:S(2)}) collective-permute-start(bf16[128,1024]{1,0:T(8,128)(2,1)S(1)} %fusion.2), channel_id=1, source_target_pairs={{64,0},{33,1},{96,32},{1,33},{128,64},{97,65},{160,96},{65,97},{19... | collective-permute-start | bytes 786440 | tf_op jit(solution)/shard_map/ppermute | solution.py:55
  40.9 15.9 %collective-permute-start.12 = (bf16[128,1024]{1,0:T(8,128)(2,1)S(1)}, bf16[128,1024]{1,0:T(8,128)(2,1)S(1)}, u32[]{:S(2)}, u32[]{:S(2)}) collective-permute-start(bf16[128,1024]{1,0:T(8,128)(2,1)S(1)} %fusion.2), channel_id=1, source_target_pairs={{224,0},{161,1},{192,32},{129,33},{32,64},{225,65},{0,96},{193,97}... | collective-permute-start | bytes 786440 | tf_op jit(solution)/shard_map/ppermute | solution.py:55
  42.3 19.5 %collective-permute-start.11 = (bf16[128,1024]{1,0:T(8,128)(2,1)S(1)}, bf16[128,1024]{1,0:T(8,128)(2,1)S(1)}, u32[]{:S(2)}, u32[]{:S(2)}) collective-permute-start(bf16[128,1024]{1,0:T(8,128)(2,1)S(1)} %fusion.2), channel_id=1, source_target_pairs={{128,0},{97,1},{160,32},{65,33},{192,64},{161,65},{224,96},{129,97... | collective-permute-start | bytes 786440 | tf_op jit(solution)/shard_map/ppermute | solution.py:55
  44.7 17.0 %collective-permute-start.14 = (bf16[128,1024]{1,0:T(8,128)(2,1)S(1)}, bf16[128,1024]{1,0:T(8,128)(2,1)S(1)}, u32[]{:S(2)}, u32[]{:S(2)}) collective-permute-start(bf16[128,1024]{1,0:T(8,128)(2,1)S(1)} %fusion.2), channel_id=1, source_target_pairs={{160,0},{225,1},{128,32},{193,33},{224,64},{33,65},{192,96},{1,97}... | collective-permute-start | bytes 786440 | tf_op jit(solution)/shard_map/ppermute | solution.py:55
  52.0 9.7 %collective-permute-start.8 = (bf16[128,1024]{1,0:T(8,128)(2,1)S(1)}, bf16[128,1024]{1,0:T(8,128)(2,1)S(1)}, u32[]{:S(2)}, u32[]{:S(2)}) collective-permute-start(bf16[128,1024]{1,0:T(8,128)(2,1)S(1)} %fusion.2), channel_id=1, source_target_pairs={{32,0},{65,1},{0,32},{97,33},{96,64},{129,65},{64,96},{161,97},{16... | collective-permute-start | bytes 786440 | tf_op jit(solution)/shard_map/ppermute | solution.py:55
  54.1 10.5 %collective-permute-start.13 = (bf16[128,1024]{1,0:T(8,128)(2,1)S(1)}, bf16[128,1024]{1,0:T(8,128)(2,1)S(1)}, u32[]{:S(2)}, u32[]{:S(2)}) collective-permute-start(bf16[128,1024]{1,0:T(8,128)(2,1)S(1)} %fusion.2), channel_id=1, source_target_pairs={{96,0},{129,1},{64,32},{161,33},{160,64},{193,65},{128,96},{225,97... | collective-permute-start | bytes 786440 | tf_op jit(solution)/shard_map/ppermute | solution.py:55
  56.8 8.6 %collective-permute-start.10 = (bf16[256,1024]{1,0:T(8,128)(2,1)S(1)}, bf16[256,1024]{1,0:T(8,128)(2,1)S(1)}, u32[]{:S(2)}, u32[]{:S(2)}) collective-permute-start(bf16[256,1024]{1,0:T(8,128)(2,1)S(1)} %convolution_convert_fusion.1), channel_id=1, source_target_pairs={{0,1},{1,0},{2,3},{3,2},{4,5},{5,4},{6,7},{7,6},{8,9},{9,8},{10,11... | collective-permute-start | bytes 1572872 | tf_op jit(solution)/shard_map/ppermute | solution.py:35
  69.1 39.2 %all-to-all-start = ((bf16[16,32,1024]{2,1,0:T(8,128)(2,1)}), bf16[16,32,1024]{2,1,0:T(8,128)(2,1)S(1)}, u32[]{:S(2)}, u32[]{:S(2)}) async-start(bf16[16,32,1024]{2,1,0:T(8,128)(2,1)} %bitcast.141), calls=%async_computation | async-start | bytes 2097152 | tf_op jit(solution)/shard_map/all_to_all | solution.py:282
  110.5 33.3 %all-to-all-start.1 = ((bf16[16,32,1024]{2,1,0:T(8,128)(2,1)}), bf16[16,32,1024]{2,1,0:T(8,128)(2,1)S(1)}, u32[]{:S(2)}, u32[]{:S(2)}) async-start(bf16[16,32,1024]{2,1,0:T(8,128)(2,1)} %broadcast_in_dim.5), calls=%async_computation.1 | async-start | bytes 2097152 | tf_op jit(solution)/shard_map/all_to_all | solution.py:303
  143.7 11.5 %collective-permute-start.19 = (bf16[4,128,1024]{2,1,0:T(8,128)(2,1)S(1)}, bf16[4,128,1024]{2,1,0:T(8,128)(2,1)S(1)}, u32[]{:S(2)}, u32[]{:S(2)}) collective-permute-start(bf16[4,128,1024]{2,1,0:T(8,128)(2,1)S(1)} %bitcast.135), channel_id=1, source_target_pairs={{0,1},{1,0},{2,3},{3,2},{4,5},{5,4},{6,7},{7,6},{8,9},{9,8},{10,11... | collective-permute-start | bytes 3145736 | tf_op jit(solution)/shard_map/ppermute | solution.py:35
  145.3 22.8 %collective-permute-start.21 = (bf16[128,1024]{1,0:T(8,128)(2,1)}, bf16[128,1024]{1,0:T(8,128)(2,1)S(1)}, u32[]{:S(2)}, u32[]{:S(2)}) collective-permute-start(bf16[128,1024]{1,0:T(8,128)(2,1)} %convolution_convert_fusion.3), channel_id=1, source_target_pairs={{0,224},{1,161},{32,192},{33,129},{64,32},{65,225},{96,0},{97,193}... | collective-permute-start | bytes 786440 | tf_op jit(solution)/shard_map/ppermute | solution.py:55
  150.1 18.0 %collective-permute-start.24 = (bf16[128,1024]{1,0:T(8,128)(2,1)}, bf16[128,1024]{1,0:T(8,128)(2,1)}, u32[]{:S(2)}, u32[]{:S(2)}) collective-permute-start(bf16[128,1024]{1,0:T(8,128)(2,1)} %convolution_convert_fusion.2), channel_id=1, source_target_pairs={{0,32},{1,65},{32,0},{33,97},{64,96},{65,129},{96,64},{97,161},{12... | collective-permute-start | bytes 786440 | tf_op jit(solution)/shard_map/ppermute | solution.py:55
  153.0 29.9 %collective-permute-start.20 = (bf16[128,1024]{1,0:T(8,128)(2,1)}, bf16[128,1024]{1,0:T(8,128)(2,1)}, u32[]{:S(2)}, u32[]{:S(2)}) collective-permute-start(bf16[128,1024]{1,0:T(8,128)(2,1)} %convolution_convert_fusion.4), channel_id=1, source_target_pairs={{0,128},{1,97},{32,160},{33,65},{64,192},{65,161},{96,224},{97,129... | collective-permute-start | bytes 786440 | tf_op jit(solution)/shard_map/ppermute | solution.py:55
  164.8 18.1 %collective-permute-start.25 = (bf16[128,1024]{1,0:T(8,128)(2,1)}, bf16[128,1024]{1,0:T(8,128)(2,1)S(1)}, u32[]{:S(2)}, u32[]{:S(2)}) collective-permute-start(bf16[128,1024]{1,0:T(8,128)(2,1)} %get-tuple-element.54), channel_id=1, source_target_pairs={{0,64},{1,33},{32,96},{33,1},{64,128},{65,97},{96,160},{97,65},{12... | collective-permute-start | bytes 786440 | tf_op jit(solution)/shard_map/ppermute | solution.py:55
  164.8 18.1 %collective-permute-start.26 = (bf16[128,1024]{1,0:T(8,128)(2,1)}, bf16[128,1024]{1,0:T(8,128)(2,1)S(1)}, u32[]{:S(2)}, u32[]{:S(2)}) collective-permute-start(bf16[128,1024]{1,0:T(8,128)(2,1)} %get-tuple-element.55), channel_id=1, source_target_pairs={{0,192},{1,193},{32,224},{33,225},{64,0},{65,1},{96,32},{97,33},{1... | collective-permute-start | bytes 786440 | tf_op jit(solution)/shard_map/ppermute | solution.py:55
  168.1 14.8 %collective-permute-start.22 = (bf16[128,1024]{1,0:T(8,128)(2,1)S(1)}, bf16[128,1024]{1,0:T(8,128)(2,1)}, u32[]{:S(2)}, u32[]{:S(2)}) collective-permute-start(bf16[128,1024]{1,0:T(8,128)(2,1)S(1)} %copy-done.12), channel_id=1, source_target_pairs={{0,96},{1,129},{32,64},{33,161},{64,160},{65,193},{96,128},{97,225... | collective-permute-start | bytes 786440 | tf_op jit(solution)/shard_map/ppermute | solution.py:55
  168.1 14.8 %collective-permute-start.23 = (bf16[128,1024]{1,0:T(8,128)(2,1)S(1)}, bf16[128,1024]{1,0:T(8,128)(2,1)}, u32[]{:S(2)}, u32[]{:S(2)}) collective-permute-start(bf16[128,1024]{1,0:T(8,128)(2,1)S(1)} %copy-done.11), channel_id=1, source_target_pairs={{0,160},{1,225},{32,128},{33,193},{64,224},{65,33},{96,192},{97,1}... | collective-permute-start | bytes 786440 | tf_op jit(solution)/shard_map/ppermute | solution.py:55
  184.5 9.3 %collective-permute-start.32 = (bf16[128,1024]{1,0:T(8,128)(2,1)S(1)}, bf16[128,1024]{1,0:T(8,128)(2,1)S(1)}, u32[]{:S(2)}, u32[]{:S(2)}) collective-permute-start(bf16[128,1024]{1,0:T(8,128)(2,1)S(1)} %multiply_convert_fusion), channel_id=1, source_target_pairs={{32,0},{65,1},{0,32},{97,33},{96,64},{129,65},{64,96},{161,97},{16... | collective-permute-start | bytes 786440 | tf_op jit(solution)/shard_map/ppermute | solution.py:55
  185.2 21.4 %collective-permute-start.31 = (bf16[128,1024]{1,0:T(8,128)(2,1)S(1)}, bf16[128,1024]{1,0:T(8,128)(2,1)S(1)}, u32[]{:S(2)}, u32[]{:S(2)}) collective-permute-start(bf16[128,1024]{1,0:T(8,128)(2,1)S(1)} %multiply_convert_fusion), channel_id=1, source_target_pairs={{192,0},{193,1},{224,32},{225,33},{0,64},{1,65},{32,96},{33,97},{6... | collective-permute-start | bytes 786440 | tf_op jit(solution)/shard_map/ppermute | solution.py:55
  187.8 19.6 %collective-permute-start.33 = (bf16[128,1024]{1,0:T(8,128)(2,1)S(1)}, bf16[128,1024]{1,0:T(8,128)(2,1)S(1)}, u32[]{:S(2)}, u32[]{:S(2)}) collective-permute-start(bf16[128,1024]{1,0:T(8,128)(2,1)S(1)} %multiply_convert_fusion), channel_id=1, source_target_pairs={{64,0},{33,1},{96,32},{1,33},{128,64},{97,65},{160,96},{65,97},{19... | collective-permute-start | bytes 786440 | tf_op jit(solution)/shard_map/ppermute | solution.py:55
  188.4 24.9 %collective-permute-start.30 = (bf16[128,1024]{1,0:T(8,128)(2,1)S(1)}, bf16[128,1024]{1,0:T(8,128)(2,1)S(1)}, u32[]{:S(2)}, u32[]{:S(2)}) collective-permute-start(bf16[128,1024]{1,0:T(8,128)(2,1)S(1)} %multiply_convert_fusion), channel_id=1, source_target_pairs={{160,0},{225,1},{128,32},{193,33},{224,64},{33,65},{192,96},{1,97}... | collective-permute-start | bytes 786440 | tf_op jit(solution)/shard_map/ppermute | solution.py:55
  190.7 22.6 %collective-permute-start.29 = (bf16[128,1024]{1,0:T(8,128)(2,1)S(1)}, bf16[128,1024]{1,0:T(8,128)(2,1)S(1)}, u32[]{:S(2)}, u32[]{:S(2)}) collective-permute-start(bf16[128,1024]{1,0:T(8,128)(2,1)S(1)} %multiply_convert_fusion), channel_id=1, source_target_pairs={{96,0},{129,1},{64,32},{161,33},{160,64},{193,65},{128,96},{225,97... | collective-permute-start | bytes 786440 | tf_op jit(solution)/shard_map/ppermute | solution.py:55
  193.8 19.6 %collective-permute-start.28 = (bf16[128,1024]{1,0:T(8,128)(2,1)S(1)}, bf16[128,1024]{1,0:T(8,128)(2,1)S(1)}, u32[]{:S(2)}, u32[]{:S(2)}) collective-permute-start(bf16[128,1024]{1,0:T(8,128)(2,1)S(1)} %multiply_convert_fusion), channel_id=1, source_target_pairs={{224,0},{161,1},{192,32},{129,33},{32,64},{225,65},{0,96},{193,97}... | collective-permute-start | bytes 786440 | tf_op jit(solution)/shard_map/ppermute | solution.py:55
  206.6 7.9 %collective-permute-start.27 = (bf16[128,1024]{1,0:T(8,128)(2,1)S(1)}, bf16[128,1024]{1,0:T(8,128)(2,1)S(1)}, u32[]{:S(2)}, u32[]{:S(2)}) collective-permute-start(bf16[128,1024]{1,0:T(8,128)(2,1)S(1)} %multiply_convert_fusion), channel_id=1, source_target_pairs={{128,0},{97,1},{160,32},{65,33},{192,64},{161,65},{224,96},{129,97... | collective-permute-start | bytes 786440 | tf_op jit(solution)/shard_map/ppermute | solution.py:55
  (25 other events, 214.5 us)

commit v7 on v4

--- a/solution.py
+++ b/solution.py
@@ -312,8 +312,8 @@
     grad_pre = (loss_scale * act_grad * slope).astype(bf16)
     near_grad, far_grad = gather_src(grad_pre)
 
-    grad_encoder = encoder_grad(res_t, near_grad, 0, None)
-    grad_encoder = encoder_grad(res_t, far_grad, 1, grad_encoder)
+    grad_encoder = encoder_grad(res_t, far_grad, 1, None)
+    grad_encoder = encoder_grad(res_t, near_grad, 0, grad_encoder)
     return (grad_encoder, grad_decoder)
 
 

time: 218 us -> 219 us (level)
  starting transfers between devices: 67.3 us -> 71.9 us
  waiting for transfers between devices: 83.5 us -> 78.9 us
    ppermute x28, waiting for transfers between devices: 41.6 us -> 37 us  [move(): return lax.ppermute(value, ('y', 'xl', 'core'), pairs)]
    ppermute x28, starting transfers between devices: 44.6 us -> 49.1 us  [move(): return lax.ppermute(value, ('y', 'xl', 'core'), pairs)]
  transfers between devices with their start and end apart: 36 -> 36, of which waited for: 21 -> 20; matrix products, arithmetic and copies ran while one was open for 4% -> 4% of each run, Pallas kernels for 16% -> 16%
where the time goes in v7:
time: 219 us; the launch traced here: 217 us
  waiting for transfers between devices  78.9 us (36%)
  starting transfers between devices  71.9 us (33%)
  Pallas kernels  45.6 us (21%)
  other arithmetic  9.16 us (4%)
  local copies, waits for them, and re-layouts  7.22 us (3%)
  matrix products  2.85 us (1%)
    ppermute x28, starting transfers between devices, move(): return lax.ppermute(value, ('y', 'xl', 'core'), pairs)  49.1 us
    ppermute x28, waiting for transfers between devices, move(): return lax.ppermute(value, ('y', 'xl', 'core'), pairs)  37 us
    all_to_all x1, waiting for transfers between devices, per_device(): mine = lax.all_to_all(errors, RING, 0, 0).reshape(4, block, -1)  21.1 us
    pallas_call x4, Pallas kernels, blocks_dot(): pl.pallas_call(kernel, grid_spec=pltpu.PrefetchScalarGridSpec(num_scalar_...  20.4 us
    all_to_all x1, waiting for transfers between devices, per_device(): shares = lax.all_to_all(shares.reshape(N_RING, rows, -1), RING, 0, 0)  13.7 us
    all_to_all x1, starting transfers between devices, per_device(): shares = lax.all_to_all(shares.reshape(N_RING, rows, -1), RING, 0, 0)  11.3 us
    pallas_call x2, Pallas kernels, encoder_grad(): pl.pallas_call(kernel, grid=(feat // tile,), in_specs=[pl.BlockSpec((tile...  10.7 us
    pallas_call x1, Pallas kernels, decoder_grad(): pl.pallas_call(kernel, grid=(width // tile,), in_specs=[pl.BlockSpec((blo...  7.73 us
  transfers between devices with their start and end apart: 36, of which 20 were waited for; matrix products, arithmetic and copies ran while one was open for 4% of the time, Pallas kernels for 16%

profile of v7, /device:TPU:32, one launch (start us, length us, event | category | flops | bytes accessed | tf_op | source)
XLA Modules:
  0.0 217.2 jit_solution(10419406621922263500)
XLA Ops:
  1.4 5.4 %blocks_dot.5 = (bf16[128,1024]{1,0:T(8,128)(2,1)}, bf16[128,1024]{1,0:T(8,128)(2,1)}, bf16[128,1024]{1,0:T(8,128)(2,1)}, bf16[128,1024]{1,0:T(8,128)(2,1)}) custom-call(s32[4]{0:T(128)} %pad_add_fusion.1.order_ref, bf16[1024,1024]{1,0:T(8,128)(2,1)} %in_ref.1, bf16[1024,1024]{1,0:T(8,128)(2,1)} %in_ref.1, bf16[1024,1024]{1,0:T(8,128)(2,1)} %in_ref.1, ...), custom_call_target="tpu_custom_call" | custom-call | tf_op jit(solution)/shard_map/blocks_dot/pallas_call | solution.py:97
  6.8 3.2 %collective-permute-start = (bf16[128,1024]{1,0:T(8,128)(2,1)}, bf16[128,1024]{1,0:T(8,128)(2,1)S(1)}, u32[]{:S(2)}, u32[]{:S(2)}) collective-permute-start(bf16[128,1024]{1,0:T(8,128)(2,1)} %get-tuple-element.34), channel_id=1, source_target_pairs={{0,128},{1,97},{32,160},{33,65},{64,192},{65,161},{96,224},{97,129... | collective-permute-start | bytes 786440 | tf_op jit(solution)/shard_map/ppermute | solution.py:55
  10.0 2.0 collective-permute-start.1
  14.7 5.5 %blocks_dot.4 = (bf16[128,1024]{1,0:T(8,128)(2,1)}, bf16[128,1024]{1,0:T(8,128)(2,1)}, bf16[128,1024]{1,0:T(8,128)(2,1)}, f32[128,1024]{1,0:T(8,128)}) custom-call(s32[4]{0:T(128)} %pad_add_fusion.order_ref, bf16[1024,1024]{1,0:T(8,128)(2,1)} %in_ref.1, bf16[1024,1024]{1,0:T(8,128)(2,1)} %in_ref.1, bf16[1024,1024]{1,0:T(8,128)(2,1)} %in_ref.1, ...), custom_call_target="tpu_custom_call" | custom-call | tf_op jit(solution)/shard_map/blocks_dot/pallas_call | solution.py:97
  21.2 3.3 %collective-permute-done = bf16[128,1024]{1,0:T(8,128)(2,1)S(1)} collective-permute-done((bf16[128,1024]{1,0:T(8,128)(2,1)}, bf16[128,1024]{1,0:T(8,128)(2,1)S(1)}, u32[]{:S(2)}, u32[]{:S(2)}) %collective-permute-start) | collective-permute-done | bytes 262176 | tf_op jit(solution)/shard_map/ppermute | solution.py:55
  25.4 2.4 %collective-permute-start.6 = (bf16[128,1024]{1,0:T(8,128)(2,1)}, bf16[128,1024]{1,0:T(8,128)(2,1)S(1)}, u32[]{:S(2)}, u32[]{:S(2)}) collective-permute-start(bf16[128,1024]{1,0:T(8,128)(2,1)} %get-tuple-element.40), channel_id=1, source_target_pairs={{0,192},{1,193},{32,224},{33,225},{64,0},{65,1},{96,32},{97,33},{1... | collective-permute-start | bytes 786440 | tf_op jit(solution)/shard_map/ppermute | solution.py:55
  27.8 4.5 %collective-permute-done.3 = bf16[128,1024]{1,0:T(8,128)(2,1)S(1)} collective-permute-done((bf16[128,1024]{1,0:T(8,128)(2,1)}, bf16[128,1024]{1,0:T(8,128)(2,1)S(1)}, u32[]{:S(2)}, u32[]{:S(2)}) %collective-permute-start.3) | collective-permute-done | bytes 262176 | tf_op jit(solution)/shard_map/ppermute | solution.py:55
  34.9 2.4 %add_divide_fusion = (f32[128,1024]{1,0:T(8,128)}, f32[128,1024]{1,0:T(8,128)S(1)}) fusion(f32[1024]{0:T(1024)S(1)} %copy-done.18, bf16[128,1024]{1,0:T(8,128)(2,1)S(1)} %collective-permute-done.6, bf16[128,1024]{1,0:T(8,128)(2,1)S(1)} %collective-permute-done.5, bf16[128,1024]{1,0:T(8,128)(2,1)S(1)} %collective-permute-done.4, ...), kind=kLoop, calls=%fused_computation.24 | loop fusion | flops 2490368 | bytes 3411968 | tf_op jit(solution)/shard_map/div | solution.py:255
  42.3 2.5 %collective-permute-start.11 = (bf16[128,1024]{1,0:T(8,128)(2,1)S(1)}, bf16[128,1024]{1,0:T(8,128)(2,1)S(1)}, u32[]{:S(2)}, u32[]{:S(2)}) collective-permute-start(bf16[128,1024]{1,0:T(8,128)(2,1)S(1)} %fusion.2), channel_id=1, source_target_pairs={{128,0},{97,1},{160,32},{65,33},{192,64},{161,65},{224,96},{129,97... | collective-permute-start | bytes 786440 | tf_op jit(solution)/shard_map/ppermute | solution.py:55
  45.7 6.3 %collective-permute-done.7 = bf16[128,1024]{1,0:T(8,128)(2,1)S(1)} collective-permute-done((bf16[128,1024]{1,0:T(8,128)(2,1)S(1)}, bf16[128,1024]{1,0:T(8,128)(2,1)S(1)}, u32[]{:S(2)}, u32[]{:S(2)}) %collective-permute-start.7) | collective-permute-done | bytes 262176 | tf_op jit(solution)/shard_map/ppermute | solution.py:55
  54.1 2.0 collective-permute-start.13
  57.0 4.8 %collective-permute-done.11.refs_4_ = bf16[128,1024]{1,0:T(8,128)(2,1)S(1)} collective-permute-done((bf16[128,1024]{1,0:T(8,128)(2,1)S(1)}, bf16[128,1024]{1,0:T(8,128)(2,1)S(1)}, u32[]{:S(2)}, u32[]{:S(2)}) %collective-permute-start.11) | collective-permute-done | bytes 262176 | tf_op jit(solution)/shard_map/ppermute | solution.py:55
  61.8 2.8 %collective-permute-done.13.refs_6_ = bf16[128,1024]{1,0:T(8,128)(2,1)S(1)} collective-permute-done((bf16[128,1024]{1,0:T(8,128)(2,1)S(1)}, bf16[128,1024]{1,0:T(8,128)(2,1)S(1)}, u32[]{:S(2)}, u32[]{:S(2)}) %collective-permute-start.13) | collective-permute-done | bytes 262176 | tf_op jit(solution)/shard_map/ppermute | solution.py:55
  69.1 11.3 %all-to-all-start = ((bf16[16,32,1024]{2,1,0:T(8,128)(2,1)}), bf16[16,32,1024]{2,1,0:T(8,128)(2,1)S(1)}, u32[]{:S(2)}, u32[]{:S(2)}) async-start(bf16[16,32,1024]{2,1,0:T(8,128)(2,1)} %bitcast.117), calls=%async_computation | async-start | bytes 2097152 | tf_op jit(solution)/shard_map/all_to_all | solution.py:272
  81.6 3.1 %collective-permute-done.16 = f32[1024]{0:T(1024)S(1)} collective-permute-done((f32[1024]{0:T(1024)S(1)}, f32[1024]{0:T(1024)S(1)}, u32[]{:S(2)}, u32[]{:S(2)}) %collective-permute-start.16) | collective-permute-done | bytes 4128 | tf_op jit(solution)/shard_map/ppermute | solution.py:35
  84.7 3.2 %collective-permute-start.17 = (f32[1024]{0:T(1024)S(1)}, f32[1024]{0:T(1024)S(1)}, u32[]{:S(2)}, u32[]{:S(2)}) collective-permute-start(f32[1024]{0:T(1024)S(1)} %add.269), channel_id=1, source_target_pairs={{0,64},{64,0},{128,192},{192,128},{1,65},{65,1},{129,193},{193,129... | collective-permute-start | bytes 12296 | tf_op jit(solution)/shard_map/ppermute | solution.py:35
  94.7 13.7 %all-to-all-done = bf16[16,32,1024]{2,1,0:T(8,128)(2,1)S(1)} async-done(((bf16[16,32,1024]{2,1,0:T(8,128)(2,1)}), bf16[16,32,1024]{2,1,0:T(8,128)(2,1)S(1)}, u32[]{:S(2)}, u32[]{:S(2)}) %all-to-all-start) | async-done | bytes 1048608 | tf_op jit(solution)/shard_map/all_to_all | solution.py:272
  110.5 5.4 %all-to-all-start.1 = ((bf16[16,32,1024]{2,1,0:T(8,128)(2,1)}), bf16[16,32,1024]{2,1,0:T(8,128)(2,1)S(1)}, u32[]{:S(2)}, u32[]{:S(2)}) async-start(bf16[16,32,1024]{2,1,0:T(8,128)(2,1)} %broadcast_in_dim.5), calls=%async_computation.1 | async-start | bytes 2097152 | tf_op jit(solution)/shard_map/all_to_all | solution.py:293
  115.9 6.8 %transpose.21.res_ref = bf16[1024,1024]{1,0:T(8,128)(2,1)} custom-call(s32[8]{0:T(128)} %stack.79.order_ref, bf16[1024,1024]{1,0:T(8,128)(2,1)} %in_ref.1), custom_call_target="tpu_custom_call" | custom-call | tf_op jit(solution)/shard_map/transpose/pallas_call | solution.py:156
  122.7 21.1 %all-to-all-done.1 = bf16[16,32,1024]{2,1,0:T(8,128)(2,1)S(1)} async-done(((bf16[16,32,1024]{2,1,0:T(8,128)(2,1)}), bf16[16,32,1024]{2,1,0:T(8,128)(2,1)S(1)}, u32[]{:S(2)}, u32[]{:S(2)}) %all-to-all-start.1) | async-done | bytes 1048608 | tf_op jit(solution)/shard_map/all_to_all | solution.py:293
  144.8 4.7 %blocks_dot.6 = (bf16[128,1024]{1,0:T(8,128)(2,1)}, bf16[128,1024]{1,0:T(8,128)(2,1)}, bf16[128,1024]{1,0:T(8,128)(2,1)}, bf16[128,1024]{1,0:T(8,128)(2,1)}) custom-call(s32[1]{0:T(128)} %constant.215.clone.1.order_ref, bf16[128,1024]{1,0:T(8,128)(2,1)} %get-tuple-element.75.refs_0_.refs_12_, bf16[128,1024]{1,0:T(8,128)(2,1)} %get-tuple-element.72.refs_1_.refs_13_, ...), custom_call_target="tpu_custom_call" | custom-call | tf_op jit(solution)/shard_map/blocks_dot/pallas_call | solution.py:97
  149.5 3.3 %collective-permute-start.20 = (bf16[128,1024]{1,0:T(8,128)(2,1)}, bf16[128,1024]{1,0:T(8,128)(2,1)S(1)}, u32[]{:S(2)}, u32[]{:S(2)}) collective-permute-start(bf16[128,1024]{1,0:T(8,128)(2,1)} %get-tuple-element.54), channel_id=1, source_target_pairs={{0,128},{1,97},{32,160},{33,65},{64,192},{65,161},{96,224},{97,129... | collective-permute-start | bytes 786440 | tf_op jit(solution)/shard_map/ppermute | solution.py:55
  152.8 2.8 %collective-permute-start.21 = (bf16[128,1024]{1,0:T(8,128)(2,1)}, bf16[128,1024]{1,0:T(8,128)(2,1)S(1)}, u32[]{:S(2)}, u32[]{:S(2)}) collective-permute-start(bf16[128,1024]{1,0:T(8,128)(2,1)} %get-tuple-element.55), channel_id=1, source_target_pairs={{0,224},{1,161},{32,192},{33,129},{64,32},{65,225},{96,0},{97,193}... | collective-permute-start | bytes 786440 | tf_op jit(solution)/shard_map/ppermute | solution.py:55
  158.1 4.8 %blocks_dot.7 = (bf16[128,1024]{1,0:T(8,128)(2,1)}, bf16[128,1024]{1,0:T(8,128)(2,1)}, bf16[128,1024]{1,0:T(8,128)(2,1)}, bf16[128,1024]{1,0:T(8,128)(2,1)}) custom-call(s32[1]{0:T(128)} %constant.215.clone.1.order_ref, bf16[128,1024]{1,0:T(8,128)(2,1)} %get-tuple-element.71.refs_0_.refs_14_, bf16[128,1024]{1,0:T(8,128)(2,1)} %get-tuple-element.68.refs_1_.refs_15_, ...), custom_call_target="tpu_custom_call" | custom-call | tf_op jit(solution)/shard_map/blocks_dot/pallas_call | solution.py:97
  163.9 2.1 collective-permute-start.22
  166.0 2.6 %collective-permute-start.23 = (bf16[128,1024]{1,0:T(8,128)(2,1)}, bf16[128,1024]{1,0:T(8,128)(2,1)S(1)}, u32[]{:S(2)}, u32[]{:S(2)}) collective-permute-start(bf16[128,1024]{1,0:T(8,128)(2,1)} %get-tuple-element.57), channel_id=1, source_target_pairs={{0,160},{1,225},{32,128},{33,193},{64,224},{65,33},{96,192},{97,1}... | collective-permute-start | bytes 786440 | tf_op jit(solution)/shard_map/ppermute | solution.py:55
  169.8 7.7 %decoder_grad.1 = bf16[1024,1024]{1,0:T(8,128)(2,1)} custom-call(bf16[128,1024]{1,0:T(8,128)(2,1)} %copy-done.2, bf16[128,1024]{1,0:T(8,128)(2,1)} %copy-done.10, bf16[128,1024]{1,0:T(8,128)(2,1)} %copy-done.3, bf16[128,1024]{1,0:T(8,128)(2,1)} %copy-done.6, bf16[128,1024]{1,0:T(8,128)(2,1)} %copy-done.8, bf16[128,1024]{1,0:T(8,128)(2,1)} %copy-done.7, ...), custom_call_target="tpu_custom_call" | custom-call | tf_op jit(solution)/shard_map/decoder_grad/pallas_call | solution.py:134
  188.3 2.7 %collective-permute-done.32.refs_2_ = bf16[128,1024]{1,0:T(8,128)(2,1)S(1)} collective-permute-done((bf16[128,1024]{1,0:T(8,128)(2,1)S(1)}, bf16[128,1024]{1,0:T(8,128)(2,1)S(1)}, u32[]{:S(2)}, u32[]{:S(2)}) %collective-permute-start.32) | collective-permute-done | bytes 262176 | tf_op jit(solution)/shard_map/ppermute | solution.py:55
  191.0 4.5 %collective-permute-start.29 = (bf16[128,1024]{1,0:T(8,128)(2,1)S(1)}, bf16[128,1024]{1,0:T(8,128)(2,1)S(1)}, u32[]{:S(2)}, u32[]{:S(2)}) collective-permute-start(bf16[128,1024]{1,0:T(8,128)(2,1)S(1)} %multiply_convert_fusion), channel_id=1, source_target_pairs={{64,0},{33,1},{96,32},{1,33},{128,64},{97,65},{160,96},{65,97},{19... | collective-permute-start | bytes 786440 | tf_op jit(solution)/shard_map/ppermute | solution.py:55
  197.7 5.8 %collective-permute-done.30.refs_0_ = bf16[128,1024]{1,0:T(8,128)(2,1)S(1)} collective-permute-done((bf16[128,1024]{1,0:T(8,128)(2,1)S(1)}, bf16[128,1024]{1,0:T(8,128)(2,1)S(1)}, u32[]{:S(2)}, u32[]{:S(2)}) %collective-permute-start.30) | collective-permute-done | bytes 262176 | tf_op jit(solution)/shard_map/ppermute | solution.py:55
  204.9 5.2 %encoder_grad.2.refs_4_ = f32[1024,1024]{1,0:T(8,128)} custom-call(bf16[1024,1024]{1,0:T(8,128)(2,1)} %transpose.21.res_ref, bf16[128,1024]{1,0:T(8,128)(2,1)} %copy-done.15, bf16[128,1024]{1,0:T(8,128)(2,1)} %copy-done.14, bf16[128,1024]{1,0:T(8,128)(2,1)} %copy-done.12, bf16[128,1024]{1,0:T(8,128)(2,1)} %copy-done.17), custom_call_target="tpu_custom_call" | custom-call | tf_op jit(solution)/shard_map/encoder_grad/pallas_call | solution.py:190
  211.7 5.5 %encoder_grad.3 = bf16[1024,1024]{1,0:T(8,128)(2,1)} custom-call(bf16[1024,1024]{1,0:T(8,128)(2,1)} %transpose.21.res_ref, bf16[128,1024]{1,0:T(8,128)(2,1)} %get-tuple-element.77.refs_0_, bf16[128,1024]{1,0:T(8,128)(2,1)} %copy-done.16, bf16[128,1024]{1,0:T(8,128)(2,1)} %get-tuple-element.76.refs_2_, bf16[128,1024]{1,0:T(8,128)(2,1)} %copy-done.13, ...), custom_call_target="tpu_custom_call" | custom-call | tf_op jit(solution)/shard_map/encoder_grad/pallas_call | solution.py:190
  (113 shorter events, 52.2 us)
Async XLA Ops:
  6.8 17.8 %collective-permute-start = (bf16[128,1024]{1,0:T(8,128)(2,1)}, bf16[128,1024]{1,0:T(8,128)(2,1)S(1)}, u32[]{:S(2)}, u32[]{:S(2)}) collective-permute-start(bf16[128,1024]{1,0:T(8,128)(2,1)} %get-tuple-element.34), channel_id=1, source_target_pairs={{0,128},{1,97},{32,160},{33,65},{64,192},{65,161},{96,224},{97,129... | collective-permute-start | bytes 786440 | tf_op jit(solution)/shard_map/ppermute | solution.py:55
  10.0 15.4 %collective-permute-start.1 = (bf16[128,1024]{1,0:T(8,128)(2,1)}, bf16[128,1024]{1,0:T(8,128)(2,1)S(1)}, u32[]{:S(2)}, u32[]{:S(2)}) collective-permute-start(bf16[128,1024]{1,0:T(8,128)(2,1)} %get-tuple-element.35), channel_id=1, source_target_pairs={{0,224},{1,161},{32,192},{33,129},{64,32},{65,225},{96,0},{97,193}... | collective-permute-start | bytes 786440 | tf_op jit(solution)/shard_map/ppermute | solution.py:55
  11.9 15.8 %collective-permute-start.2 = (bf16[128,1024]{1,0:T(8,128)(2,1)}, bf16[128,1024]{1,0:T(8,128)(2,1)S(1)}, u32[]{:S(2)}, u32[]{:S(2)}) collective-permute-start(bf16[128,1024]{1,0:T(8,128)(2,1)} %get-tuple-element.36), channel_id=1, source_target_pairs={{0,96},{1,129},{32,64},{33,161},{64,160},{65,193},{96,128},{97,225... | collective-permute-start | bytes 786440 | tf_op jit(solution)/shard_map/ppermute | solution.py:55
  12.9 19.4 %collective-permute-start.3 = (bf16[128,1024]{1,0:T(8,128)(2,1)}, bf16[128,1024]{1,0:T(8,128)(2,1)S(1)}, u32[]{:S(2)}, u32[]{:S(2)}) collective-permute-start(bf16[128,1024]{1,0:T(8,128)(2,1)} %get-tuple-element.37), channel_id=1, source_target_pairs={{0,160},{1,225},{32,128},{33,193},{64,224},{65,33},{96,192},{97,1}... | collective-permute-start | bytes 786440 | tf_op jit(solution)/shard_map/ppermute | solution.py:55
  20.2 13.4 %collective-permute-start.4 = (bf16[128,1024]{1,0:T(8,128)(2,1)}, bf16[128,1024]{1,0:T(8,128)(2,1)S(1)}, u32[]{:S(2)}, u32[]{:S(2)}) collective-permute-start(bf16[128,1024]{1,0:T(8,128)(2,1)} %get-tuple-element.38), channel_id=1, source_target_pairs={{0,32},{1,65},{32,0},{33,97},{64,96},{65,129},{96,64},{97,161},{12... | collective-permute-start | bytes 786440 | tf_op jit(solution)/shard_map/ppermute | solution.py:55
  24.6 10.0 %collective-permute-start.5 = (bf16[128,1024]{1,0:T(8,128)(2,1)}, bf16[128,1024]{1,0:T(8,128)(2,1)S(1)}, u32[]{:S(2)}, u32[]{:S(2)}) collective-permute-start(bf16[128,1024]{1,0:T(8,128)(2,1)} %get-tuple-element.39), channel_id=1, source_target_pairs={{0,64},{1,33},{32,96},{33,1},{64,128},{65,97},{96,160},{97,65},{12... | collective-permute-start | bytes 786440 | tf_op jit(solution)/shard_map/ppermute | solution.py:55
  25.4 9.5 %collective-permute-start.6 = (bf16[128,1024]{1,0:T(8,128)(2,1)}, bf16[128,1024]{1,0:T(8,128)(2,1)S(1)}, u32[]{:S(2)}, u32[]{:S(2)}) collective-permute-start(bf16[128,1024]{1,0:T(8,128)(2,1)} %get-tuple-element.40), channel_id=1, source_target_pairs={{0,192},{1,193},{32,224},{33,225},{64,0},{65,1},{96,32},{97,33},{1... | collective-permute-start | bytes 786440 | tf_op jit(solution)/shard_map/ppermute | solution.py:55
  37.6 14.4 %collective-permute-start.7 = (bf16[128,1024]{1,0:T(8,128)(2,1)S(1)}, bf16[128,1024]{1,0:T(8,128)(2,1)S(1)}, u32[]{:S(2)}, u32[]{:S(2)}) collective-permute-start(bf16[128,1024]{1,0:T(8,128)(2,1)S(1)} %fusion.2), channel_id=1, source_target_pairs={{192,0},{193,1},{224,32},{225,33},{0,64},{1,65},{32,96},{33,97},{6... | collective-permute-start | bytes 786440 | tf_op jit(solution)/shard_map/ppermute | solution.py:55
  39.2 14.8 %collective-permute-start.9 = (bf16[128,1024]{1,0:T(8,128)(2,1)S(1)}, bf16[128,1024]{1,0:T(8,128)(2,1)S(1)}, u32[]{:S(2)}, u32[]{:S(2)}) collective-permute-start(bf16[128,1024]{1,0:T(8,128)(2,1)S(1)} %fusion.2), channel_id=1, source_target_pairs={{64,0},{33,1},{96,32},{1,33},{128,64},{97,65},{160,96},{65,97},{19... | collective-permute-start | bytes 786440 | tf_op jit(solution)/shard_map/ppermute | solution.py:55
  40.9 15.9 %collective-permute-start.12 = (bf16[128,1024]{1,0:T(8,128)(2,1)S(1)}, bf16[128,1024]{1,0:T(8,128)(2,1)S(1)}, u32[]{:S(2)}, u32[]{:S(2)}) collective-permute-start(bf16[128,1024]{1,0:T(8,128)(2,1)S(1)} %fusion.2), channel_id=1, source_target_pairs={{224,0},{161,1},{192,32},{129,33},{32,64},{225,65},{0,96},{193,97}... | collective-permute-start | bytes 786440 | tf_op jit(solution)/shard_map/ppermute | solution.py:55
  42.3 19.5 %collective-permute-start.11 = (bf16[128,1024]{1,0:T(8,128)(2,1)S(1)}, bf16[128,1024]{1,0:T(8,128)(2,1)S(1)}, u32[]{:S(2)}, u32[]{:S(2)}) collective-permute-start(bf16[128,1024]{1,0:T(8,128)(2,1)S(1)} %fusion.2), channel_id=1, source_target_pairs={{128,0},{97,1},{160,32},{65,33},{192,64},{161,65},{224,96},{129,97... | collective-permute-start | bytes 786440 | tf_op jit(solution)/shard_map/ppermute | solution.py:55
  44.7 17.0 %collective-permute-start.14 = (bf16[128,1024]{1,0:T(8,128)(2,1)S(1)}, bf16[128,1024]{1,0:T(8,128)(2,1)S(1)}, u32[]{:S(2)}, u32[]{:S(2)}) collective-permute-start(bf16[128,1024]{1,0:T(8,128)(2,1)S(1)} %fusion.2), channel_id=1, source_target_pairs={{160,0},{225,1},{128,32},{193,33},{224,64},{33,65},{192,96},{1,97}... | collective-permute-start | bytes 786440 | tf_op jit(solution)/shard_map/ppermute | solution.py:55
  52.0 9.7 %collective-permute-start.8 = (bf16[128,1024]{1,0:T(8,128)(2,1)S(1)}, bf16[128,1024]{1,0:T(8,128)(2,1)S(1)}, u32[]{:S(2)}, u32[]{:S(2)}) collective-permute-start(bf16[128,1024]{1,0:T(8,128)(2,1)S(1)} %fusion.2), channel_id=1, source_target_pairs={{32,0},{65,1},{0,32},{97,33},{96,64},{129,65},{64,96},{161,97},{16... | collective-permute-start | bytes 786440 | tf_op jit(solution)/shard_map/ppermute | solution.py:55
  54.1 10.5 %collective-permute-start.13 = (bf16[128,1024]{1,0:T(8,128)(2,1)S(1)}, bf16[128,1024]{1,0:T(8,128)(2,1)S(1)}, u32[]{:S(2)}, u32[]{:S(2)}) collective-permute-start(bf16[128,1024]{1,0:T(8,128)(2,1)S(1)} %fusion.2), channel_id=1, source_target_pairs={{96,0},{129,1},{64,32},{161,33},{160,64},{193,65},{128,96},{225,97... | collective-permute-start | bytes 786440 | tf_op jit(solution)/shard_map/ppermute | solution.py:55
  56.9 8.6 %collective-permute-start.10 = (bf16[256,1024]{1,0:T(8,128)(2,1)S(1)}, bf16[256,1024]{1,0:T(8,128)(2,1)S(1)}, u32[]{:S(2)}, u32[]{:S(2)}) collective-permute-start(bf16[256,1024]{1,0:T(8,128)(2,1)S(1)} %convolution_convert_fusion.1), channel_id=1, source_target_pairs={{0,1},{1,0},{2,3},{3,2},{4,5},{5,4},{6,7},{7,6},{8,9},{9,8},{10,11... | collective-permute-start | bytes 1572872 | tf_op jit(solution)/shard_map/ppermute | solution.py:35
  69.1 39.2 %all-to-all-start = ((bf16[16,32,1024]{2,1,0:T(8,128)(2,1)}), bf16[16,32,1024]{2,1,0:T(8,128)(2,1)S(1)}, u32[]{:S(2)}, u32[]{:S(2)}) async-start(bf16[16,32,1024]{2,1,0:T(8,128)(2,1)} %bitcast.117), calls=%async_computation | async-start | bytes 2097152 | tf_op jit(solution)/shard_map/all_to_all | solution.py:272
  110.5 33.3 %all-to-all-start.1 = ((bf16[16,32,1024]{2,1,0:T(8,128)(2,1)}), bf16[16,32,1024]{2,1,0:T(8,128)(2,1)S(1)}, u32[]{:S(2)}, u32[]{:S(2)}) async-start(bf16[16,32,1024]{2,1,0:T(8,128)(2,1)} %broadcast_in_dim.5), calls=%async_computation.1 | async-start | bytes 2097152 | tf_op jit(solution)/shard_map/all_to_all | solution.py:293
  143.7 13.3 %collective-permute-start.19 = (bf16[4,128,1024]{2,1,0:T(8,128)(2,1)S(1)}, bf16[4,128,1024]{2,1,0:T(8,128)(2,1)S(1)}, u32[]{:S(2)}, u32[]{:S(2)}) collective-permute-start(bf16[4,128,1024]{2,1,0:T(8,128)(2,1)S(1)} %bitcast.118), channel_id=1, source_target_pairs={{0,1},{1,0},{2,3},{3,2},{4,5},{5,4},{6,7},{7,6},{8,9},{9,8},{10,11... | collective-permute-start | bytes 3145736 | tf_op jit(solution)/shard_map/ppermute | solution.py:35
  149.5 16.5 %collective-permute-start.20 = (bf16[128,1024]{1,0:T(8,128)(2,1)}, bf16[128,1024]{1,0:T(8,128)(2,1)S(1)}, u32[]{:S(2)}, u32[]{:S(2)}) collective-permute-start(bf16[128,1024]{1,0:T(8,128)(2,1)} %get-tuple-element.54), channel_id=1, source_target_pairs={{0,128},{1,97},{32,160},{33,65},{64,192},{65,161},{96,224},{97,129... | collective-permute-start | bytes 786440 | tf_op jit(solution)/shard_map/ppermute | solution.py:55
  152.8 15.8 %collective-permute-start.21 = (bf16[128,1024]{1,0:T(8,128)(2,1)}, bf16[128,1024]{1,0:T(8,128)(2,1)S(1)}, u32[]{:S(2)}, u32[]{:S(2)}) collective-permute-start(bf16[128,1024]{1,0:T(8,128)(2,1)} %get-tuple-element.55), channel_id=1, source_target_pairs={{0,224},{1,161},{32,192},{33,129},{64,32},{65,225},{96,0},{97,193}... | collective-permute-start | bytes 786440 | tf_op jit(solution)/shard_map/ppermute | solution.py:55
  155.6 22.0 %collective-permute-start.24 = (bf16[128,1024]{1,0:T(8,128)(2,1)}, bf16[128,1024]{1,0:T(8,128)(2,1)S(1)}, u32[]{:S(2)}, u32[]{:S(2)}) collective-permute-start(bf16[128,1024]{1,0:T(8,128)(2,1)} %get-tuple-element.58), channel_id=1, source_target_pairs={{0,32},{1,65},{32,0},{33,97},{64,96},{65,129},{96,64},{97,161},{12... | collective-permute-start | bytes 786440 | tf_op jit(solution)/shard_map/ppermute | solution.py:55
  163.8 14.3 %collective-permute-start.26 = (bf16[128,1024]{1,0:T(8,128)(2,1)S(1)}, bf16[128,1024]{1,0:T(8,128)(2,1)S(1)}, u32[]{:S(2)}, u32[]{:S(2)}) collective-permute-start(bf16[128,1024]{1,0:T(8,128)(2,1)S(1)} %broadcast_select_fusion.2), channel_id=1, source_target_pairs={{0,192},{1,193},{32,224},{33,225},{64,0},{65,1},{96,32},{97,33},{1... | collective-permute-start | bytes 786440 | tf_op jit(solution)/shard_map/ppermute | solution.py:55
  163.9 14.2 %collective-permute-start.22 = (bf16[128,1024]{1,0:T(8,128)(2,1)}, bf16[128,1024]{1,0:T(8,128)(2,1)S(1)}, u32[]{:S(2)}, u32[]{:S(2)}) collective-permute-start(bf16[128,1024]{1,0:T(8,128)(2,1)} %get-tuple-element.56), channel_id=1, source_target_pairs={{0,96},{1,129},{32,64},{33,161},{64,160},{65,193},{96,128},{97,225... | collective-permute-start | bytes 786440 | tf_op jit(solution)/shard_map/ppermute | solution.py:55
  166.0 13.8 %collective-permute-start.23 = (bf16[128,1024]{1,0:T(8,128)(2,1)}, bf16[128,1024]{1,0:T(8,128)(2,1)S(1)}, u32[]{:S(2)}, u32[]{:S(2)}) collective-permute-start(bf16[128,1024]{1,0:T(8,128)(2,1)} %get-tuple-element.57), channel_id=1, source_target_pairs={{0,160},{1,225},{32,128},{33,193},{64,224},{65,33},{96,192},{97,1}... | collective-permute-start | bytes 786440 | tf_op jit(solution)/shard_map/ppermute | solution.py:55
  168.6 11.7 %collective-permute-start.25 = (bf16[128,1024]{1,0:T(8,128)(2,1)}, bf16[128,1024]{1,0:T(8,128)(2,1)S(1)}, u32[]{:S(2)}, u32[]{:S(2)}) collective-permute-start(bf16[128,1024]{1,0:T(8,128)(2,1)} %get-tuple-element.59), channel_id=1, source_target_pairs={{0,64},{1,33},{32,96},{33,1},{64,128},{65,97},{96,160},{97,65},{12... | collective-permute-start | bytes 786440 | tf_op jit(solution)/shard_map/ppermute | solution.py:55
  180.7 10.3 %collective-permute-start.32 = (bf16[128,1024]{1,0:T(8,128)(2,1)S(1)}, bf16[128,1024]{1,0:T(8,128)(2,1)S(1)}, u32[]{:S(2)}, u32[]{:S(2)}) collective-permute-start(bf16[128,1024]{1,0:T(8,128)(2,1)S(1)} %multiply_convert_fusion), channel_id=1, source_target_pairs={{96,0},{129,1},{64,32},{161,33},{160,64},{193,65},{128,96},{225,97... | collective-permute-start | bytes 786440 | tf_op jit(solution)/shard_map/ppermute | solution.py:55
  182.6 14.4 %collective-permute-start.31 = (bf16[128,1024]{1,0:T(8,128)(2,1)S(1)}, bf16[128,1024]{1,0:T(8,128)(2,1)S(1)}, u32[]{:S(2)}, u32[]{:S(2)}) collective-permute-start(bf16[128,1024]{1,0:T(8,128)(2,1)S(1)} %multiply_convert_fusion), channel_id=1, source_target_pairs={{224,0},{161,1},{192,32},{129,33},{32,64},{225,65},{0,96},{193,97}... | collective-permute-start | bytes 786440 | tf_op jit(solution)/shard_map/ppermute | solution.py:55
  183.7 19.8 %collective-permute-start.30 = (bf16[128,1024]{1,0:T(8,128)(2,1)S(1)}, bf16[128,1024]{1,0:T(8,128)(2,1)S(1)}, u32[]{:S(2)}, u32[]{:S(2)}) collective-permute-start(bf16[128,1024]{1,0:T(8,128)(2,1)S(1)} %multiply_convert_fusion), channel_id=1, source_target_pairs={{128,0},{97,1},{160,32},{65,33},{192,64},{161,65},{224,96},{129,97... | collective-permute-start | bytes 786440 | tf_op jit(solution)/shard_map/ppermute | solution.py:55
  185.6 17.9 %collective-permute-start.33 = (bf16[128,1024]{1,0:T(8,128)(2,1)S(1)}, bf16[128,1024]{1,0:T(8,128)(2,1)S(1)}, u32[]{:S(2)}, u32[]{:S(2)}) collective-permute-start(bf16[128,1024]{1,0:T(8,128)(2,1)S(1)} %multiply_convert_fusion), channel_id=1, source_target_pairs={{160,0},{225,1},{128,32},{193,33},{224,64},{33,65},{192,96},{1,97}... | collective-permute-start | bytes 786440 | tf_op jit(solution)/shard_map/ppermute | solution.py:55
  187.6 22.5 %collective-permute-start.27 = (bf16[128,1024]{1,0:T(8,128)(2,1)S(1)}, bf16[128,1024]{1,0:T(8,128)(2,1)S(1)}, u32[]{:S(2)}, u32[]{:S(2)}) collective-permute-start(bf16[128,1024]{1,0:T(8,128)(2,1)S(1)} %multiply_convert_fusion), channel_id=1, source_target_pairs={{192,0},{193,1},{224,32},{225,33},{0,64},{1,65},{32,96},{33,97},{6... | collective-permute-start | bytes 786440 | tf_op jit(solution)/shard_map/ppermute | solution.py:55
  191.0 19.9 %collective-permute-start.29 = (bf16[128,1024]{1,0:T(8,128)(2,1)S(1)}, bf16[128,1024]{1,0:T(8,128)(2,1)S(1)}, u32[]{:S(2)}, u32[]{:S(2)}) collective-permute-start(bf16[128,1024]{1,0:T(8,128)(2,1)S(1)} %multiply_convert_fusion), channel_id=1, source_target_pairs={{64,0},{33,1},{96,32},{1,33},{128,64},{97,65},{160,96},{65,97},{19... | collective-permute-start | bytes 786440 | tf_op jit(solution)/shard_map/ppermute | solution.py:55
  197.0 13.9 %collective-permute-start.28 = (bf16[128,1024]{1,0:T(8,128)(2,1)S(1)}, bf16[128,1024]{1,0:T(8,128)(2,1)S(1)}, u32[]{:S(2)}, u32[]{:S(2)}) collective-permute-start(bf16[128,1024]{1,0:T(8,128)(2,1)S(1)} %multiply_convert_fusion), channel_id=1, source_target_pairs={{32,0},{65,1},{0,32},{97,33},{96,64},{129,65},{64,96},{161,97},{16... | collective-permute-start | bytes 786440 | tf_op jit(solution)/shard_map/ppermute | solution.py:55
  (24 other events, 203.7 us)
